TPU v7x, 32 devices: a whole 2x2x4 slice. The times are simulated.
32 devices in a mesh: tm: 4 (over y, x), lat: 8 (over z, core).
Axes of the slice: x: 2, y: 2, z: 4, core: 2. Of those that a mesh axis runs over, the one named last changes fastest.
Arguments:
- states: float32 [8, 69, 32, 256], P('tm', None, 'lat'), may hold values from -6 to 6
- observed: float32 [8, 69, 32, 256], P('tm', None, 'lat'), may hold values from -6 to 6
- conv_in: bfloat16 [3, 3, 256, 345], replicated, may hold values from -0.109375 to 0.109375
- bias_in: float32 [256], replicated, may hold values from -3 to 3
- conv_out: bfloat16 [3, 3, 69, 256], replicated, may hold values from -0.125 to 0.125
- bias_out: float32 [69], replicated, may hold values from -3 to 3
Outputs:
- scores: float32 [8, 69, 32, 256], P('tm', None, 'lat')
- guidance: float32 [8, 69, 32, 256], P('tm', None, 'lat')
All inputs are finite; a program needn't handle non-finite values.
Results may differ from a plain program's by a relative error of at most 0.0045.
Values may be sent and summed in bfloat16 or wider, within the bound.
No kernel may reach another device: no remote copies, remote signals or barrier semaphores. Data moves between devices by JAX's collectives and lax.ppermute only.
A program may use at most 64 MiB of HBM per device.

v0:
```python
import jax
import jax.numpy as jnp
from jax import lax
from jax.sharding import PartitionSpec as P

WINDOW = 5


def with_halo(block, sides, width, periodic):
    for axis, dim in sides:
        count = lax.axis_size(axis)
        forward = [(i, i + 1) for i in range(count - 1)]
        if periodic:
            forward.append((count - 1, 0))
        backward = [(target, source) for source, target in forward]
        low = lax.ppermute(
            lax.slice_in_dim(block, block.shape[dim] - width, None, axis=dim), axis, forward
        )
        high = lax.ppermute(lax.slice_in_dim(block, 0, width, axis=dim), axis, backward)
        block = jnp.concatenate([low, block, high], axis=dim)
    return block


def from_behind(value, axis, steps):
    count = lax.axis_size(axis)
    pairs = [(source, (source + steps) % count) for source in range(count)]
    return lax.ppermute(value, axis, pairs)


def convolve(padded, weights):
    rows = padded.shape[2] - 2
    total = None
    for j in range(3):
        moved = jnp.roll(padded, 1 - j, axis=3)
        for i in range(3):
            band = moved[:, :, i : i + rows, :]
            term = jnp.einsum(
                "oc,tcrw->torw", weights[i, j], band, preferred_element_type=jnp.float32
            )
            total = term if total is None else total + term
    return total


def flipped(weights):
    return jnp.transpose(weights[::-1, ::-1], (0, 1, 3, 2))


def silu_slope(value):
    sig = jax.nn.sigmoid(value)
    return sig * (1.0 + value * (1.0 - sig))


def gather_windows(extended, count):
    return jnp.concatenate([extended[k : k + count] for k in range(WINDOW)], axis=1)


def shards(states, observed, conv_in, bias_in, conv_out, bias_out):
    count = states.shape[0]
    chans = states.shape[1]
    rows = states.shape[2]
    width = states.shape[3]
    back_in = flipped(conv_in)
    back_out = flipped(conv_out)
    cast = states.astype(jnp.bfloat16)
    extended = with_halo(cast, (("tm", 0),), 2, True)
    bias_hidden = bias_in[None, :, None, None]
    bias_score = bias_out[None, :, None, None]
    widened = with_halo(extended, (("lat", 2),), 1, False)
    windows = gather_windows(widened, count)
    pre = convolve(windows, conv_in) + bias_hidden
    act = jax.nn.silu(pre).astype(jnp.bfloat16)
    act_wide = with_halo(act, (("lat", 2),), 1, False)
    scores = convolve(act_wide, conv_out) + bias_score
    resid = (scores - observed).astype(jnp.bfloat16)
    resid_wide = with_halo(resid, (("lat", 2),), 1, False)
    grad_act = convolve(resid_wide, back_out)
    grad_pre = (grad_act * silu_slope(pre)).astype(jnp.bfloat16)
    grad_wide = with_halo(grad_pre, (("lat", 2),), 1, False)
    grad_window = convolve(grad_wide, back_in)
    slots = grad_window.reshape(count, WINDOW, chans, rows, width)
    gathered = None
    for k in range(WINDOW):
        placed = jnp.pad(slots[:, k], ((k, WINDOW - 1 - k), (0, 0), (0, 0), (0, 0)))
        gathered = placed if gathered is None else gathered + placed
    owned = gathered[2 : count + 2]
    from_next = from_behind(gathered[:2].astype(jnp.bfloat16), "tm", -1).astype(jnp.float32)
    from_prev = from_behind(gathered[count + 2 :].astype(jnp.bfloat16), "tm", 1).astype(jnp.float32)
    guidance = owned + from_next
    guidance = guidance + from_prev
    return (scores, guidance)


def solution(mesh):
    in_specs = (P("tm", None, "lat", None), P("tm", None, "lat", None), P(), P(), P(), P())
    out_specs = (P("tm", None, "lat", None), P("tm", None, "lat", None))
    return jax.shard_map(shards, mesh=mesh, in_specs=in_specs, out_specs=out_specs, check_vma=False)
```

profile of v0, /device:TPU:21, one launch (start us, length us, event | category | flops | bytes accessed | tf_op | source)
XLA Modules:
  0.0 114.9 jit_solution(7847374871776428621)
XLA Ops:
  0.7 1.3 %copy.122 = bf16[2,69,4,256]{3,1,2,0:T(8,128)(2,1)S(1)} copy(f32[2,69,4,256]{3,2,1,0:T(4,128)} %param.6) | data formatting | bytes 847872 | tf_op args[0]
  1.9 1.2 %collective-permute-start.1 = (bf16[2,69,4,256]{3,1,2,0:T(8,128)(2,1)S(1)}, bf16[2,69,4,256]{3,1,2,0:T(8,128)(2,1)S(1)}, u32[]{:S(2)}, u32[]{:S(2)}) collective-permute-start(bf16[2,69,4,256]{3,1,2,0:T(8,128)(2,1)S(1)} %copy.122), channel_id=1, source_target_pairs={{8,0},{16,8},{24,16},{0,24},{9,1},{17,9},{25,17},{1,25},{10,2},{18... | collective-permute-start | bytes 847880 | tf_op jit(solution)/shard_map/ppermute | solution.py:19
  3.5 6.4 %collective-permute-done.1 = bf16[2,69,4,256]{3,1,2,0:T(8,128)(2,1)S(1)} collective-permute-done((bf16[2,69,4,256]{3,1,2,0:T(8,128)(2,1)S(1)}, bf16[2,69,4,256]{3,1,2,0:T(8,128)(2,1)S(1)}, u32[]{:S(2)}, u32[]{:S(2)}) %collective-permute-start.1) | collective-permute-done | bytes 282656 | tf_op jit(solution)/shard_map/ppermute | solution.py:19
  9.9 6.3 %collective-permute-done = bf16[2,69,4,256]{3,1,2,0:T(8,128)(2,1)S(1)} collective-permute-done((bf16[2,69,4,256]{3,1,2,0:T(8,128)(2,1)S(1)}, bf16[2,69,4,256]{3,1,2,0:T(8,128)(2,1)S(1)}, u32[]{:S(2)}, u32[]{:S(2)}) %collective-permute-start) | collective-permute-done | bytes 282656 | tf_op jit(solution)/shard_map/ppermute | solution.py:16
  16.2 4.6 %collective-permute-start.2 = (bf16[6,69,1,256]{3,1,2,0:T(8,128)(2,1)S(1)}, bf16[6,69,1,256]{3,1,2,0:T(8,128)(2,1)S(1)}, u32[]{:S(2)}, u32[]{:S(2)}) collective-permute-start(bf16[6,69,1,256]{3,1,2,0:T(8,128)(2,1)S(1)} %get-tuple-element.32), channel_id=1, source_target_pairs={{0,1},{1,2},{2,3},{3,4},{4,5},{5,6},{6,7},{8,9},{9,10},{10,11},{11... | collective-permute-start | bytes 635912 | tf_op jit(solution)/shard_map/ppermute | solution.py:16
  20.8 1.9 %collective-permute-start.3 = (bf16[6,69,1,256]{3,1,2,0:T(8,128)(2,1)S(1)}, bf16[6,69,1,256]{3,1,2,0:T(8,128)(2,1)S(1)}, u32[]{:S(2)}, u32[]{:S(2)}) collective-permute-start(bf16[6,69,1,256]{3,1,2,0:T(8,128)(2,1)S(1)} %get-tuple-element.33), channel_id=1, source_target_pairs={{1,0},{2,1},{3,2},{4,3},{5,4},{6,5},{7,6},{9,8},{10,9},{11,10},{12... | collective-permute-start | bytes 635912 | tf_op jit(solution)/shard_map/ppermute | solution.py:19
  22.8 0.7 reverse_bitcast_fusion.1
  23.5 1.3 %reverse_bitcast_fusion = bf16[3,3,345,256]{3,2,1,0:T(8,128)(2,1)} fusion(bf16[3,3,256,345]{2,3,1,0:T(8,128)(2,1)S(1)} %copy-done), kind=kLoop, calls=%fused_computation.16 | loop fusion | bytes 3179520 | tf_op jit(solution)/shard_map/transpose | solution.py:45
  24.8 3.3 %collective-permute-done.3 = bf16[6,69,1,256]{3,1,2,0:T(8,128)(2,1)S(1)} collective-permute-done((bf16[6,69,1,256]{3,1,2,0:T(8,128)(2,1)S(1)}, bf16[6,69,1,256]{3,1,2,0:T(8,128)(2,1)S(1)}, u32[]{:S(2)}, u32[]{:S(2)}) %collective-permute-start.3) | collective-permute-done | bytes 212000 | tf_op jit(solution)/shard_map/ppermute | solution.py:19
  28.3 1.1 fusion.126
  29.4 6.8 %concatenate.68 = bf16[2,345,6,256]{3,1,2,0:T(8,128)(2,1)S(1)} concatenate(bf16[2,69,6,256]{3,1,2,0:T(8,128)(2,1)} %get-tuple-element.27, bf16[2,69,6,256]{3,1,2,0:T(8,128)(2,1)} %get-tuple-element.26, bf16[2,69,6,256]{3,1,2,0:T(8,128)(2,1)S(1)} %get-tuple-element.25, bf16[2,69,6,256]{3,1,2,0:T(8,128)(2,1)S(1)} %get-tuple-element.24, bf16[2,69,6,256]{3,1,2,0:T(8,128)(2,1)S(1)} %get-tuple-element.23), dimensions={1} | concatenate | bytes 4239360 | tf_op jit(solution)/shard_map/concatenate | solution.py:54
  36.2 1.8 %fusion.59 = f32[2,4,256,256]{3,2,1,0:T(8,128)S(1)} fusion(bf16[2,345,6,256]{3,1,2,0:T(8,128)(2,1)S(1)} %concatenate.68, bf16[3,3,256,345]{2,3,1,0:T(8,128)(2,1)} %param.8), kind=kOutput, calls=%fused_computation.105 | convolution fusion | flops 361758720 | bytes 4397056 | tf_op jit(solution)/shard_map/oc,tcrw->torw/dot_general | solution.py:37
  38.0 0.8 fusion.61
  38.8 0.5 fusion.122
  39.3 1.2 %fusion.123 = (bf16[2,345,6,255]{3,1,2,0:T(8,128)(2,1)S(1)}, bf16[2,345,6,255]{3,1,2,0:T(8,128)(2,1)S(1)}) fusion(bf16[2,345,6,256]{3,1,2,0:T(8,128)(2,1)S(1)} %concatenate.68), kind=kLoop, calls=%fused_computation.172 | loop fusion | bytes 8445600 | tf_op jit(solution)/shard_map/jit(_roll_static)/slice | solution.py:34
  40.5 1.3 %fusion.65 = f32[2,4,256,256]{3,2,1,0:T(8,128)S(1)} fusion(bf16[3,3,256,345]{2,3,1,0:T(8,128)(2,1)S(1)} %copy-done.1, bf16[2,345,6,255]{3,1,2,0:T(8,128)(2,1)S(1)} %get-tuple-element.15, bf16[2,345,6,1]{3,1,2,0:T(8,128)(2,1)S(1)} %get-tuple-element.13), kind=kOutput, calls=%fused_computation.111 | convolution fusion | flops 365998080 | bytes 5521408 | tf_op jit(solution)/shard_map/oc,tcrw->torw/dot_general | solution.py:37
  41.8 1.3 %fusion.63 = f32[2,4,256,256]{3,2,1,0:T(8,128)S(1)} fusion(bf16[3,3,256,345]{2,3,1,0:T(8,128)(2,1)S(1)} %copy-done.1, bf16[2,345,6,255]{3,1,2,0:T(8,128)(2,1)S(1)} %get-tuple-element.15, bf16[2,345,6,1]{3,1,2,0:T(8,128)(2,1)S(1)} %get-tuple-element.13), kind=kOutput, calls=%fused_computation.109 | convolution fusion | flops 365998080 | bytes 5521408 | tf_op jit(solution)/shard_map/oc,tcrw->torw/dot_general | solution.py:37
  43.1 1.3 %fusion.67 = f32[2,4,256,256]{3,2,1,0:T(8,128)S(1)} fusion(bf16[3,3,256,345]{2,3,1,0:T(8,128)(2,1)S(1)} %copy-done.1, bf16[2,345,6,255]{3,1,2,0:T(8,128)(2,1)S(1)} %get-tuple-element.15, bf16[2,345,6,1]{3,1,2,0:T(8,128)(2,1)S(1)} %get-tuple-element.13), kind=kOutput, calls=%fused_computation.113 | convolution fusion | flops 365998080 | bytes 5521408 | tf_op jit(solution)/shard_map/oc,tcrw->torw/dot_general | solution.py:37
  44.4 1.0 fusion.54
  45.5 1.0 fusion.52
  46.5 1.0 fusion.56
  47.6 1.7 %fusion.4 = (bf16[2,256,4,256]{1,3,2,0:T(8,128)(2,1)S(1)}, f32[2,4,256,256]{3,2,1,0:T(8,128)S(1)}) fusion(f32[256]{0:T(256)S(1)} %copy-done.7, f32[2,4,256,256]{3,2,1,0:T(8,128)S(1)} %fusion.52, f32[2,4,256,256]{3,2,1,0:T(8,128)S(1)} %fusion.54, f32[2,4,256,256]{3,2,1,0:T(8,128)S(1)} %fusion.56, bf16[2,345,6,256]{3,1,2,0:T(8,128)(2,1)S(1)} %concatenate.68, ...), kind=kOutput, calls=%fused_computation.11 | convolution fusion | flops 369098752 | bytes 22266880 | tf_op jit(solution)/shard_map/oc,tcrw->torw/dot_general | solution.py:37
  49.3 1.9 %collective-permute-start.4 = (bf16[2,256,1,256]{1,3,2,0:T(8,128)(2,1)S(1)}, bf16[2,256,1,256]{1,3,2,0:T(8,128)(2,1)S(1)}, u32[]{:S(2)}, u32[]{:S(2)}) collective-permute-start(bf16[2,256,1,256]{1,3,2,0:T(8,128)(2,1)S(1)} %get-tuple-element.30), channel_id=1, source_target_pairs={{0,1},{1,2},{2,3},{3,4},{4,5},{5,6},{6,7},{8,9},{9,10},{10,11},{11... | collective-permute-start | bytes 786440 | tf_op jit(solution)/shard_map/ppermute | solution.py:16
  51.2 2.6 %collective-permute-start.5 = (bf16[2,256,1,256]{1,3,2,0:T(8,128)(2,1)S(1)}, bf16[2,256,1,256]{1,3,2,0:T(8,128)(2,1)S(1)}, u32[]{:S(2)}, u32[]{:S(2)}) collective-permute-start(bf16[2,256,1,256]{1,3,2,0:T(8,128)(2,1)S(1)} %get-tuple-element.31), channel_id=1, source_target_pairs={{1,0},{2,1},{3,2},{4,3},{5,4},{6,5},{7,6},{9,8},{10,9},{11,10},{12... | collective-permute-start | bytes 786440 | tf_op jit(solution)/shard_map/ppermute | solution.py:19
  54.5 4.4 %collective-permute-done.5 = bf16[2,256,1,256]{1,3,2,0:T(8,128)(2,1)S(1)} collective-permute-done((bf16[2,256,1,256]{1,3,2,0:T(8,128)(2,1)S(1)}, bf16[2,256,1,256]{1,3,2,0:T(8,128)(2,1)S(1)}, u32[]{:S(2)}, u32[]{:S(2)}) %collective-permute-start.5) | collective-permute-done | bytes 262176 | tf_op jit(solution)/shard_map/ppermute | solution.py:19
  59.1 0.6 fusion.125
  59.7 0.8 fusion.10
  60.9 0.4 fusion.97
  61.4 0.4 fusion.85
  63.2 0.4 fusion.11
  63.8 0.7 fusion.36
  64.5 1.9 %collective-permute-start.6 = (bf16[2,69,1,256]{3,1,2,0:T(8,128)(2,1)S(1)}, bf16[2,69,1,256]{3,1,2,0:T(8,128)(2,1)S(1)}, u32[]{:S(2)}, u32[]{:S(2)}) collective-permute-start(bf16[2,69,1,256]{3,1,2,0:T(8,128)(2,1)S(1)} %get-tuple-element.40), channel_id=1, source_target_pairs={{0,1},{1,2},{2,3},{3,4},{4,5},{5,6},{6,7},{8,9},{9,10},{10,11},{11... | collective-permute-start | bytes 211976 | tf_op jit(solution)/shard_map/ppermute | solution.py:16
  66.4 2.4 %collective-permute-start.7 = (bf16[2,69,1,256]{3,1,2,0:T(8,128)(2,1)S(1)}, bf16[2,69,1,256]{3,1,2,0:T(8,128)(2,1)S(1)}, u32[]{:S(2)}, u32[]{:S(2)}) collective-permute-start(bf16[2,69,1,256]{3,1,2,0:T(8,128)(2,1)S(1)} %get-tuple-element.41), channel_id=1, source_target_pairs={{1,0},{2,1},{3,2},{4,3},{5,4},{6,5},{7,6},{9,8},{10,9},{11,10},{12... | collective-permute-start | bytes 211976 | tf_op jit(solution)/shard_map/ppermute | solution.py:19
  68.8 0.5 fusion.81
  69.3 2.8 %collective-permute-done.7 = bf16[2,69,1,256]{3,1,2,0:T(8,128)(2,1)S(1)} collective-permute-done((bf16[2,69,1,256]{3,1,2,0:T(8,128)(2,1)S(1)}, bf16[2,69,1,256]{3,1,2,0:T(8,128)(2,1)S(1)}, u32[]{:S(2)}, u32[]{:S(2)}) %collective-permute-start.7) | collective-permute-done | bytes 70688 | tf_op jit(solution)/shard_map/ppermute | solution.py:19
  72.5 0.8 fusion.83
  73.3 0.8 fusion.82
  74.1 0.8 fusion.84
  75.0 0.6 fusion.79
  75.6 0.6 fusion.78
  76.2 0.6 fusion.80
  76.9 0.5 fusion.38
  77.4 1.5 %fusion = bf16[2,256,4,256]{1,3,2,0:T(8,128)(2,1)S(1)} fusion(f32[2,4,256,256]{3,2,1,0:T(8,128)S(1)} %get-tuple-element.43, f32[2,4,256,256]{3,2,1,0:T(8,128)S(1)} %fusion.78, f32[2,4,256,256]{3,2,1,0:T(8,128)S(1)} %fusion.79, f32[2,4,256,256]{3,2,1,0:T(8,128)S(1)} %fusion.80, f32[2,4,256,256]{3,2,1,0:T(8,128)S(1)} %fusion.81, ...), kind=kOutput, calls=%fused_computation.4 | convolution fusion | flops 81971200 | bytes 20328448 | tf_op jit(solution)/shard_map/oc,tcrw->torw/dot_general | solution.py:37
  78.9 1.9 %collective-permute-start.8 = (bf16[2,256,1,256]{1,3,2,0:T(8,128)(2,1)S(1)}, bf16[2,256,1,256]{1,3,2,0:T(8,128)(2,1)S(1)}, u32[]{:S(2)}, u32[]{:S(2)}) collective-permute-start(bf16[2,256,1,256]{1,3,2,0:T(8,128)(2,1)S(1)} %get-tuple-element.28), channel_id=1, source_target_pairs={{0,1},{1,2},{2,3},{3,4},{4,5},{5,6},{6,7},{8,9},{9,10},{10,11},{11... | collective-permute-start | bytes 786440 | tf_op jit(solution)/shard_map/ppermute | solution.py:16
  80.9 2.6 %collective-permute-start.9 = (bf16[2,256,1,256]{1,3,2,0:T(8,128)(2,1)S(1)}, bf16[2,256,1,256]{1,3,2,0:T(8,128)(2,1)S(1)}, u32[]{:S(2)}, u32[]{:S(2)}) collective-permute-start(bf16[2,256,1,256]{1,3,2,0:T(8,128)(2,1)S(1)} %get-tuple-element.29), channel_id=1, source_target_pairs={{1,0},{2,1},{3,2},{4,3},{5,4},{6,5},{7,6},{9,8},{10,9},{11,10},{12... | collective-permute-start | bytes 786440 | tf_op jit(solution)/shard_map/ppermute | solution.py:19
  83.5 2.1 %fusion.48 = f32[2,4,256,345]{2,3,1,0:T(8,128)} fusion(bf16[2,256,4,256]{1,3,2,0:T(8,128)(2,1)S(1)} %fusion, bf16[3,3,345,256]{3,2,1,0:T(8,128)(2,1)S(1)} %copy-done.2), kind=kOutput, calls=%fused_computation.90 | convolution fusion | flops 361758720 | bytes 4055040 | tf_op jit(solution)/shard_map/oc,tcrw->torw/dot_general | solution.py:37
  85.7 2.9 %collective-permute-done.9 = bf16[2,256,1,256]{1,3,2,0:T(8,128)(2,1)S(1)} collective-permute-done((bf16[2,256,1,256]{1,3,2,0:T(8,128)(2,1)S(1)}, bf16[2,256,1,256]{1,3,2,0:T(8,128)(2,1)S(1)}, u32[]{:S(2)}, u32[]{:S(2)}) %collective-permute-start.9) | collective-permute-done | bytes 262176 | tf_op jit(solution)/shard_map/ppermute | solution.py:19
  88.8 0.5 fusion.124
  89.3 0.6 fusion.50
  89.9 0.6 fusion.49
  90.5 0.6 fusion.51
  91.1 0.6 fusion.46
  91.6 0.6 fusion.47
  92.2 0.6 fusion.23
  92.8 0.6 fusion.19
  93.4 2.8 %add_bitcast_fusion = f32[2,345,4,256]{3,1,2,0:T(8,128)S(1)} fusion(f32[2,4,256,345]{2,3,1,0:T(8,128)S(1)} %fusion.46, f32[2,4,256,345]{2,3,1,0:T(8,128)S(1)} %fusion.47, f32[2,4,256,345]{2,3,1,0:T(8,128)S(1)} %fusion.23, f32[2,4,256,345]{2,3,1,0:T(8,128)} %fusion.48, f32[2,4,256,345]{2,3,1,0:T(8,128)S(1)} %fusion.19, f32[2,4,256,345]{2,3,1,0:T(8,128)S(1)} %fusion.49, ...), kind=kOutput, calls=%fused_computation | convolution fusion | flops 373702656 | bytes 28813312 | tf_op jit(solution)/shard_map/oc,tcrw->torw/dot_general | solution.py:37
  96.2 1.8 %copy.54 = f32[2,345,4,256]{3,2,1,0:T(4,128)S(1)} copy(f32[2,345,4,256]{3,1,2,0:T(8,128)S(1)} %add_bitcast_fusion) | data formatting | bytes 5652480 | tf_op jit(solution)/shard_map/add | solution.py:40
  98.0 0.5 slice_bitcast_fusion.4
  98.5 0.5 fusion.121
  99.2 2.2 %collective-permute-start.10 = (bf16[2,69,4,256]{3,2,1,0:T(4,128)(2,1)S(1)}, bf16[2,69,4,256]{3,2,1,0:T(4,128)(2,1)S(1)}, u32[]{:S(2)}, u32[]{:S(2)}) collective-permute-start(bf16[2,69,4,256]{3,2,1,0:T(4,128)(2,1)S(1)} %get-tuple-element.34), channel_id=1, source_target_pairs={{0,24},{8,0},{16,8},{24,16},{1,25},{9,1},{17,9},{25,17},{2,26},{10... | collective-permute-start | bytes 847880 | tf_op jit(solution)/shard_map/ppermute | solution.py:27
  101.5 1.0 copy.59
  102.5 5.6 %collective-permute-done.10 = bf16[2,69,4,256]{3,2,1,0:T(4,128)(2,1)S(1)} collective-permute-done((bf16[2,69,4,256]{3,2,1,0:T(4,128)(2,1)S(1)}, bf16[2,69,4,256]{3,2,1,0:T(4,128)(2,1)S(1)}, u32[]{:S(2)}, u32[]{:S(2)}) %collective-permute-start.10) | collective-permute-done | bytes 282656 | tf_op jit(solution)/shard_map/ppermute | solution.py:27
  108.0 5.8 %collective-permute-done.11 = bf16[2,69,4,256]{3,2,1,0:T(4,128)(2,1)S(1)} collective-permute-done((bf16[2,69,4,256]{3,2,1,0:T(4,128)(2,1)S(1)}, bf16[2,69,4,256]{3,2,1,0:T(4,128)(2,1)S(1)}, u32[]{:S(2)}, u32[]{:S(2)}) %collective-permute-start.11) | collective-permute-done | bytes 282656 | tf_op jit(solution)/shard_map/ppermute | solution.py:27
  113.9 1.0 fusion.37
  (40 shorter events, 4.3 us)
Async XLA Ops:
  0.6 22.1 %copy-start.4 = (bf16[3,3,69,256]{3,2,1,0:T(8,128)(2,1)S(1)}, bf16[3,3,69,256]{3,2,1,0:T(8,128)(2,1)}, u32[]{:S(2)}) copy-start(bf16[3,3,69,256]{3,2,1,0:T(8,128)(2,1)} %param.10) | copy-start | bytes 953860
  0.6 22.9 %copy-start = (bf16[3,3,256,345]{2,3,1,0:T(8,128)(2,1)S(1)}, bf16[3,3,256,345]{2,3,1,0:T(8,128)(2,1)}, u32[]{:S(2)}) copy-start(bf16[3,3,256,345]{2,3,1,0:T(8,128)(2,1)} %param.8) | copy-start | bytes 4769284
  1.9 7.9 %collective-permute-start.1 = (bf16[2,69,4,256]{3,1,2,0:T(8,128)(2,1)S(1)}, bf16[2,69,4,256]{3,1,2,0:T(8,128)(2,1)S(1)}, u32[]{:S(2)}, u32[]{:S(2)}) collective-permute-start(bf16[2,69,4,256]{3,1,2,0:T(8,128)(2,1)S(1)} %copy.122), channel_id=1, source_target_pairs={{8,0},{16,8},{24,16},{0,24},{9,1},{17,9},{25,17},{1,25},{10,2},{18... | collective-permute-start | bytes 847880 | tf_op jit(solution)/shard_map/ppermute | solution.py:19
  3.1 13.0 %collective-permute-start = (bf16[2,69,4,256]{3,1,2,0:T(8,128)(2,1)S(1)}, bf16[2,69,4,256]{3,1,2,0:T(8,128)(2,1)S(1)}, u32[]{:S(2)}, u32[]{:S(2)}) collective-permute-start(bf16[2,69,4,256]{3,1,2,0:T(8,128)(2,1)S(1)} %copy.122), channel_id=1, source_target_pairs={{0,8},{8,16},{16,24},{24,0},{1,9},{9,17},{17,25},{25,1},{2,10},{10... | collective-permute-start | bytes 847880 | tf_op jit(solution)/shard_map/ppermute | solution.py:16
  16.2 8.6 %collective-permute-start.2 = (bf16[6,69,1,256]{3,1,2,0:T(8,128)(2,1)S(1)}, bf16[6,69,1,256]{3,1,2,0:T(8,128)(2,1)S(1)}, u32[]{:S(2)}, u32[]{:S(2)}) collective-permute-start(bf16[6,69,1,256]{3,1,2,0:T(8,128)(2,1)S(1)} %get-tuple-element.32), channel_id=1, source_target_pairs={{0,1},{1,2},{2,3},{3,4},{4,5},{5,6},{6,7},{8,9},{9,10},{10,11},{11... | collective-permute-start | bytes 635912 | tf_op jit(solution)/shard_map/ppermute | solution.py:16
  20.8 7.3 %collective-permute-start.3 = (bf16[6,69,1,256]{3,1,2,0:T(8,128)(2,1)S(1)}, bf16[6,69,1,256]{3,1,2,0:T(8,128)(2,1)S(1)}, u32[]{:S(2)}, u32[]{:S(2)}) collective-permute-start(bf16[6,69,1,256]{3,1,2,0:T(8,128)(2,1)S(1)} %get-tuple-element.33), channel_id=1, source_target_pairs={{1,0},{2,1},{3,2},{4,3},{5,4},{6,5},{7,6},{9,8},{10,9},{11,10},{12... | collective-permute-start | bytes 635912 | tf_op jit(solution)/shard_map/ppermute | solution.py:19
  36.2 1.8 %copy-start.1 = (bf16[3,3,256,345]{2,3,1,0:T(8,128)(2,1)S(1)}, bf16[3,3,256,345]{2,3,1,0:T(8,128)(2,1)}, u32[]{:S(2)}) copy-start(bf16[3,3,256,345]{2,3,1,0:T(8,128)(2,1)} %param.8) | copy-start | bytes 4769284
  46.5 1.0 copy-start.7
  47.6 6.3 %copy-start.5 = (bf16[3,3,69,256]{3,2,1,0:T(8,128)(2,1)S(1)}, bf16[3,3,69,256]{3,2,1,0:T(8,128)(2,1)}, u32[]{:S(2)}) copy-start(bf16[3,3,69,256]{3,2,1,0:T(8,128)(2,1)} %param.10) | copy-start | bytes 953860
  49.3 5.2 %collective-permute-start.4 = (bf16[2,256,1,256]{1,3,2,0:T(8,128)(2,1)S(1)}, bf16[2,256,1,256]{1,3,2,0:T(8,128)(2,1)S(1)}, u32[]{:S(2)}, u32[]{:S(2)}) collective-permute-start(bf16[2,256,1,256]{1,3,2,0:T(8,128)(2,1)S(1)} %get-tuple-element.30), channel_id=1, source_target_pairs={{0,1},{1,2},{2,3},{3,4},{4,5},{5,6},{6,7},{8,9},{9,10},{10,11},{11... | collective-permute-start | bytes 786440 | tf_op jit(solution)/shard_map/ppermute | solution.py:16
  51.2 7.7 %collective-permute-start.5 = (bf16[2,256,1,256]{1,3,2,0:T(8,128)(2,1)S(1)}, bf16[2,256,1,256]{1,3,2,0:T(8,128)(2,1)S(1)}, u32[]{:S(2)}, u32[]{:S(2)}) collective-permute-start(bf16[2,256,1,256]{1,3,2,0:T(8,128)(2,1)S(1)} %get-tuple-element.31), channel_id=1, source_target_pairs={{1,0},{2,1},{3,2},{4,3},{5,4},{6,5},{7,6},{9,8},{10,9},{11,10},{12... | collective-permute-start | bytes 786440 | tf_op jit(solution)/shard_map/ppermute | solution.py:19
  62.7 1.1 copy-start.6
  62.7 1.1 copy-start.8
  63.8 5.0 %copy-start.3 = (bf16[3,3,256,69]{2,3,1,0:T(8,128)(2,1)S(1)}, bf16[3,3,256,69]{2,3,1,0:T(8,128)(2,1)}, u32[]{:S(2)}) copy-start(bf16[3,3,256,69]{2,3,1,0:T(8,128)(2,1)} %reverse_bitcast_fusion.1) | copy-start | bytes 953860
  64.5 4.8 %collective-permute-start.6 = (bf16[2,69,1,256]{3,1,2,0:T(8,128)(2,1)S(1)}, bf16[2,69,1,256]{3,1,2,0:T(8,128)(2,1)S(1)}, u32[]{:S(2)}, u32[]{:S(2)}) collective-permute-start(bf16[2,69,1,256]{3,1,2,0:T(8,128)(2,1)S(1)} %get-tuple-element.40), channel_id=1, source_target_pairs={{0,1},{1,2},{2,3},{3,4},{4,5},{5,6},{6,7},{8,9},{9,10},{10,11},{11... | collective-permute-start | bytes 211976 | tf_op jit(solution)/shard_map/ppermute | solution.py:16
  66.4 5.7 %collective-permute-start.7 = (bf16[2,69,1,256]{3,1,2,0:T(8,128)(2,1)S(1)}, bf16[2,69,1,256]{3,1,2,0:T(8,128)(2,1)S(1)}, u32[]{:S(2)}, u32[]{:S(2)}) collective-permute-start(bf16[2,69,1,256]{3,1,2,0:T(8,128)(2,1)S(1)} %get-tuple-element.41), channel_id=1, source_target_pairs={{1,0},{2,1},{3,2},{4,3},{5,4},{6,5},{7,6},{9,8},{10,9},{11,10},{12... | collective-permute-start | bytes 211976 | tf_op jit(solution)/shard_map/ppermute | solution.py:19
  77.3 6.2 %copy-start.2 = (bf16[3,3,345,256]{3,2,1,0:T(8,128)(2,1)S(1)}, bf16[3,3,345,256]{3,2,1,0:T(8,128)(2,1)}, u32[]{:S(2)}) copy-start(bf16[3,3,345,256]{3,2,1,0:T(8,128)(2,1)} %reverse_bitcast_fusion) | copy-start | bytes 4769284
  78.9 6.7 %collective-permute-start.8 = (bf16[2,256,1,256]{1,3,2,0:T(8,128)(2,1)S(1)}, bf16[2,256,1,256]{1,3,2,0:T(8,128)(2,1)S(1)}, u32[]{:S(2)}, u32[]{:S(2)}) collective-permute-start(bf16[2,256,1,256]{1,3,2,0:T(8,128)(2,1)S(1)} %get-tuple-element.28), channel_id=1, source_target_pairs={{0,1},{1,2},{2,3},{3,4},{4,5},{5,6},{6,7},{8,9},{9,10},{10,11},{11... | collective-permute-start | bytes 786440 | tf_op jit(solution)/shard_map/ppermute | solution.py:16
  80.9 7.7 %collective-permute-start.9 = (bf16[2,256,1,256]{1,3,2,0:T(8,128)(2,1)S(1)}, bf16[2,256,1,256]{1,3,2,0:T(8,128)(2,1)S(1)}, u32[]{:S(2)}, u32[]{:S(2)}) collective-permute-start(bf16[2,256,1,256]{1,3,2,0:T(8,128)(2,1)S(1)} %get-tuple-element.29), channel_id=1, source_target_pairs={{1,0},{2,1},{3,2},{4,3},{5,4},{6,5},{7,6},{9,8},{10,9},{11,10},{12... | collective-permute-start | bytes 786440 | tf_op jit(solution)/shard_map/ppermute | solution.py:19
  99.2 8.8 %collective-permute-start.10 = (bf16[2,69,4,256]{3,2,1,0:T(4,128)(2,1)S(1)}, bf16[2,69,4,256]{3,2,1,0:T(4,128)(2,1)S(1)}, u32[]{:S(2)}, u32[]{:S(2)}) collective-permute-start(bf16[2,69,4,256]{3,2,1,0:T(4,128)(2,1)S(1)} %get-tuple-element.34), channel_id=1, source_target_pairs={{0,24},{8,0},{16,8},{24,16},{1,25},{9,1},{17,9},{25,17},{2,26},{10... | collective-permute-start | bytes 847880 | tf_op jit(solution)/shard_map/ppermute | solution.py:27
  101.5 12.4 %collective-permute-start.11 = (bf16[2,69,4,256]{3,2,1,0:T(4,128)(2,1)S(1)}, bf16[2,69,4,256]{3,2,1,0:T(4,128)(2,1)S(1)}, u32[]{:S(2)}, u32[]{:S(2)}) collective-permute-start(bf16[2,69,4,256]{3,2,1,0:T(4,128)(2,1)S(1)} %get-tuple-element.35), channel_id=1, source_target_pairs={{0,8},{8,16},{16,24},{24,0},{1,9},{9,17},{17,25},{25,1},{2,10},{10... | collective-permute-start | bytes 847880 | tf_op jit(solution)/shard_map/ppermute | solution.py:27
where the time goes:
time: 115 us
  waiting for transfers between devices  37.7 us (33%)
  matrix products  31.2 us (27%)
  starting transfers between devices  23.7 us (21%)
  local copies, waits for them, and re-layouts  18.2 us (16%)
  other arithmetic  3.02 us (3%)
    dot_general x36, matrix products, convolve(): jnp.einsum('oc,tcrw->torw', weights[i, j], band, preferred_element_type=j...  31.2 us
    ppermute x5, waiting for transfers between devices, with_halo(): lax.ppermute(lax.slice_in_dim(block, 0, width, axis=dim), axis, backward)  19.7 us
    ppermute x2, waiting for transfers between devices, from_behind(): return lax.ppermute(value, axis, pairs)  11.4 us
    ppermute x5, starting transfers between devices, with_halo(): lax.ppermute(lax.slice_in_dim(block, 0, width, axis=dim), axis, backward)  10.7 us
    ppermute x5, starting transfers between devices, with_halo(): lax.ppermute(lax.slice_in_dim(block, block.shape[dim] - width, None, axis...  10.7 us
    concatenate x1, local copies, waits for them, and re-layouts, gather_windows(): jnp.concatenate([extended[k:k + count] for k in range(WINDOW)], axis=1)  6.83 us
    ppermute x5, waiting for transfers between devices, with_halo(): lax.ppermute(lax.slice_in_dim(block, block.shape[dim] - width, None, axis...  6.52 us
    slice x6, local copies, waits for them, and re-layouts, convolve(): moved = jnp.roll(padded, 1 - j, axis=3)  3.21 us
  transfers between devices with their start and end apart: 12, of which 9 were waited for; matrix products, arithmetic and copies ran while one was open for 5% of the time, Pallas kernels for 0%

commit v1 on v0

v1 whole, which is shorter than its diff:
```python
import functools

import jax
import jax.numpy as jnp
from jax import lax
from jax.experimental import pallas as pl
from jax.experimental.pallas import tpu as pltpu
from jax.sharding import PartitionSpec as P

F32 = jnp.float32
BF16 = jnp.bfloat16
LANES = 128
DEPTH = 4
REACH = 2
VMEM = pl.BlockSpec(memory_space=pltpu.VMEM)
SMEM = pl.BlockSpec(memory_space=pltpu.SMEM)


def up(value, step):
    return -(-value // step) * step


class Plan:
    def __init__(self, states, conv_in):
        self.n = lax.axis_size("tm")
        self.m = lax.axis_size("lat")
        self.local, self.chans, self.rows, self.lon = states.shape
        self.taps = conv_in.shape[0]
        self.hidden = conv_in.shape[2]
        self.window = conv_in.shape[3] // self.chans
        self.side = self.window // 2
        self.total = self.local * self.n
        self.wc = self.lon // self.n
        self.wx = self.wc + 2 * DEPTH
        self.wp = up(self.wx, 16)
        self.cp = up(self.chans, 8)
        self.packed = 2 * LANES
        self.pos = self.rows * self.local * self.wx
        self.posp = up(self.pos, LANES)
        self.half = REACH * self.local * self.wx
        self.cut = (self.pos - self.half) // LANES * LANES
        self.msg = max(self.posp - self.cut, up(self.half, LANES))
        self.cut = self.posp - self.msg
        self.shift = self.pos - self.half - self.cut
        self.out = self.rows * self.local * self.wc
        assert self.taps == 3 and LANES <= 2 * self.chans and 3 * self.chans <= self.packed
        assert self.out % LANES == 0 and LANES % self.wc == 0 and self.wx % 8 == 0
        assert self.lon % LANES == 0 and self.rows >= 2 * REACH and self.n & (self.n - 1) == 0

    def at(self, row, t):
        return (row * self.local + t) * self.wx


def call(kernel, outs, scratch, args, limit=48 << 20, name=None, cost=None):
    scalars = [SMEM if a.dtype == jnp.int32 else VMEM for a in args]
    return pl.pallas_call(
        kernel,
        out_shape=outs,
        in_specs=scalars,
        out_specs=[VMEM] * len(outs),
        scratch_shapes=scratch,
        compiler_params=pltpu.CompilerParams(vmem_limit_bytes=limit),
        name=name,
        cost_estimate=cost,
    )(*args)


def lanes_of(shape):
    return lax.broadcasted_iota(jnp.int32, shape, len(shape) - 1)


def split_kernel(p, where_ref, x_ref, *refs):
    outs, held = refs[: p.n], refs[p.n]
    me = where_ref[0]
    held[...] = jnp.zeros_like(held)
    for r in range(p.rows):
        for t in range(p.local):
            v = x_ref[t, r].astype(F32)
            start = p.at(r, t)
            base, off = start // LANES * LANES, start % LANES
            width = LANES if off + p.wx <= LANES else 2 * LANES
            lane = lanes_of((p.chans, width))
            inside = (lane >= off) & (lane < off + p.wx)
            for q in range(p.n):
                y = pltpu.roll(v, (off + DEPTH - p.wc * q) % p.lon, 1)[:, :width]
                old = held[q, : p.chans, base : base + width]
                held[q, : p.chans, base : base + width] = jnp.where(inside, y, old)
    for d in range(p.n):
        outs[d][...] = held[me ^ d].astype(outs[d].dtype)


def to_columns(block, rows_ref):
    depth, width = block.shape
    for m in range(width // LANES):
        tile = block[:, m * LANES : (m + 1) * LANES].astype(F32)
        tile = jnp.concatenate([tile, jnp.zeros((LANES - depth, LANES), F32)], axis=0)
        rows_ref[8 + m * LANES : 8 + (m + 1) * LANES, :] = tile.T


def taps_of(p, rows_ref, start, flip):
    v = [rows_ref[8 + start + j : 8 + start + j + p.wp, :] for j in (-1, 0, 1)]
    if flip:
        v = v[::-1]
    lane = lanes_of((p.wp, LANES))
    middle = pltpu.roll(v[1], p.chans, 1)
    low = jnp.where(lane < p.chans, v[0], middle)
    high = jnp.where(lane < 2 * p.chans - LANES, middle, pltpu.roll(v[2], 2 * p.chans - LANES, 1))
    return jnp.concatenate([low, high], axis=1).astype(BF16)


def untap(p, ref, lead, start, count, flip):
    before, after = (1, -1) if flip else (-1, 1)
    s = start
    first = ref[lead, s + before : s + before + count, :LANES]
    low = pltpu.roll(ref[lead, s : s + count, :LANES], LANES - p.chans, 1)
    high = pltpu.roll(ref[lead, s : s + count, LANES:], LANES - p.chans, 1)
    lane = lanes_of((count, LANES))
    middle = jnp.where(lane < LANES - p.chans, low, high)
    last = pltpu.roll(ref[lead, s + after : s + after + count, LANES:], 2 * LANES - 2 * p.chans, 1)
    return jnp.where(lane < p.chans, first + middle + last, 0.0)


def fill_taps(p, where_ref, blocks, near, far, rows_ref, taps_ref, flip, base):
    me, even = where_ref[0], where_ref[1] == 1
    for d in range(p.n):
        t0 = (me ^ d) * p.local + base
        to_columns(blocks[d][...], rows_ref)
        for r in range(p.rows):
            for t in range(p.local):
                taps_ref[REACH + r, t0 + t] = taps_of(p, rows_ref, p.at(r, t), flip)
        below = jnp.where(even, far[d], near[d])
        to_columns(below, rows_ref)
        for r in range(REACH):
            for t in range(p.local):
                taps_ref[r, t0 + t] = taps_of(p, rows_ref, p.shift + p.at(r, t), flip)
        above = jnp.where(even, near[d], far[d])
        to_columns(above, rows_ref)
        for r in range(REACH):
            for t in range(p.local):
                taps_ref[REACH + p.rows + r, t0 + t] = taps_of(p, rows_ref, p.at(r, t), flip)


def row_mask(p, where_ref, row):
    outside = ((row == 0) & (where_ref[2] == 1)) | ((row == p.rows + 1) & (where_ref[3] == 1))
    return jnp.where(outside, 0.0, 1.0)


def dot(a, b, transposed):
    dims = (((1,), (1 if transposed else 0,)), ((), ()))
    return lax.dot_general(a, b, dims, preferred_element_type=F32)


def forward_kernel(p, where_ref, *refs):
    n = p.n
    blocks, near, far, targets = refs[:n], refs[n], refs[n + 1], refs[n + 2 : 2 * n + 2]
    w_in, bias_in, w_out, bias_out = refs[2 * n + 2 : 2 * n + 6]
    slope_ref, own_ref = refs[2 * n + 6 : 2 * n + 8]
    scores = refs[2 * n + 8 : 3 * n + 7]
    resids = refs[3 * n + 7 : 4 * n + 7]
    rows_ref, taps_ref, act_ref, part_ref, wide_ref, thin_ref = refs[4 * n + 7 :]
    me = where_ref[0]
    flat = p.total * p.wp
    fill_taps(p, where_ref, blocks, near, far, rows_ref, taps_ref, False, p.side)
    for e in range(p.side):
        taps_ref[:, e] = taps_ref[:, p.total + e]
        taps_ref[:, p.total + p.side + e] = taps_ref[:, p.side + e]

    def hidden_row(row, carry):
        total = None
        for i in range(p.taps):
            for k in range(p.window):
                a = taps_ref[row + i, k : k + p.total].reshape(flat, p.packed)
                term = dot(a, w_in[i * p.window + k], True)
                total = term if total is None else total + term
        pre = total + bias_in[...]
        sig = 0.5 * jnp.tanh(0.5 * pre) + 0.5
        act = pre * sig
        slope = sig + act * (1.0 - sig)
        mask = row_mask(p, where_ref, row)
        act_ref[row] = (act * mask).astype(BF16).reshape(p.total, p.wp, p.hidden)
        slope_ref[row] = (slope * mask).reshape(p.total, p.wp, p.hidden)
        return carry

    lax.fori_loop(0, p.rows + 2, hidden_row, 0)
    wide_ref[...] = jnp.zeros_like(wide_ref)

    def score_row(row, carry):
        total = None
        for i in range(p.taps):
            term = dot(act_ref[row + i].reshape(flat, p.hidden), w_out[i], True)
            total = term if total is None else total + term
        part_ref[:, 8 : 8 + p.wp, :] = total.reshape(p.total, p.wp, p.packed)
        for d in range(n):
            for t in range(p.local):
                s = untap(p, part_ref, (me ^ d) * p.local + t, 8, p.wx, False) + bias_out[...]
                wide_ref[d, pl.ds(pl.multiple_of((row * p.local + t) * p.wx, 8), p.wx), :] = s
                thin_ref[d, pl.ds(pl.multiple_of((row * p.local + t) * p.wc, 8), p.wc), :] = s[DEPTH : DEPTH + p.wc]
        return carry

    lax.fori_loop(0, p.rows, score_row, 0)
    for d in range(n):
        for m in range(p.posp // LANES):
            cols = slice(m * LANES, (m + 1) * LANES)
            tile = wide_ref[d, cols, :].T[: p.cp]
            resids[d][:, cols] = (tile - targets[d][:, cols]).astype(BF16)
        for m in range(p.out // LANES):
            cols = slice(m * LANES, (m + 1) * LANES)
            tile = thin_ref[d, cols, :].T[: p.cp]
            if d == 0:
                own_ref[:, cols] = tile
            else:
                scores[d - 1][:, cols] = tile.astype(BF16)


def backward_kernel(p, where_ref, *refs):
    n = p.n
    blocks, near, far = refs[:n], refs[n], refs[n + 1]
    slope_ref, w_in, w_out, own_ref = refs[n + 2 : n + 6]
    outs = refs[n + 6 : 2 * n + 5]
    rows_ref, taps_ref, grad_ref, part_ref, thin_ref = refs[2 * n + 5 :]
    me = where_ref[0]
    flat = p.total * p.wp
    fill_taps(p, where_ref, blocks, near, far, rows_ref, taps_ref, True, 0)

    def hidden_row(row, carry):
        total = None
        for i in range(p.taps):
            a = taps_ref[row + 2 - i].reshape(flat, p.packed)
            term = dot(a, w_out[i], False)
            total = term if total is None else total + term
        grad = total.reshape(p.total, p.wp, p.hidden) * slope_ref[row]
        grad_ref[row, p.side : p.side + p.total] = grad.astype(BF16)
        return carry

    lax.fori_loop(0, p.rows + 2, hidden_row, 0)
    for e in range(p.side):
        grad_ref[:, e] = grad_ref[:, p.total + e]
        grad_ref[:, p.total + p.side + e] = grad_ref[:, p.side + e]

    def out_row(row, carry):
        total = None
        for i in range(p.taps):
            for k in range(p.window):
                shift = 2 * p.side - k
                a = grad_ref[row + 2 - i, shift : shift + p.total].reshape(flat, p.hidden)
                term = dot(a, w_in[i * p.window + k], False)
                total = term if total is None else total + term
        part_ref[:, 8 : 8 + p.wp, :] = total.reshape(p.total, p.wp, p.packed)
        for d in range(n):
            for t in range(p.local):
                g = untap(p, part_ref, (me ^ d) * p.local + t, 8 + DEPTH, p.wc, True)
                thin_ref[d, pl.ds(pl.multiple_of((row * p.local + t) * p.wc, 8), p.wc), :] = g
        return carry

    lax.fori_loop(0, p.rows, out_row, 0)
    for d in range(n):
        for m in range(p.out // LANES):
            cols = slice(m * LANES, (m + 1) * LANES)
            tile = thin_ref[d, cols, :].T[: p.cp]
            if d == 0:
                own_ref[:, cols] = tile
            else:
                outs[d - 1][:, cols] = tile.astype(BF16)


def join_kernel(p, where_ref, *refs):
    ins, out_ref, held = refs[: p.n], refs[p.n], refs[p.n + 1]
    me = where_ref[0]
    for d in range(p.n):
        held[me ^ d] = ins[d][...].astype(F32)
    per = LANES // p.wc
    for r in range(p.rows):
        for t in range(p.local):
            start = (r * p.local + t) * p.wc
            base, off = start // LANES * LANES, start % LANES
            for m in range(p.lon // LANES):
                tile = None
                for u in range(per):
                    piece = held[m * per + u, : p.chans, base : base + LANES]
                    step = (u * p.wc - off) % LANES
                    if step:
                        piece = pltpu.roll(piece, step, 1)
                    lane = lanes_of((p.chans, LANES))
                    tile = piece if tile is None else jnp.where(lane < u * p.wc, tile, piece)
                out_ref[t, r, :, m * LANES : (m + 1) * LANES] = tile


def send_tm(p, value, d):
    return lax.ppermute(value, "tm", [(i, i ^ d) for i in range(p.n)])


def send_lat(p, even, blocks):
    low = jnp.stack([b[:, : p.msg] for b in blocks])
    high = jnp.stack([b[:, p.cut :] for b in blocks])
    inner = [(i, i ^ 1) for i in range(p.m)]
    outer = [(i, ((i + 1) ^ 1) - 1) for i in range(1, p.m - 1)]
    far = lax.ppermute(jnp.where(even, low, high), "lat", outer)
    near = lax.ppermute(jnp.where(even, high, low), "lat", inner)
    return near, far


def shards(states, observed, conv_in, bias_in, conv_out, bias_out):
    p = Plan(states, conv_in)
    me, row = lax.axis_index("tm"), lax.axis_index("lat")
    even = row % 2 == 0
    where = jnp.stack([me, even.astype(jnp.int32), (row == 0).astype(jnp.int32), (row == p.m - 1).astype(jnp.int32)])
    where = where.astype(jnp.int32)
    sds = jax.ShapeDtypeStruct
    block = sds((p.cp, p.posp), BF16)
    thin = sds((p.cp, p.out), BF16)

    def split(field, dtype, name):
        turned = jnp.transpose(field.astype(dtype), (0, 2, 1, 3))
        scratch = [pltpu.VMEM((p.n, p.cp, p.posp), F32)]
        shape = [sds((p.cp, p.posp), dtype)] * p.n
        return call(functools.partial(split_kernel, p), shape, scratch, [where, turned], 8 << 20, name)

    mine = split(states, BF16, "split_states")
    theirs = [send_tm(p, mine[d], d) for d in range(1, p.n)]
    goal = split(observed, F32, "split_observed")
    goals = [goal[0]] + [send_tm(p, goal[d], d) for d in range(1, p.n)]
    blocks = [mine[0]] + theirs
    w_in = conv_in.reshape(p.taps, p.taps, p.hidden, p.window, p.chans)
    w_in = jnp.transpose(w_in, (0, 3, 2, 1, 4)).reshape(p.taps * p.window, p.hidden, p.taps * p.chans)
    w_in = jnp.pad(w_in, ((0, 0), (0, 0), (0, p.packed - p.taps * p.chans)))
    w_out = conv_out.reshape(p.taps, p.taps * p.chans, p.hidden)
    w_out = jnp.pad(w_out, ((0, 0), (0, p.packed - p.taps * p.chans), (0, 0)))
    b_in = bias_in.reshape(1, p.hidden)
    b_out = jnp.pad(bias_out, (0, LANES - p.chans)).reshape(1, LANES)
    near, far = send_lat(p, even, blocks)

    columns = pltpu.VMEM((p.posp + 32, LANES), F32)
    part = pltpu.VMEM((p.total, p.wp + 16, p.packed), F32)
    thin_rows = pltpu.VMEM((p.n, p.out, LANES), F32)
    deep = p.rows + 2 * REACH
    out = call(
        functools.partial(forward_kernel, p),
        [sds((p.rows + 2, p.total, p.wp, p.hidden), F32), sds((p.cp, p.out), F32)]
        + [thin] * (p.n - 1) + [block] * p.n,
        [
            columns,
            pltpu.VMEM((deep, p.total + 2 * p.side, p.wp, p.packed), BF16),
            pltpu.VMEM((p.rows + 2, p.total, p.wp, p.hidden), BF16),
            part,
            pltpu.VMEM((p.n, p.posp, LANES), F32),
            thin_rows,
        ],
        [where, *blocks, near, far, *goals, w_in, b_in, w_out, b_out],
        name="forward",
    )
    slope, own_scores, away, resids = out[0], out[1], out[2 : p.n + 1], out[p.n + 1 :]
    near, far = send_lat(p, even, resids)
    back = [own_scores] + [send_tm(p, away[d - 1], d) for d in range(1, p.n)]
    out = call(
        functools.partial(backward_kernel, p),
        [sds((p.cp, p.out), F32)] + [thin] * (p.n - 1),
        [
            columns,
            pltpu.VMEM((deep, p.total, p.wp, p.packed), BF16),
            pltpu.VMEM((p.rows + 2, p.total + 2 * p.side, p.wp, p.hidden), BF16),
            part,
            thin_rows,
        ],
        [where, *resids, near, far, slope, w_in, w_out],
        name="backward",
    )
    grads = [out[0]] + [send_tm(p, out[d], d) for d in range(1, p.n)]

    def join(parts, name):
        scratch = [pltpu.VMEM((p.n, p.cp, p.out), F32)]
        shape = [sds((p.local, p.rows, p.chans, p.lon), F32)]
        joined = call(functools.partial(join_kernel, p), shape, scratch, [where, *parts], 8 << 20, name)[0]
        return jnp.transpose(joined, (0, 2, 1, 3))

    return join(back, "join_scores"), join(grads, "join_guidance")


def solution(mesh):
    in_specs = (P("tm", None, "lat", None), P("tm", None, "lat", None), P(), P(), P(), P())
    out_specs = (P("tm", None, "lat", None), P("tm", None, "lat", None))
    return jax.shard_map(shards, mesh=mesh, in_specs=in_specs, out_specs=out_specs, check_vma=False)
```

time: 115 us -> 83.6 us (0.73)
  the two profiles are of different devices: /device:TPU:21 before, /device:TPU:0 now
where the time goes in v1:
time: 83.6 us; the launch traced here: 83.1 us
  Pallas kernels  33.5 us (40%)
  starting transfers between devices  22.5 us (27%)
  local copies, waits for them, and re-layouts  18 us (22%)
  waiting for transfers between devices  6.78 us (8%)
  other arithmetic  1.48 us (2%)
  between operations  0.9 us (1%)
    pallas_call x6, Pallas kernels, call(): pl.pallas_call(kernel, out_shape=outs, in_specs=scalars, out_specs=[VMEM]...  33.5 us
    ppermute x12, starting transfers between devices, send_tm(): return lax.ppermute(value, 'tm', [(i, i ^ d) for i in range(p.n)])  15.2 us
    reshape x2, local copies, waits for them, and re-layouts, shards(): jnp.transpose(w_in, (0, 3, 2, 1, 4))  7.34 us
    ppermute x12, waiting for transfers between devices, send_tm(): return lax.ppermute(value, 'tm', [(i, i ^ d) for i in range(p.n)])  6.77 us
    reshape x2, local copies, waits for them, and re-layouts, shards(): w_in = conv_in.reshape(p.taps, p.taps, p.hidden, p.window, p.chans)  6.34 us
    ppermute x2, starting transfers between devices, send_lat(): near = lax.ppermute(jnp.where(even, high, low), 'lat', inner)  5.98 us
    unnamed x11, local copies, waits for them, and re-layouts  2.19 us
    pad x1, local copies, waits for them, and re-layouts, shards(): w_in = jnp.pad(w_in, ((0, 0), (0, 0), (0, p.packed - p.taps * p.chans)))  1.91 us
  transfers between devices with their start and end apart: 16, of which 3 were waited for; matrix products, arithmetic and copies ran while one was open for 20% of the time, Pallas kernels for 18%

profile of v1, /device:TPU:0, one launch (start us, length us, event | category | flops | bytes accessed | tf_op | source)
XLA Modules:
  0.0 83.1 jit_solution(10825918909433529265)
XLA Ops:
  0.6 0.0 copy-start.1
  0.7 1.2 %convert_element_type.6 = bf16[2,69,4,256]{3,2,1,0:T(4,128)(2,1)S(1)} convert(f32[2,69,4,256]{3,2,1,0:T(4,128)} %param.6) | non-fusion elementwise | flops 141312 | bytes 847872 | tf_op jit(solution)/shard_map/convert_element_type | solution.py:313
  1.9 0.1 pad_add_fusion.where_ref
  2.0 0.8 split_states.1
  2.8 3.0 %collective-permute-start = (bf16[72,640]{1,0:T(8,128)(2,1)S(1)}, bf16[72,640]{1,0:T(8,128)(2,1)S(1)}, u32[]{:S(2)}, u32[]{:S(2)}) collective-permute-start(bf16[72,640]{1,0:T(8,128)(2,1)S(1)} %get-tuple-element.24), channel_id=1, source_target_pairs={{0,8},{8,0},{16,24},{24,16},{1,9},{9,1},{17,25},{25,17},{2,10},{10... | collective-permute-start | bytes 276488 | tf_op jit(solution)/shard_map/ppermute | solution.py:289
  5.8 1.5 %collective-permute-start.1 = (bf16[72,640]{1,0:T(8,128)(2,1)S(1)}, bf16[72,640]{1,0:T(8,128)(2,1)S(1)}, u32[]{:S(2)}, u32[]{:S(2)}) collective-permute-start(bf16[72,640]{1,0:T(8,128)(2,1)S(1)} %get-tuple-element.25), channel_id=1, source_target_pairs={{0,16},{8,24},{16,0},{24,8},{1,17},{9,25},{17,1},{25,9},{2,18},{10... | collective-permute-start | bytes 276488 | tf_op jit(solution)/shard_map/ppermute | solution.py:289
  7.4 0.0 collective-permute-start.2
  7.4 0.0 copy-start.2
  7.4 5.4 %collective-permute-done.2.refs_3_ = bf16[72,640]{1,0:T(8,128)(2,1)S(1)} collective-permute-done((bf16[72,640]{1,0:T(8,128)(2,1)S(1)}, bf16[72,640]{1,0:T(8,128)(2,1)S(1)}, u32[]{:S(2)}, u32[]{:S(2)}) %collective-permute-start.2) | collective-permute-done | bytes 92192 | tf_op jit(solution)/shard_map/ppermute | solution.py:289
  12.8 0.0 collective-permute-done.1.refs_2_
  12.9 0.0 collective-permute-done.refs_1_
  12.9 0.1 broadcast_select_fusion.2
  13.0 0.7 collective-permute-start.4
  13.7 3.0 %collective-permute-start.3 = (bf16[4,72,384]{2,1,0:T(8,128)(2,1)S(1)}, bf16[4,72,384]{2,1,0:T(8,128)(2,1)S(1)}, u32[]{:S(2)}, u32[]{:S(2)}) collective-permute-start(bf16[4,72,384]{2,1,0:T(8,128)(2,1)S(1)} %get-tuple-element.53), channel_id=1, source_target_pairs={{0,1},{1,0},{2,3},{3,2},{4,5},{5,4},{6,7},{7,6},{8,9},{9,8},{10,11... | collective-permute-start | bytes 663560 | tf_op jit(solution)/shard_map/ppermute | solution.py:298
  16.7 0.0 copy-done.1
  16.7 0.1 copy.29
  16.8 1.0 %split_observed.1 = (f32[72,640]{1,0:T(8,128)S(1)}, f32[72,640]{1,0:T(8,128)S(1)}, f32[72,640]{1,0:T(8,128)S(1)}, f32[72,640]{1,0:T(8,128)S(1)}) custom-call(s32[4]{0:T(128)S(1)} %pad_add_fusion.where_ref, f32[2,4,69,256]{3,2,1,0:T(8,128)S(1)} %bitcast.55), custom_call_target="tpu_custom_call" | custom-call | tf_op jit(solution)/shard_map/split_observed/pallas_call | solution.py:56
  17.8 0.6 collective-permute-start.5
  18.4 0.9 %collective-permute-start.6 = (f32[72,640]{1,0:T(8,128)S(1)}, f32[72,640]{1,0:T(8,128)S(1)}, u32[]{:S(2)}, u32[]{:S(2)}) collective-permute-start(f32[72,640]{1,0:T(8,128)S(1)} %get-tuple-element.29), channel_id=1, source_target_pairs={{0,16},{8,24},{16,0},{24,8},{1,17},{9,25},{17,1},{25,9},{2,18},{10... | collective-permute-start | bytes 552968 | tf_op jit(solution)/shard_map/ppermute | solution.py:289
  19.3 2.1 %collective-permute-start.7 = (f32[72,640]{1,0:T(8,128)S(1)}, f32[72,640]{1,0:T(8,128)S(1)}, u32[]{:S(2)}, u32[]{:S(2)}) collective-permute-start(f32[72,640]{1,0:T(8,128)S(1)} %get-tuple-element.30), channel_id=1, source_target_pairs={{0,24},{8,16},{16,8},{24,0},{1,25},{9,17},{17,9},{25,1},{2,26},{10... | collective-permute-start | bytes 552968 | tf_op jit(solution)/shard_map/ppermute | solution.py:289
  21.3 0.0 copy-done.2
  21.3 0.1 reshape.22
  21.4 3.6 %reshape.19 = bf16[3,3,256,5,69]{2,4,3,1,0:T(8,128)(2,1)} reshape(bf16[3,3,256,345]{2,3,1,0:T(8,128)(2,1)} %param.8) | data formatting | bytes 3179520 | tf_op jit(solution)/shard_map/reshape | solution.py:323
  25.0 2.7 %copy.28 = bf16[3,3,256,5,69]{2,4,1,3,0:T(8,128)(2,1)} copy(bf16[3,3,256,5,69]{2,4,3,1,0:T(8,128)(2,1)} %reshape.19) | data formatting | bytes 3179520 | tf_op jit(solution)/shard_map/reshape | solution.py:323
  27.7 3.5 %reshape.20 = bf16[15,256,207]{1,2,0:T(8,128)(2,1)} reshape(bf16[3,5,256,3,69]{2,4,3,1,0:T(8,128)(2,1)} %bitcast.59) | data formatting | bytes 3179520 | tf_op jit(solution)/shard_map/reshape | solution.py:324
  31.3 3.8 %copy.22 = bf16[15,256,207]{2,1,0:T(8,128)(2,1)} copy(bf16[15,256,207]{1,2,0:T(8,128)(2,1)} %reshape.20) | data formatting | bytes 3179520 | tf_op jit(solution)/shard_map/reshape | solution.py:324
  35.1 0.0 copy-start.3
  35.1 0.0 copy-start
  35.1 1.9 %pad.12.refs_10_.refs_7_ = bf16[15,256,256]{2,1,0:T(8,128)(2,1)S(1)} pad(bf16[15,256,207]{2,1,0:T(8,128)(2,1)} %copy.22, bf16[]{:T(256)} %constant.26.clone.1), padding=0_0x0_0x0_49 | pad | bytes 3555842 | tf_op jit(solution)/shard_map/jit(_pad)/pad | solution.py:325
  37.1 0.0 copy-done.3
  37.1 0.0 collective-permute-done.5.refs_7_
  37.1 0.0 collective-permute-done.6.refs_8_
  37.1 0.0 collective-permute-done.7.refs_9_
  37.1 0.0 collective-permute-done.4.refs_5_
  37.1 0.0 collective-permute-done.3.refs_4_
  37.1 0.0 copy-done
  37.1 16.8 %forward.1 = (f32[6,8,80,256]{3,2,1,0:T(8,128)}, f32[72,512]{1,0:T(8,128)S(1)}, bf16[72,512]{1,0:T(8,128)(2,1)S(1)}, bf16[72,512]{1,0:T(8,128)(2,1)S(1)}, bf16[7...) custom-call(s32[4]{0:T(128)S(1)} %pad_add_fusion.where_ref, ...), custom_call_target="tpu_custom_call" | custom-call | tf_op jit(solution)/shard_map/forward/pallas_call | solution.py:56
  54.0 0.1 broadcast_select_fusion
  54.1 0.7 collective-permute-start.12
  54.8 3.0 %collective-permute-start.11 = (bf16[4,72,384]{2,1,0:T(8,128)(2,1)S(1)}, bf16[4,72,384]{2,1,0:T(8,128)(2,1)S(1)}, u32[]{:S(2)}, u32[]{:S(2)}) collective-permute-start(bf16[4,72,384]{2,1,0:T(8,128)(2,1)S(1)} %get-tuple-element.51), channel_id=1, source_target_pairs={{0,1},{1,0},{2,3},{3,2},{4,5},{5,4},{6,7},{7,6},{8,9},{9,8},{10,11... | collective-permute-start | bytes 663560 | tf_op jit(solution)/shard_map/ppermute | solution.py:298
  57.7 0.5 collective-permute-start.8
  58.3 0.9 %collective-permute-start.9 = (bf16[72,512]{1,0:T(8,128)(2,1)S(1)}, bf16[72,512]{1,0:T(8,128)(2,1)S(1)}, u32[]{:S(2)}, u32[]{:S(2)}) collective-permute-start(bf16[72,512]{1,0:T(8,128)(2,1)S(1)} %get-tuple-element.33), channel_id=1, source_target_pairs={{0,16},{8,24},{16,0},{24,8},{1,17},{9,25},{17,1},{25,9},{2,18},{10... | collective-permute-start | bytes 221192 | tf_op jit(solution)/shard_map/ppermute | solution.py:289
  59.2 2.1 %collective-permute-start.10 = (bf16[72,512]{1,0:T(8,128)(2,1)S(1)}, bf16[72,512]{1,0:T(8,128)(2,1)S(1)}, u32[]{:S(2)}, u32[]{:S(2)}) collective-permute-start(bf16[72,512]{1,0:T(8,128)(2,1)S(1)} %get-tuple-element.34), channel_id=1, source_target_pairs={{0,24},{8,16},{16,8},{24,0},{1,25},{9,17},{17,9},{25,1},{2,26},{10... | collective-permute-start | bytes 221192 | tf_op jit(solution)/shard_map/ppermute | solution.py:289
  61.2 0.0 collective-permute-done.12.refs_5_
  61.2 0.0 collective-permute-done.11.refs_4_
  61.2 13.3 %backward.1 = (f32[72,512]{1,0:T(8,128)S(1)}, bf16[72,512]{1,0:T(8,128)(2,1)S(1)}, bf16[72,512]{1,0:T(8,128)(2,1)S(1)}, bf16[72,512]{1,0:T(8,128)(2,1)S(1)}) custom-call(s32[4]{0:T(128)S(1)} %pad_add_fusion.where_ref, bf16[72,640]{1,0:T(8,128)(2,1)S(1)} %get-tuple-element.35.refs_0_, bf16[72,640]{1,0:T(8,128)(2,1)S(1)} %get-tuple-element.36.refs_1_, ...), custom_call_target="tpu_custom_call" | custom-call | tf_op jit(solution)/shard_map/backward/pallas_call | solution.py:56
  74.6 0.6 collective-permute-start.13
  75.2 0.9 %collective-permute-start.14 = (bf16[72,512]{1,0:T(8,128)(2,1)S(1)}, bf16[72,512]{1,0:T(8,128)(2,1)S(1)}, u32[]{:S(2)}, u32[]{:S(2)}) collective-permute-start(bf16[72,512]{1,0:T(8,128)(2,1)S(1)} %get-tuple-element.42), channel_id=1, source_target_pairs={{0,16},{8,24},{16,0},{24,8},{1,17},{9,25},{17,1},{25,9},{2,18},{10... | collective-permute-start | bytes 221192 | tf_op jit(solution)/shard_map/ppermute | solution.py:289
  76.1 0.0 collective-permute-done.8.refs_1_
  76.1 2.1 %collective-permute-start.15 = (bf16[72,512]{1,0:T(8,128)(2,1)S(1)}, bf16[72,512]{1,0:T(8,128)(2,1)S(1)}, u32[]{:S(2)}, u32[]{:S(2)}) collective-permute-start(bf16[72,512]{1,0:T(8,128)(2,1)S(1)} %get-tuple-element.43), channel_id=1, source_target_pairs={{0,24},{8,16},{16,8},{24,0},{1,25},{9,17},{17,9},{25,1},{2,26},{10... | collective-permute-start | bytes 221192 | tf_op jit(solution)/shard_map/ppermute | solution.py:289
  78.1 0.0 collective-permute-done.9.refs_2_
  78.1 0.0 collective-permute-done.10.refs_3_
  78.1 0.8 join_scores.1
  78.9 1.0 %copy.23 = f32[2,69,4,256]{3,2,1,0:T(4,128)} copy(f32[2,69,4,256]{3,1,2,0:T(8,128)S(1)} %bitcast.56) | data formatting | bytes 1130496
  80.0 0.0 collective-permute-done.13.refs_1_
  80.0 0.3 collective-permute-done.14.refs_2_
  80.3 1.0 %collective-permute-done.15.refs_3_ = bf16[72,512]{1,0:T(8,128)(2,1)S(1)} collective-permute-done((bf16[72,512]{1,0:T(8,128)(2,1)S(1)}, bf16[72,512]{1,0:T(8,128)(2,1)S(1)}, u32[]{:S(2)}, u32[]{:S(2)}) %collective-permute-start.15) | collective-permute-done | bytes 73760 | tf_op jit(solution)/shard_map/ppermute | solution.py:289
  81.3 0.8 join_guidance.1
  82.1 1.0 %copy.24 = f32[2,69,4,256]{3,2,1,0:T(4,128)} copy(f32[2,69,4,256]{3,1,2,0:T(8,128)S(1)} %bitcast.54) | data formatting | bytes 1130496
  (9 shorter events, 0.2 us)
Async XLA Ops:
  0.6 16.0 %copy-start.1 = (f32[2,69,4,256]{3,2,1,0:T(4,128)S(1)}, f32[2,69,4,256]{3,2,1,0:T(4,128)}, u32[]{:S(2)}) copy-start(f32[2,69,4,256]{3,2,1,0:T(4,128)} %param.7) | copy-start | bytes 1695748
  2.8 10.1 %collective-permute-start = (bf16[72,640]{1,0:T(8,128)(2,1)S(1)}, bf16[72,640]{1,0:T(8,128)(2,1)S(1)}, u32[]{:S(2)}, u32[]{:S(2)}) collective-permute-start(bf16[72,640]{1,0:T(8,128)(2,1)S(1)} %get-tuple-element.24), channel_id=1, source_target_pairs={{0,8},{8,0},{16,24},{24,16},{1,9},{9,1},{17,25},{25,17},{2,10},{10... | collective-permute-start | bytes 276488 | tf_op jit(solution)/shard_map/ppermute | solution.py:289
  5.8 7.0 %collective-permute-start.1 = (bf16[72,640]{1,0:T(8,128)(2,1)S(1)}, bf16[72,640]{1,0:T(8,128)(2,1)S(1)}, u32[]{:S(2)}, u32[]{:S(2)}) collective-permute-start(bf16[72,640]{1,0:T(8,128)(2,1)S(1)} %get-tuple-element.25), channel_id=1, source_target_pairs={{0,16},{8,24},{16,0},{24,8},{1,17},{9,25},{17,1},{25,9},{2,18},{10... | collective-permute-start | bytes 276488 | tf_op jit(solution)/shard_map/ppermute | solution.py:289
  7.4 5.5 %collective-permute-start.2 = (bf16[72,640]{1,0:T(8,128)(2,1)S(1)}, bf16[72,640]{1,0:T(8,128)(2,1)S(1)}, u32[]{:S(2)}, u32[]{:S(2)}) collective-permute-start(bf16[72,640]{1,0:T(8,128)(2,1)S(1)} %get-tuple-element.26), channel_id=1, source_target_pairs={{0,24},{8,16},{16,8},{24,0},{1,25},{9,17},{17,9},{25,1},{2,26},{10... | collective-permute-start | bytes 276488 | tf_op jit(solution)/shard_map/ppermute | solution.py:289
  7.4 13.9 %copy-start.2 = (bf16[3,3,69,256]{3,2,1,0:T(8,128)(2,1)S(1)}, bf16[3,3,69,256]{3,2,1,0:T(8,128)(2,1)}, u32[]{:S(2)}) copy-start(bf16[3,3,69,256]{3,2,1,0:T(8,128)(2,1)} %param.10) | copy-start | bytes 953860
  13.0 24.1 %collective-permute-start.4 = (bf16[4,72,384]{2,1,0:T(8,128)(2,1)S(1)}, bf16[4,72,384]{2,1,0:T(8,128)(2,1)S(1)}, u32[]{:S(2)}, u32[]{:S(2)}) collective-permute-start(bf16[4,72,384]{2,1,0:T(8,128)(2,1)S(1)} %get-tuple-element.52), channel_id=1, source_target_pairs={{1,2},{2,1},{3,4},{4,3},{5,6},{6,5},{9,10},{10,9},{11,12},{12,11},... | collective-permute-start | bytes 663560 | tf_op jit(solution)/shard_map/ppermute | solution.py:297
  13.7 23.5 %collective-permute-start.3 = (bf16[4,72,384]{2,1,0:T(8,128)(2,1)S(1)}, bf16[4,72,384]{2,1,0:T(8,128)(2,1)S(1)}, u32[]{:S(2)}, u32[]{:S(2)}) collective-permute-start(bf16[4,72,384]{2,1,0:T(8,128)(2,1)S(1)} %get-tuple-element.53), channel_id=1, source_target_pairs={{0,1},{1,0},{2,3},{3,2},{4,5},{5,4},{6,7},{7,6},{8,9},{9,8},{10,11... | collective-permute-start | bytes 663560 | tf_op jit(solution)/shard_map/ppermute | solution.py:298
  17.8 19.3 %collective-permute-start.5 = (f32[72,640]{1,0:T(8,128)S(1)}, f32[72,640]{1,0:T(8,128)S(1)}, u32[]{:S(2)}, u32[]{:S(2)}) collective-permute-start(f32[72,640]{1,0:T(8,128)S(1)} %get-tuple-element.28), channel_id=1, source_target_pairs={{0,8},{8,0},{16,24},{24,16},{1,9},{9,1},{17,25},{25,17},{2,10},{10... | collective-permute-start | bytes 552968 | tf_op jit(solution)/shard_map/ppermute | solution.py:289
  18.4 18.7 %collective-permute-start.6 = (f32[72,640]{1,0:T(8,128)S(1)}, f32[72,640]{1,0:T(8,128)S(1)}, u32[]{:S(2)}, u32[]{:S(2)}) collective-permute-start(f32[72,640]{1,0:T(8,128)S(1)} %get-tuple-element.29), channel_id=1, source_target_pairs={{0,16},{8,24},{16,0},{24,8},{1,17},{9,25},{17,1},{25,9},{2,18},{10... | collective-permute-start | bytes 552968 | tf_op jit(solution)/shard_map/ppermute | solution.py:289
  19.3 17.8 %collective-permute-start.7 = (f32[72,640]{1,0:T(8,128)S(1)}, f32[72,640]{1,0:T(8,128)S(1)}, u32[]{:S(2)}, u32[]{:S(2)}) collective-permute-start(f32[72,640]{1,0:T(8,128)S(1)} %get-tuple-element.30), channel_id=1, source_target_pairs={{0,24},{8,16},{16,8},{24,0},{1,25},{9,17},{17,9},{25,1},{2,26},{10... | collective-permute-start | bytes 552968 | tf_op jit(solution)/shard_map/ppermute | solution.py:289
  35.1 1.9 %copy-start.3 = (f32[69]{0:T(128)S(1)}, f32[69]{0:T(128)}, u32[]{:S(2)}) copy-start(f32[69]{0:T(128)} %param.11) | copy-start | bytes 832
  35.1 2.0 %copy-start = (f32[256]{0:T(256)S(1)}, f32[256]{0:T(256)}, u32[]{:S(2)}) copy-start(f32[256]{0:T(256)} %param.9) | copy-start | bytes 3076
  54.1 7.2 %collective-permute-start.12 = (bf16[4,72,384]{2,1,0:T(8,128)(2,1)S(1)}, bf16[4,72,384]{2,1,0:T(8,128)(2,1)S(1)}, u32[]{:S(2)}, u32[]{:S(2)}) collective-permute-start(bf16[4,72,384]{2,1,0:T(8,128)(2,1)S(1)} %get-tuple-element.50), channel_id=1, source_target_pairs={{1,2},{2,1},{3,4},{4,3},{5,6},{6,5},{9,10},{10,9},{11,12},{12,11},... | collective-permute-start | bytes 663560 | tf_op jit(solution)/shard_map/ppermute | solution.py:297
  54.8 6.5 %collective-permute-start.11 = (bf16[4,72,384]{2,1,0:T(8,128)(2,1)S(1)}, bf16[4,72,384]{2,1,0:T(8,128)(2,1)S(1)}, u32[]{:S(2)}, u32[]{:S(2)}) collective-permute-start(bf16[4,72,384]{2,1,0:T(8,128)(2,1)S(1)} %get-tuple-element.51), channel_id=1, source_target_pairs={{0,1},{1,0},{2,3},{3,2},{4,5},{5,4},{6,7},{7,6},{8,9},{9,8},{10,11... | collective-permute-start | bytes 663560 | tf_op jit(solution)/shard_map/ppermute | solution.py:298
  57.7 18.3 %collective-permute-start.8 = (bf16[72,512]{1,0:T(8,128)(2,1)S(1)}, bf16[72,512]{1,0:T(8,128)(2,1)S(1)}, u32[]{:S(2)}, u32[]{:S(2)}) collective-permute-start(bf16[72,512]{1,0:T(8,128)(2,1)S(1)} %get-tuple-element.32), channel_id=1, source_target_pairs={{0,8},{8,0},{16,24},{24,16},{1,9},{9,1},{17,25},{25,17},{2,10},{10... | collective-permute-start | bytes 221192 | tf_op jit(solution)/shard_map/ppermute | solution.py:289
  58.3 19.8 %collective-permute-start.9 = (bf16[72,512]{1,0:T(8,128)(2,1)S(1)}, bf16[72,512]{1,0:T(8,128)(2,1)S(1)}, u32[]{:S(2)}, u32[]{:S(2)}) collective-permute-start(bf16[72,512]{1,0:T(8,128)(2,1)S(1)} %get-tuple-element.33), channel_id=1, source_target_pairs={{0,16},{8,24},{16,0},{24,8},{1,17},{9,25},{17,1},{25,9},{2,18},{10... | collective-permute-start | bytes 221192 | tf_op jit(solution)/shard_map/ppermute | solution.py:289
  59.2 19.0 %collective-permute-start.10 = (bf16[72,512]{1,0:T(8,128)(2,1)S(1)}, bf16[72,512]{1,0:T(8,128)(2,1)S(1)}, u32[]{:S(2)}, u32[]{:S(2)}) collective-permute-start(bf16[72,512]{1,0:T(8,128)(2,1)S(1)} %get-tuple-element.34), channel_id=1, source_target_pairs={{0,24},{8,16},{16,8},{24,0},{1,25},{9,17},{17,9},{25,1},{2,26},{10... | collective-permute-start | bytes 221192 | tf_op jit(solution)/shard_map/ppermute | solution.py:289
  74.6 5.4 %collective-permute-start.13 = (bf16[72,512]{1,0:T(8,128)(2,1)S(1)}, bf16[72,512]{1,0:T(8,128)(2,1)S(1)}, u32[]{:S(2)}, u32[]{:S(2)}) collective-permute-start(bf16[72,512]{1,0:T(8,128)(2,1)S(1)} %get-tuple-element.41), channel_id=1, source_target_pairs={{0,8},{8,0},{16,24},{24,16},{1,9},{9,1},{17,25},{25,17},{2,10},{10... | collective-permute-start | bytes 221192 | tf_op jit(solution)/shard_map/ppermute | solution.py:289
  75.2 5.1 %collective-permute-start.14 = (bf16[72,512]{1,0:T(8,128)(2,1)S(1)}, bf16[72,512]{1,0:T(8,128)(2,1)S(1)}, u32[]{:S(2)}, u32[]{:S(2)}) collective-permute-start(bf16[72,512]{1,0:T(8,128)(2,1)S(1)} %get-tuple-element.42), channel_id=1, source_target_pairs={{0,16},{8,24},{16,0},{24,8},{1,17},{9,25},{17,1},{25,9},{2,18},{10... | collective-permute-start | bytes 221192 | tf_op jit(solution)/shard_map/ppermute | solution.py:289
  76.1 5.3 %collective-permute-start.15 = (bf16[72,512]{1,0:T(8,128)(2,1)S(1)}, bf16[72,512]{1,0:T(8,128)(2,1)S(1)}, u32[]{:S(2)}, u32[]{:S(2)}) collective-permute-start(bf16[72,512]{1,0:T(8,128)(2,1)S(1)} %get-tuple-element.43), channel_id=1, source_target_pairs={{0,24},{8,16},{16,8},{24,0},{1,25},{9,17},{17,9},{25,1},{2,26},{10... | collective-permute-start | bytes 221192 | tf_op jit(solution)/shard_map/ppermute | solution.py:289

commit v2 on v1

v2 whole, which is shorter than its diff:
```python
import functools

import jax
import jax.numpy as jnp
from jax import lax
from jax.experimental import pallas as pl
from jax.experimental.pallas import tpu as pltpu
from jax.sharding import PartitionSpec as P


F32 = jnp.float32
BF16 = jnp.bfloat16
LANES = 128
DEPTH = 4
REACH = 2
VMEM = pl.BlockSpec(memory_space=pltpu.VMEM)
SMEM = pl.BlockSpec(memory_space=pltpu.SMEM)


def up(value, step):
    return -(-value // step) * step


class Plan:
    def __init__(self, states, conv_in):
        self.n = lax.axis_size("tm")
        self.m = lax.axis_size("lat")
        self.local, self.chans, self.rows, self.lon = states.shape
        self.taps = conv_in.shape[0]
        self.hidden = conv_in.shape[2]
        self.window = conv_in.shape[3] // self.chans
        self.side = self.window // 2
        self.total = self.local * self.n
        self.wc = self.lon // self.n
        self.wx = self.wc + 2 * DEPTH
        self.wp = up(self.wx, 16)
        self.cp = up(self.chans, 8)
        self.packed = 2 * LANES
        self.pos = self.rows * self.local * self.wx
        self.posp = up(self.pos, LANES)
        self.half = REACH * self.local * self.wx
        self.cut = (self.pos - self.half) // LANES * LANES
        self.msg = max(self.posp - self.cut, up(self.half, LANES))
        self.cut = self.posp - self.msg
        self.shift = self.pos - self.half - self.cut
        self.out = self.rows * self.local * self.wc
        assert self.taps == 3 and LANES <= 2 * self.chans and 3 * self.chans <= self.packed
        assert self.out % LANES == 0 and LANES % self.wc == 0 and self.wx % 8 == 0
        assert self.lon % LANES == 0 and self.rows >= 2 * REACH and self.n & (self.n - 1) == 0

    def at(self, row, t):
        return (row * self.local + t) * self.wx


def call(kernel, outs, scratch, args, limit, microseconds, aliases={}):
    return pl.pallas_call(
        kernel,
        out_shape=outs,
        in_specs=[SMEM if a.dtype == jnp.int32 else VMEM for a in args],
        out_specs=[VMEM] * len(outs),
        scratch_shapes=scratch,
        input_output_aliases=aliases,
        compiler_params=pltpu.CompilerParams(vmem_limit_bytes=limit),
        cost_estimate=pl.CostEstimate(flops=int(microseconds * 1e9), bytes_accessed=0, transcendentals=0),
    )(*args)


def lanes_of(shape):
    return lax.broadcasted_iota(jnp.int32, shape, len(shape) - 1)


def split_kernel(p, where_ref, x_ref, *refs):
    outs, held = refs[: p.n], refs[p.n]
    me = where_ref[0]
    held[...] = jnp.zeros_like(held)
    for r in range(p.rows):
        for t in range(p.local):
            v = x_ref[t, :, r, :]
            start = p.at(r, t)
            base, off = start // LANES * LANES, start % LANES
            width = LANES if off + p.wx <= LANES else 2 * LANES
            lane = lanes_of((p.chans, width))
            inside = (lane >= off) & (lane < off + p.wx)
            for q in range(p.n):
                y = pltpu.roll(v, (off + DEPTH - p.wc * q) % p.lon, 1)[:, :width]
                old = held[q, : p.chans, base : base + width]
                held[q, : p.chans, base : base + width] = jnp.where(inside, y, old)
    for d in range(p.n):
        outs[d][...] = held[me ^ d].astype(outs[d].dtype)


def weights_kernel(p, k_in, k_out, w_in, w_out, flat_ref, held):
    held[...] = jnp.zeros_like(held)
    c = p.chans
    for i in range(p.taps):
        for j in range(p.taps):
            flat_ref[j, : p.window * c] = k_in[i, j].astype(F32)
        for k in range(p.window):
            for j in range(p.taps):
                held[k, j * c : (j + 1) * c, :] = flat_ref[j, k * c : (k + 1) * c, :]
            w_in[i * p.window + k] = held[k].astype(BF16)
        for j in range(p.taps):
            held[p.window, j * c : (j + 1) * c, :] = k_out[i, j].astype(F32)
        w_out[i] = held[p.window].astype(BF16)


def to_columns(block, rows_ref):
    depth, width = block.shape
    for m in range(width // LANES):
        tile = block[:, m * LANES : (m + 1) * LANES].astype(F32)
        tile = jnp.concatenate([tile, jnp.zeros((LANES - depth, LANES), F32)], axis=0)
        rows_ref[8 + m * LANES : 8 + (m + 1) * LANES, :] = tile.T


def taps_of(p, rows_ref, start, flip):
    v = [rows_ref[8 + start + j : 8 + start + j + p.wp, :] for j in (-1, 0, 1)]
    if flip:
        v = v[::-1]
    lane = lanes_of((p.wp, LANES))
    middle = pltpu.roll(v[1], p.chans, 1)
    low = jnp.where(lane < p.chans, v[0], middle)
    high = jnp.where(lane < 2 * p.chans - LANES, middle, pltpu.roll(v[2], 2 * p.chans - LANES, 1))
    return jnp.concatenate([low, high], axis=1).astype(BF16)


def untap(p, ref, lead, start, count, flip):
    before, after = (1, -1) if flip else (-1, 1)
    s = start
    first = ref[lead, s + before : s + before + count, :LANES]
    low = pltpu.roll(ref[lead, s : s + count, :LANES], LANES - p.chans, 1)
    high = pltpu.roll(ref[lead, s : s + count, LANES:], LANES - p.chans, 1)
    lane = lanes_of((count, LANES))
    middle = jnp.where(lane < LANES - p.chans, low, high)
    last = pltpu.roll(ref[lead, s + after : s + after + count, LANES:], 2 * LANES - 2 * p.chans, 1)
    return jnp.where(lane < p.chans, first + middle + last, 0.0)


def fill_own(p, where_ref, blocks, rows_ref, taps_ref, flip, base):
    me = where_ref[0]
    for d in range(p.n):
        t0 = (me ^ d) * p.local + base
        to_columns(blocks[d][...], rows_ref)
        for r in range(p.rows):
            for t in range(p.local):
                taps_ref[REACH + r, t0 + t] = taps_of(p, rows_ref, p.at(r, t), flip)


def fill_halo(p, where_ref, near, far, rows_ref, taps_ref, flip, base):
    me, even = where_ref[0], where_ref[1] == 1
    for d in range(p.n):
        t0 = (me ^ d) * p.local + base
        to_columns(jnp.where(even, far[d], near[d]), rows_ref)
        for r in range(REACH):
            for t in range(p.local):
                taps_ref[r, t0 + t] = taps_of(p, rows_ref, p.shift + p.at(r, t), flip)
        to_columns(jnp.where(even, near[d], far[d]), rows_ref)
        for r in range(REACH):
            for t in range(p.local):
                taps_ref[REACH + p.rows + r, t0 + t] = taps_of(p, rows_ref, p.at(r, t), flip)


def wrap(p, ref, begin, count):
    for row in range(begin, begin + count):
        for e in range(p.side):
            ref[row, e] = ref[row, p.total + e]
            ref[row, p.total + p.side + e] = ref[row, p.side + e]


def row_mask(p, where_ref, row):
    outside = ((row == 0) & (where_ref[2] == 1)) | ((row == p.rows + 1) & (where_ref[3] == 1))
    return jnp.where(outside, 0.0, 1.0)


def dot(a, b, transposed):
    dims = (((1,), (1 if transposed else 0,)), ((), ()))
    return lax.dot_general(a, b, dims, preferred_element_type=F32)


def hidden_rows(p, where_ref, taps_ref, w_in, bias_in, act_ref, slope_ref, count, row_of):
    def body(step, carry):
        row = row_of(step)
        total = None
        for i in range(p.taps):
            for k in range(p.window):
                a = taps_ref[row + i, k : k + p.total].reshape(p.total * p.wp, p.packed)
                term = dot(a, w_in[i * p.window + k], False)
                total = term if total is None else total + term
        pre = total + bias_in[...]
        sig = 0.5 * jnp.tanh(0.5 * pre) + 0.5
        act = pre * sig
        slope = sig + act * (1.0 - sig)
        mask = row_mask(p, where_ref, row)
        act_ref[row] = (act * mask).astype(BF16).reshape(p.total, p.wp, p.hidden)
        slope_ref[row] = (slope * mask).reshape(p.total, p.wp, p.hidden)
        return carry

    lax.fori_loop(0, count, body, 0)


def inner_kernel(p, where_ref, *refs):
    blocks, w_in, bias_in = refs[: p.n], refs[p.n], refs[p.n + 1]
    taps_ref, act_ref, slope_ref, rows_ref = refs[p.n + 2 :]
    fill_own(p, where_ref, blocks, rows_ref, taps_ref, False, p.side)
    wrap(p, taps_ref, REACH, p.rows)
    hidden_rows(p, where_ref, taps_ref, w_in, bias_in, act_ref, slope_ref, p.rows - 2, lambda s: s + REACH)


def score_kernel(p, where_ref, *refs):
    n = p.n
    near, far, targets = refs[0], refs[1], refs[2 : n + 2]
    w_in, bias_in, w_out, bias_out = refs[n + 2 : n + 6]
    refs = refs[n + 9 :]
    taps_ref, act_ref, slope_ref, wide_ref = refs[:4]
    resids = refs[4 : n + 4]
    rows_ref, part_ref = refs[n + 4 :]
    me = where_ref[0]
    fill_halo(p, where_ref, near, far, rows_ref, taps_ref, False, p.side)
    wrap(p, taps_ref, 0, REACH)
    wrap(p, taps_ref, REACH + p.rows, REACH)
    edge = lambda s: jnp.where(s < REACH, s, s + p.rows - 2)
    hidden_rows(p, where_ref, taps_ref, w_in, bias_in, act_ref, slope_ref, 2 * REACH, edge)
    wide_ref[...] = jnp.zeros_like(wide_ref)

    def score_row(row, carry):
        total = None
        for i in range(p.taps):
            term = dot(act_ref[row + i].reshape(p.total * p.wp, p.hidden), w_out[i], True)
            total = term if total is None else total + term
        part_ref[:, 8 : 8 + p.wp, :] = total.reshape(p.total, p.wp, p.packed)
        for d in range(n):
            for t in range(p.local):
                s = untap(p, part_ref, (me ^ d) * p.local + t, 8, p.wx, False) + bias_out[...]
                wide_ref[d, pl.ds(pl.multiple_of((row * p.local + t) * p.wx, 8), p.wx), :] = s
        return carry

    lax.fori_loop(0, p.rows, score_row, 0)
    for d in range(n):
        for m in range(p.posp // LANES):
            cols = slice(m * LANES, (m + 1) * LANES)
            tile = wide_ref[d, cols, :].T[: p.cp]
            resids[d][:, cols] = (tile - targets[d][:, cols]).astype(BF16)


def gradient_rows(p, taps_ref, w_out, slope_ref, grad_ref, count, row_of):
    def body(step, carry):
        row = row_of(step)
        total = None
        for i in range(p.taps):
            a = taps_ref[row + 2 - i].reshape(p.total * p.wp, p.packed)
            term = dot(a, w_out[i], False)
            total = term if total is None else total + term
        grad = total.reshape(p.total, p.wp, p.hidden) * slope_ref[row]
        grad_ref[row, p.side : p.side + p.total] = grad.astype(BF16)
        return carry

    lax.fori_loop(0, count, body, 0)


def back_inner_kernel(p, where_ref, *refs):
    n = p.n
    blocks, slope_ref, w_out, wide_ref = refs[:n], refs[n], refs[n + 1], refs[n + 2]
    taps_ref, grad_ref = refs[n + 3 : n + 5]
    own_ref, scores = refs[n + 5], refs[n + 6 : 2 * n + 5]
    rows_ref, thin_ref = refs[2 * n + 5 :]
    fill_own(p, where_ref, blocks, rows_ref, taps_ref, True, 0)
    gradient_rows(p, taps_ref, w_out, slope_ref, grad_ref, p.rows - 2, lambda s: s + REACH)
    wrap(p, grad_ref, REACH, p.rows - 2)
    for d in range(n):
        for r in range(p.rows):
            for t in range(p.local):
                start = p.at(r, t) + DEPTH
                at = (r * p.local + t) * p.wc
                thin_ref[at : at + p.wc, :] = wide_ref[d, start : start + p.wc, :]
        turn(p, thin_ref, own_ref if d == 0 else scores[d - 1], 0)


def turn(p, thin_ref, out_ref, begin):
    for m in range(p.out // LANES):
        tile = thin_ref[m * LANES : (m + 1) * LANES, :].T[: p.cp]
        out_ref[:, begin + m * LANES : begin + (m + 1) * LANES] = tile.astype(out_ref.dtype)


def back_outer_kernel(p, where_ref, near, far, slope_ref, w_out, _taps, _grad, taps_ref, grad_ref, rows_ref):
    fill_halo(p, where_ref, near, far, rows_ref, taps_ref, True, 0)
    edge = lambda s: jnp.where(s < REACH, s, s + p.rows - 2)
    gradient_rows(p, taps_ref, w_out, slope_ref, grad_ref, 2 * REACH, edge)
    wrap(p, grad_ref, 0, REACH)
    wrap(p, grad_ref, p.rows, REACH)


def guide_kernel(p, d, where_ref, grad_ref, w_in, scores_ref, out_ref, part_ref, thin_ref):
    t0 = (where_ref[0] ^ d) * p.local
    total = None
    for i in range(p.taps):
        for k in range(p.window):
            a = grad_ref[2 - i : 2 - i + p.rows, pl.ds(t0 + 2 * p.side - k, p.local)]
            a = a.reshape(p.rows * p.local * p.wp, p.hidden)
            term = dot(a, w_in[i * p.window + k], True)
            total = term if total is None else total + term
    part_ref[:, 8 : 8 + p.wp, :] = total.reshape(p.rows * p.local, p.wp, p.packed)
    for r in range(p.rows * p.local):
        thin_ref[r * p.wc : (r + 1) * p.wc, :] = untap(p, part_ref, r, 8 + DEPTH, p.wc, True)
    out_ref[:, : p.out] = scores_ref[...]
    turn(p, thin_ref, out_ref, p.out)


def join_kernel(p, where_ref, *refs):
    ins, outs, held = refs[: p.n], refs[p.n : p.n + 2], refs[p.n + 2]
    me = where_ref[0]
    for d in range(p.n):
        held[me ^ d] = ins[d][...].astype(F32)
    per = LANES // p.wc
    lane = lanes_of((p.chans, LANES))
    for which in range(2):
        for r in range(p.rows):
            for t in range(p.local):
                start = which * p.out + (r * p.local + t) * p.wc
                base, off = start // LANES * LANES, start % LANES
                for m in range(p.lon // LANES):
                    tile = None
                    for u in range(per):
                        piece = held[m * per + u, : p.chans, base : base + LANES]
                        step = (u * p.wc - off) % LANES
                        if step:
                            piece = pltpu.roll(piece, step, 1)
                        tile = piece if tile is None else jnp.where(lane < u * p.wc, tile, piece)
                    outs[which][t, :, r, m * LANES : (m + 1) * LANES] = tile


def send_tm(p, value, d):
    return lax.ppermute(value, "tm", [(i, i ^ d) for i in range(p.n)])


def send_lat(p, even, blocks):
    low = jnp.stack([b[:, : p.msg] for b in blocks])
    high = jnp.stack([b[:, p.cut :] for b in blocks])
    inner = [(i, i ^ 1) for i in range(p.m)]
    outer = [(i, ((i + 1) ^ 1) - 1) for i in range(1, p.m - 1)]
    far = lax.ppermute(jnp.where(even, low, high), "lat", outer)
    near = lax.ppermute(jnp.where(even, high, low), "lat", inner)
    return near, far


def shards(states, observed, conv_in, bias_in, conv_out, bias_out):
    p = Plan(states, conv_in)
    n = p.n
    me, row = lax.axis_index("tm"), lax.axis_index("lat")
    even = row % 2 == 0
    where = jnp.stack([me, even.astype(jnp.int32), (row == 0).astype(jnp.int32), (row == p.m - 1).astype(jnp.int32)])
    where = where.astype(jnp.int32)
    sds = jax.ShapeDtypeStruct
    kernel = functools.partial
    scratch = pltpu.VMEM

    def split(field, dtype):
        shape = [sds((p.cp, p.posp), dtype)] * n
        held = [scratch((n, p.cp, p.posp), F32)]
        return call(kernel(split_kernel, p), shape, held, [where, field], 8 << 20, 1.5)

    mine = split(states, BF16)
    blocks = [mine[0]] + [send_tm(p, mine[d], d) for d in range(1, n)]
    w_in, w_out = call(
        kernel(weights_kernel, p),
        [sds((p.taps * p.window, p.packed, p.hidden), BF16), sds((p.taps, p.packed, p.hidden), BF16)],
        [scratch((p.taps, up(p.window * p.chans, 8), p.hidden), F32), scratch((p.window + 1, p.packed, p.hidden), F32)],
        [jnp.swapaxes(conv_in, 2, 3), conv_out],
        16 << 20, 2,
    )
    goal = split(observed, F32)
    goals = [goal[0]] + [send_tm(p, goal[d], d) for d in range(1, n)]
    b_in = bias_in.reshape(1, p.hidden)
    b_out = jnp.pad(bias_out, (0, LANES - p.chans)).reshape(1, LANES)
    near, far = send_lat(p, even, blocks)

    columns = scratch((p.posp + 32, LANES), F32)
    deep = p.rows + 2 * REACH
    around = p.total + 2 * p.side
    taps_shape = sds((deep, around, p.wp, p.packed), BF16)
    act_shape = sds((p.rows + 2, p.total, p.wp, p.hidden), BF16)
    slope_shape = sds((p.rows + 2, p.total, p.wp, p.hidden), F32)
    inner = call(
        kernel(inner_kernel, p), [taps_shape, act_shape, slope_shape], [columns],
        [where, *blocks, w_in, b_in], 24 << 20, 6,
    )
    part = scratch((p.total, p.wp + 16, p.packed), F32)
    out = call(
        kernel(score_kernel, p),
        [taps_shape, act_shape, slope_shape, sds((n, p.posp, LANES), F32)] + [sds((p.cp, p.posp), BF16)] * n,
        [columns, part],
        [where, near, far, *goals, w_in, b_in, w_out, b_out, *inner],
        32 << 20, 12, {n + 7: 0, n + 8: 1, n + 9: 2},
    )
    slope, wide, resids = out[2], out[3], out[4:]
    near, far = send_lat(p, even, resids)
    taps_shape = sds((deep, p.total, p.wp, p.packed), BF16)
    grad_shape = sds((p.rows + 2, around, p.wp, p.hidden), BF16)
    thin_rows = scratch((p.out, LANES), F32)
    out = call(
        kernel(back_inner_kernel, p),
        [taps_shape, grad_shape, sds((p.cp, p.out), F32)] + [sds((p.cp, p.out), BF16)] * (n - 1),
        [columns, thin_rows],
        [where, *resids, slope, w_out, wide], 24 << 20, 4,
    )
    taps, grad, scores = out[0], out[1], out[2:]
    taps, grad = call(
        kernel(back_outer_kernel, p), [taps_shape, grad_shape], [columns],
        [where, near, far, slope, w_out, taps, grad], 24 << 20, 3, {5: 0, 6: 1},
    )
    parts = [None] * n
    for d in [*range(n - 1, 0, -1), 0]:
        part = scratch((p.rows * p.local, p.wp + 16, p.packed), F32)
        parts[d] = call(
            kernel(guide_kernel, p, d), [sds((p.cp, 2 * p.out), scores[d].dtype)], [part, thin_rows],
            [where, grad, w_in, scores[d]], 16 << 20, 2,
        )[0]
        if d:
            parts[d] = send_tm(p, parts[d], d)
    shape = [sds((p.local, p.chans, p.rows, p.lon), F32)] * 2
    held = [scratch((n, p.cp, 2 * p.out), F32)]
    return tuple(call(kernel(join_kernel, p), shape, held, [where, *parts], 16 << 20, 1.5))


def solution(mesh):
    in_specs = (P("tm", None, "lat", None), P("tm", None, "lat", None), P(), P(), P(), P())
    out_specs = (P("tm", None, "lat", None), P("tm", None, "lat", None))
    return jax.shard_map(shards, mesh=mesh, in_specs=in_specs, out_specs=out_specs, check_vma=False)
```

time: 83.6 us -> 63.4 us (0.76)
  local copies, waits for them, and re-layouts: 18 us -> 1.25 us
  starting transfers between devices: 22.5 us -> 19.2 us
  other arithmetic: 1.48 us -> 0.26 us
  Pallas kernels: 33.5 us -> 34.5 us
    reshape x5 -> x0, local copies, waits for them, and re-layouts: 13.8 us -> none  [the longest x2 7.34 us: shards(): jnp.transpose(w_in, (0, 3, 2, 1, 4))]
    ppermute x12 -> x9, starting transfers between devices: 15.2 us -> 11.7 us  [send_tm(): return lax.ppermute(value, 'tm', [(i, i ^ d) for i in range(p.n)])]
    pad x2 -> x0, local copies, waits for them, and re-layouts: 1.94 us -> none  [the longest x1 1.91 us: shards(): w_in = jnp.pad(w_in, ((0, 0), (0, 0), (0, p.packed - p.taps * p.chans)))]
    convert_element_type x1 -> x0, other arithmetic: 1.21 us -> none  [split(): turned = jnp.transpose(field.astype(dtype), (0, 2, 1, 3))]
    pallas_call x6 -> x12, Pallas kernels: 33.5 us -> 34.5 us  [call(): pl.pallas_call(kernel, out_shape=outs, in_specs=[SMEM if a.dtype == jnp.i...]
    unnamed x11 -> x12, local copies, waits for them, and re-layouts: 2.19 us -> 1.14 us
    ppermute x12 -> x9, waiting for transfers between devices: 6.77 us -> 7.07 us  [send_tm(): return lax.ppermute(value, 'tm', [(i, i ^ d) for i in range(p.n)])]
  transfers between devices with their start and end apart: 16 -> 13, of which waited for: 3 -> 3; matrix products, arithmetic and copies ran while one was open for 20% -> 0% of each run, Pallas kernels for 18% -> 17%
where the time goes in v2:
time: 63.4 us; the launch traced here: 63.2 us
  Pallas kernels  34.5 us (54%)
  starting transfers between devices  19.2 us (30%)
  waiting for transfers between devices  7.08 us (11%)
  local copies, waits for them, and re-layouts  1.25 us (2%)
  between operations  0.89 us (1%)
    pallas_call x12, Pallas kernels, call(): pl.pallas_call(kernel, out_shape=outs, in_specs=[SMEM if a.dtype == jnp.i...  34.5 us
    ppermute x9, starting transfers between devices, send_tm(): return lax.ppermute(value, 'tm', [(i, i ^ d) for i in range(p.n)])  11.7 us
    ppermute x9, waiting for transfers between devices, send_tm(): return lax.ppermute(value, 'tm', [(i, i ^ d) for i in range(p.n)])  7.07 us
    ppermute x2, starting transfers between devices, send_lat(): near = lax.ppermute(jnp.where(even, high, low), 'lat', inner)  5.98 us
    ppermute x2, starting transfers between devices, send_lat(): far = lax.ppermute(jnp.where(even, low, high), 'lat', outer)  1.53 us
  transfers between devices with their start and end apart: 13, of which 3 were waited for; matrix products, arithmetic and copies ran while one was open for 0% of the time, Pallas kernels for 17%

profile of v2, /device:TPU:0, one launch (start us, length us, event | category | flops | bytes accessed | tf_op | source)
XLA Modules:
  0.0 63.2 jit_solution(507251858764267969)
XLA Ops:
  0.6 0.1 pad_add_fusion.where_ref
  0.7 0.0 copy-start.1
  0.7 1.1 %copy-done.1 = f32[2,69,4,256]{3,2,1,0:T(4,128)S(1)} copy-done((f32[2,69,4,256]{3,2,1,0:T(4,128)S(1)}, f32[2,69,4,256]{3,2,1,0:T(4,128)}, u32[]{:S(2)}) %copy-start.1) | copy-done | bytes 565272
  1.8 0.0 copy-start.2
  1.8 1.0 %shard_map.77 = (bf16[72,640]{1,0:T(8,128)(2,1)S(1)}, bf16[72,640]{1,0:T(8,128)(2,1)S(1)}, bf16[72,640]{1,0:T(8,128)(2,1)S(1)}, bf16[72,640]{1,0:T(8,128)(2,1)S(1)}) custom-call(s32[4]{0:T(128)S(1)} %pad_add_fusion.where_ref, f32[2,69,4,256]{3,2,1,0:T(4,128)S(1)} %copy-done.1), custom_call_target="tpu_custom_call" | custom-call | flops 1500000000 | tf_op jit(solution)/shard_map/pallas_call | solution.py:56
  2.8 3.0 %collective-permute-start = (bf16[72,640]{1,0:T(8,128)(2,1)S(1)}, bf16[72,640]{1,0:T(8,128)(2,1)S(1)}, u32[]{:S(2)}, u32[]{:S(2)}) collective-permute-start(bf16[72,640]{1,0:T(8,128)(2,1)S(1)} %get-tuple-element.29), channel_id=1, source_target_pairs={{0,8},{8,0},{16,24},{24,16},{1,9},{9,1},{17,25},{25,17},{2,10},{10... | collective-permute-start | bytes 276488 | tf_op jit(solution)/shard_map/ppermute | solution.py:331
  5.8 1.5 %collective-permute-start.1 = (bf16[72,640]{1,0:T(8,128)(2,1)S(1)}, bf16[72,640]{1,0:T(8,128)(2,1)S(1)}, u32[]{:S(2)}, u32[]{:S(2)}) collective-permute-start(bf16[72,640]{1,0:T(8,128)(2,1)S(1)} %get-tuple-element.30), channel_id=1, source_target_pairs={{0,16},{8,24},{16,0},{24,8},{1,17},{9,25},{17,1},{25,9},{2,18},{10... | collective-permute-start | bytes 276488 | tf_op jit(solution)/shard_map/ppermute | solution.py:331
  7.3 0.0 copy-start
  7.3 0.0 copy-start.3
  7.3 0.0 collective-permute-start.2
  7.3 0.0 copy-done.2
  7.3 1.0 %shard_map.78 = (f32[72,640]{1,0:T(8,128)S(1)}, f32[72,640]{1,0:T(8,128)S(1)}, f32[72,640]{1,0:T(8,128)S(1)}, f32[72,640]{1,0:T(8,128)S(1)}) custom-call(s32[4]{0:T(128)S(1)} %pad_add_fusion.where_ref, f32[2,69,4,256]{3,2,1,0:T(4,128)S(1)} %copy-done.2), custom_call_target="tpu_custom_call" | custom-call | flops 1500000000 | tf_op jit(solution)/shard_map/pallas_call | solution.py:56
  8.3 2.0 %collective-permute-start.5 = (f32[72,640]{1,0:T(8,128)S(1)}, f32[72,640]{1,0:T(8,128)S(1)}, u32[]{:S(2)}, u32[]{:S(2)}) collective-permute-start(f32[72,640]{1,0:T(8,128)S(1)} %get-tuple-element.33), channel_id=1, source_target_pairs={{0,8},{8,0},{16,24},{24,16},{1,9},{9,1},{17,25},{25,17},{2,10},{10... | collective-permute-start | bytes 552968 | tf_op jit(solution)/shard_map/ppermute | solution.py:331
  10.4 1.5 %collective-permute-start.6 = (f32[72,640]{1,0:T(8,128)S(1)}, f32[72,640]{1,0:T(8,128)S(1)}, u32[]{:S(2)}, u32[]{:S(2)}) collective-permute-start(f32[72,640]{1,0:T(8,128)S(1)} %get-tuple-element.34), channel_id=1, source_target_pairs={{0,16},{8,24},{16,0},{24,8},{1,17},{9,25},{17,1},{25,9},{2,18},{10... | collective-permute-start | bytes 552968 | tf_op jit(solution)/shard_map/ppermute | solution.py:331
  11.9 0.0 copy-done
  11.9 0.0 copy-done.3
  11.9 0.0 copy-start.5
  11.9 0.0 copy-start.4
  11.9 0.6 shard_map.79
  12.5 0.1 copy-done.5
  12.6 1.2 %collective-permute-done.2.refs_3_ = bf16[72,640]{1,0:T(8,128)(2,1)S(1)} collective-permute-done((bf16[72,640]{1,0:T(8,128)(2,1)S(1)}, bf16[72,640]{1,0:T(8,128)(2,1)S(1)}, u32[]{:S(2)}, u32[]{:S(2)}) %collective-permute-start.2) | collective-permute-done | bytes 92192 | tf_op jit(solution)/shard_map/ppermute | solution.py:331
  13.8 0.0 collective-permute-start.7
  13.8 0.0 collective-permute-done.1.refs_2_
  13.8 0.0 collective-permute-done.refs_1_
  13.8 0.1 broadcast_select_fusion.2
  13.9 0.7 %collective-permute-start.4 = (bf16[4,72,384]{2,1,0:T(8,128)(2,1)S(1)}, bf16[4,72,384]{2,1,0:T(8,128)(2,1)S(1)}, u32[]{:S(2)}, u32[]{:S(2)}) collective-permute-start(bf16[4,72,384]{2,1,0:T(8,128)(2,1)S(1)} %get-tuple-element.56), channel_id=1, source_target_pairs={{1,2},{2,1},{3,4},{4,3},{5,6},{6,5},{9,10},{10,9},{11,12},{12,11},... | collective-permute-start | bytes 663560 | tf_op jit(solution)/shard_map/ppermute | solution.py:339
  14.6 3.0 %collective-permute-start.3 = (bf16[4,72,384]{2,1,0:T(8,128)(2,1)S(1)}, bf16[4,72,384]{2,1,0:T(8,128)(2,1)S(1)}, u32[]{:S(2)}, u32[]{:S(2)}) collective-permute-start(bf16[4,72,384]{2,1,0:T(8,128)(2,1)S(1)} %get-tuple-element.57), channel_id=1, source_target_pairs={{0,1},{1,0},{2,3},{3,2},{4,5},{5,4},{6,7},{7,6},{8,9},{9,8},{10,11... | collective-permute-start | bytes 663560 | tf_op jit(solution)/shard_map/ppermute | solution.py:340
  17.6 0.0 copy-done.4
  17.6 4.4 %shard_map.80 = (bf16[8,12,80,256]{3,2,1,0:T(8,128)(2,1)S(1)}, bf16[6,8,80,256]{3,2,1,0:T(8,128)(2,1)S(1)}, f32[6,8,80,256]{3,2,1,0:T(8,128)S(1)}) custom-call(s32[4]{0:T(128)S(1)} %pad_add_fusion.where_ref, bf16[72,640]{1,0:T(8,128)(2,1)S(1)} %get-tuple-element.28.refs_0_, bf16[72,640]{1,0:T(8,128)(2,1)S(1)} %collective-permute-done.refs_1_, ...), custom_call_target="tpu_custom_call" | custom-call | flops 6000000000 | tf_op jit(solution)/shard_map/pallas_call | solution.py:56
  22.0 0.0 collective-permute-done.5.refs_3_
  22.0 0.0 collective-permute-done.6.refs_4_
  22.0 0.0 collective-permute-done.7.refs_5_
  22.0 0.0 collective-permute-done.4.refs_1_
  22.1 0.0 collective-permute-done.3.refs_0_
  22.1 11.1 %shard_map.81 = (bf16[8,12,80,256]{3,2,1,0:T(8,128)(2,1)S(1)}, bf16[6,8,80,256]{3,2,1,0:T(8,128)(2,1)S(1)}, f32[6,8,80,256]{3,2,1,0:T(8,128)S(1)}, f32[4,640,128...) custom-call(s32[4]{0:T(128)S(1)} %pad_add_fusion.where_ref, ...), custom_call_target="tpu_custom_call", output_to_operand_aliasing={{0}: (11, {}), {1}: (12, {}), {2}: (13, {})} | custom-call | flops 12000000000 | tf_op jit(solution)/shard_map/pallas_call | solution.py:56
  33.2 0.1 broadcast_select_fusion
  33.3 0.9 %collective-permute-start.9 = (bf16[4,72,384]{2,1,0:T(8,128)(2,1)S(1)}, bf16[4,72,384]{2,1,0:T(8,128)(2,1)S(1)}, u32[]{:S(2)}, u32[]{:S(2)}) collective-permute-start(bf16[4,72,384]{2,1,0:T(8,128)(2,1)S(1)} %get-tuple-element.54), channel_id=1, source_target_pairs={{1,2},{2,1},{3,4},{4,3},{5,6},{6,5},{9,10},{10,9},{11,12},{12,11},... | collective-permute-start | bytes 663560 | tf_op jit(solution)/shard_map/ppermute | solution.py:339
  34.2 3.0 %collective-permute-start.8 = (bf16[4,72,384]{2,1,0:T(8,128)(2,1)S(1)}, bf16[4,72,384]{2,1,0:T(8,128)(2,1)S(1)}, u32[]{:S(2)}, u32[]{:S(2)}) collective-permute-start(bf16[4,72,384]{2,1,0:T(8,128)(2,1)S(1)} %get-tuple-element.55), channel_id=1, source_target_pairs={{0,1},{1,0},{2,3},{3,2},{4,5},{5,4},{6,7},{7,6},{8,9},{9,8},{10,11... | collective-permute-start | bytes 663560 | tf_op jit(solution)/shard_map/ppermute | solution.py:340
  37.2 2.4 %shard_map.82 = (bf16[8,8,80,256]{3,2,1,0:T(8,128)(2,1)S(1)}, bf16[6,12,80,256]{3,2,1,0:T(8,128)(2,1)S(1)}, f32[72,512]{1,0:T(8,128)S(1)}, bf16[72,512]{1,0:T(8,...) custom-call(s32[4]{0:T(128)S(1)} %pad_add_fusion.where_ref, ...), custom_call_target="tpu_custom_call" | custom-call | flops 4000000000 | tf_op jit(solution)/shard_map/pallas_call | solution.py:56
  39.5 0.0 collective-permute-done.9.far
  39.5 0.0 collective-permute-done.8.near
  39.5 3.2 %shard_map.83 = (bf16[8,8,80,256]{3,2,1,0:T(8,128)(2,1)S(1)}, bf16[6,12,80,256]{3,2,1,0:T(8,128)(2,1)S(1)}) custom-call(s32[4]{0:T(128)S(1)} %pad_add_fusion.where_ref, bf16[4,72,384]{2,1,0:T(8,128)(2,1)S(1)} %collective-permute-done.8.near, bf16[4,72,384]{2,1,0:T(8,128)(2,1)S(1)} %collective-permute-done.9.far, ...), custom_call_target="tpu_custom_call", output_to_operand_aliasing={{0}: (5, {}), {1}: (6, {})} | custom-call | flops 3000000000 | tf_op jit(solution)/shard_map/pallas_call | solution.py:56
  42.7 2.2 %shard_map.87 = bf16[72,1024]{1,0:T(8,128)(2,1)S(1)} custom-call(s32[4]{0:T(128)S(1)} %pad_add_fusion.where_ref, bf16[6,12,80,256]{3,2,1,0:T(8,128)(2,1)S(1)} %get-tuple-element.49.grad_ref, bf16[15,256,256]{2,1,0:T(8,128)(2,1)S(1)} %get-tuple-element.36.refs_4_.refs_6_.w_in, bf16[72,512]{1,0:T(8,128)(2,1)S(1)} %get-tuple-element.53.scores_ref), custom_call_target="tpu_custom_call" | custom-call | flops 2000000000 | tf_op jit(solution)/shard_map/pallas_call | solution.py:56
  44.9 2.2 %shard_map.86 = bf16[72,1024]{1,0:T(8,128)(2,1)S(1)} custom-call(s32[4]{0:T(128)S(1)} %pad_add_fusion.where_ref, bf16[6,12,80,256]{3,2,1,0:T(8,128)(2,1)S(1)} %get-tuple-element.49.grad_ref, bf16[15,256,256]{2,1,0:T(8,128)(2,1)S(1)} %get-tuple-element.36.refs_4_.refs_6_.w_in, bf16[72,512]{1,0:T(8,128)(2,1)S(1)} %get-tuple-element.52.scores_ref), custom_call_target="tpu_custom_call" | custom-call | flops 2000000000 | tf_op jit(solution)/shard_map/pallas_call | solution.py:56
  47.1 2.2 %shard_map.85 = bf16[72,1024]{1,0:T(8,128)(2,1)S(1)} custom-call(s32[4]{0:T(128)S(1)} %pad_add_fusion.where_ref, bf16[6,12,80,256]{3,2,1,0:T(8,128)(2,1)S(1)} %get-tuple-element.49.grad_ref, bf16[15,256,256]{2,1,0:T(8,128)(2,1)S(1)} %get-tuple-element.36.refs_4_.refs_6_.w_in, bf16[72,512]{1,0:T(8,128)(2,1)S(1)} %get-tuple-element.51.scores_ref), custom_call_target="tpu_custom_call" | custom-call | flops 2000000000 | tf_op jit(solution)/shard_map/pallas_call | solution.py:56
  49.4 2.0 %collective-permute-start.10 = (bf16[72,1024]{1,0:T(8,128)(2,1)S(1)}, bf16[72,1024]{1,0:T(8,128)(2,1)S(1)}, u32[]{:S(2)}, u32[]{:S(2)}) collective-permute-start(bf16[72,1024]{1,0:T(8,128)(2,1)S(1)} %shard_map.85), channel_id=1, source_target_pairs={{0,8},{8,0},{16,24},{24,16},{1,9},{9,1},{17,25},{25,17},{2,10},{10... | collective-permute-start | bytes 442376 | tf_op jit(solution)/shard_map/ppermute | solution.py:331
  51.4 1.5 %collective-permute-start.11 = (bf16[72,1024]{1,0:T(8,128)(2,1)S(1)}, bf16[72,1024]{1,0:T(8,128)(2,1)S(1)}, u32[]{:S(2)}, u32[]{:S(2)}) collective-permute-start(bf16[72,1024]{1,0:T(8,128)(2,1)S(1)} %shard_map.86), channel_id=1, source_target_pairs={{0,16},{8,24},{16,0},{24,8},{1,17},{9,25},{17,1},{25,9},{2,18},{10... | collective-permute-start | bytes 442376 | tf_op jit(solution)/shard_map/ppermute | solution.py:331
  52.9 0.0 collective-permute-start.12
  52.9 2.3 %shard_map.84.refs_0_ = f32[72,1024]{1,0:T(8,128)S(1)} custom-call(s32[4]{0:T(128)S(1)} %pad_add_fusion.where_ref, bf16[6,12,80,256]{3,2,1,0:T(8,128)(2,1)S(1)} %get-tuple-element.49.grad_ref, bf16[15,256,256]{2,1,0:T(8,128)(2,1)S(1)} %get-tuple-element.36.refs_4_.refs_6_.w_in, f32[72,512]{1,0:T(8,128)S(1)} %get-tuple-element.50.scores_ref), custom_call_target="tpu_custom_call" | custom-call | flops 2000000000 | tf_op jit(solution)/shard_map/pallas_call | solution.py:56
  55.2 0.7 %collective-permute-done.10.refs_1_ = bf16[72,1024]{1,0:T(8,128)(2,1)S(1)} collective-permute-done((bf16[72,1024]{1,0:T(8,128)(2,1)S(1)}, bf16[72,1024]{1,0:T(8,128)(2,1)S(1)}, u32[]{:S(2)}, u32[]{:S(2)}) %collective-permute-start.10) | collective-permute-done | bytes 147488 | tf_op jit(solution)/shard_map/ppermute | solution.py:331
  55.9 5.2 %collective-permute-done.11.refs_2_ = bf16[72,1024]{1,0:T(8,128)(2,1)S(1)} collective-permute-done((bf16[72,1024]{1,0:T(8,128)(2,1)S(1)}, bf16[72,1024]{1,0:T(8,128)(2,1)S(1)}, u32[]{:S(2)}, u32[]{:S(2)}) %collective-permute-start.11) | collective-permute-done | bytes 147488 | tf_op jit(solution)/shard_map/ppermute | solution.py:331
  61.0 0.0 collective-permute-done.12.refs_3_
  61.0 2.2 %shard_map.88 = (f32[2,69,4,256]{3,2,1,0:T(4,128)}, f32[2,69,4,256]{3,2,1,0:T(4,128)}) custom-call(s32[4]{0:T(128)S(1)} %pad_add_fusion.where_ref, f32[72,1024]{1,0:T(8,128)S(1)} %shard_map.84.refs_0_, bf16[72,1024]{1,0:T(8,128)(2,1)S(1)} %collective-permute-done.10.refs_1_, bf16[72,1024]{1,0:T(8,128)(2,1)S(1)} %collective-permute-done.11.refs_2_, ...), custom_call_target="tpu_custom_call" | custom-call | flops 1500000000 | tf_op jit(solution)/shard_map/pallas_call | solution.py:56
  (7 shorter events, 0.1 us)
Async XLA Ops:
  0.7 1.1 %copy-start.1 = (f32[2,69,4,256]{3,2,1,0:T(4,128)S(1)}, f32[2,69,4,256]{3,2,1,0:T(4,128)}, u32[]{:S(2)}) copy-start(f32[2,69,4,256]{3,2,1,0:T(4,128)} %x_ref.2) | copy-start | bytes 1695748
  1.8 5.6 %copy-start.2 = (f32[2,69,4,256]{3,2,1,0:T(4,128)S(1)}, f32[2,69,4,256]{3,2,1,0:T(4,128)}, u32[]{:S(2)}) copy-start(f32[2,69,4,256]{3,2,1,0:T(4,128)} %x_ref.3) | copy-start | bytes 1695748
  2.8 11.1 %collective-permute-start = (bf16[72,640]{1,0:T(8,128)(2,1)S(1)}, bf16[72,640]{1,0:T(8,128)(2,1)S(1)}, u32[]{:S(2)}, u32[]{:S(2)}) collective-permute-start(bf16[72,640]{1,0:T(8,128)(2,1)S(1)} %get-tuple-element.29), channel_id=1, source_target_pairs={{0,8},{8,0},{16,24},{24,16},{1,9},{9,1},{17,25},{25,17},{2,10},{10... | collective-permute-start | bytes 276488 | tf_op jit(solution)/shard_map/ppermute | solution.py:331
  5.8 8.0 %collective-permute-start.1 = (bf16[72,640]{1,0:T(8,128)(2,1)S(1)}, bf16[72,640]{1,0:T(8,128)(2,1)S(1)}, u32[]{:S(2)}, u32[]{:S(2)}) collective-permute-start(bf16[72,640]{1,0:T(8,128)(2,1)S(1)} %get-tuple-element.30), channel_id=1, source_target_pairs={{0,16},{8,24},{16,0},{24,8},{1,17},{9,25},{17,1},{25,9},{2,18},{10... | collective-permute-start | bytes 276488 | tf_op jit(solution)/shard_map/ppermute | solution.py:331
  7.3 4.6 %copy-start = (bf16[3,3,256,345]{2,3,1,0:T(8,128)(2,1)S(1)}, bf16[3,3,256,345]{2,3,1,0:T(8,128)(2,1)}, u32[]{:S(2)}) copy-start(bf16[3,3,256,345]{2,3,1,0:T(8,128)(2,1)} %param.8) | copy-start | bytes 4769284
  7.3 4.6 %copy-start.3 = (bf16[3,3,69,256]{3,2,1,0:T(8,128)(2,1)S(1)}, bf16[3,3,69,256]{3,2,1,0:T(8,128)(2,1)}, u32[]{:S(2)}) copy-start(bf16[3,3,69,256]{3,2,1,0:T(8,128)(2,1)} %k_out.1) | copy-start | bytes 953860
  7.3 6.4 %collective-permute-start.2 = (bf16[72,640]{1,0:T(8,128)(2,1)S(1)}, bf16[72,640]{1,0:T(8,128)(2,1)S(1)}, u32[]{:S(2)}, u32[]{:S(2)}) collective-permute-start(bf16[72,640]{1,0:T(8,128)(2,1)S(1)} %get-tuple-element.31), channel_id=1, source_target_pairs={{0,24},{8,16},{16,8},{24,0},{1,25},{9,17},{17,9},{25,1},{2,26},{10... | collective-permute-start | bytes 276488 | tf_op jit(solution)/shard_map/ppermute | solution.py:331
  8.3 13.7 %collective-permute-start.5 = (f32[72,640]{1,0:T(8,128)S(1)}, f32[72,640]{1,0:T(8,128)S(1)}, u32[]{:S(2)}, u32[]{:S(2)}) collective-permute-start(f32[72,640]{1,0:T(8,128)S(1)} %get-tuple-element.33), channel_id=1, source_target_pairs={{0,8},{8,0},{16,24},{24,16},{1,9},{9,1},{17,25},{25,17},{2,10},{10... | collective-permute-start | bytes 552968 | tf_op jit(solution)/shard_map/ppermute | solution.py:331
  10.4 11.7 %collective-permute-start.6 = (f32[72,640]{1,0:T(8,128)S(1)}, f32[72,640]{1,0:T(8,128)S(1)}, u32[]{:S(2)}, u32[]{:S(2)}) collective-permute-start(f32[72,640]{1,0:T(8,128)S(1)} %get-tuple-element.34), channel_id=1, source_target_pairs={{0,16},{8,24},{16,0},{24,8},{1,17},{9,25},{17,1},{25,9},{2,18},{10... | collective-permute-start | bytes 552968 | tf_op jit(solution)/shard_map/ppermute | solution.py:331
  11.9 0.7 %copy-start.5 = (f32[69]{0:T(128)S(1)}, f32[69]{0:T(128)}, u32[]{:S(2)}) copy-start(f32[69]{0:T(128)} %param.11) | copy-start | bytes 832
  11.9 5.7 %copy-start.4 = (f32[256]{0:T(256)S(1)}, f32[256]{0:T(256)}, u32[]{:S(2)}) copy-start(f32[256]{0:T(256)} %param.9) | copy-start | bytes 3076
  13.8 8.3 %collective-permute-start.7 = (f32[72,640]{1,0:T(8,128)S(1)}, f32[72,640]{1,0:T(8,128)S(1)}, u32[]{:S(2)}, u32[]{:S(2)}) collective-permute-start(f32[72,640]{1,0:T(8,128)S(1)} %get-tuple-element.35), channel_id=1, source_target_pairs={{0,24},{8,16},{16,8},{24,0},{1,25},{9,17},{17,9},{25,1},{2,26},{10... | collective-permute-start | bytes 552968 | tf_op jit(solution)/shard_map/ppermute | solution.py:331
  13.9 8.1 %collective-permute-start.4 = (bf16[4,72,384]{2,1,0:T(8,128)(2,1)S(1)}, bf16[4,72,384]{2,1,0:T(8,128)(2,1)S(1)}, u32[]{:S(2)}, u32[]{:S(2)}) collective-permute-start(bf16[4,72,384]{2,1,0:T(8,128)(2,1)S(1)} %get-tuple-element.56), channel_id=1, source_target_pairs={{1,2},{2,1},{3,4},{4,3},{5,6},{6,5},{9,10},{10,9},{11,12},{12,11},... | collective-permute-start | bytes 663560 | tf_op jit(solution)/shard_map/ppermute | solution.py:339
  14.6 7.4 %collective-permute-start.3 = (bf16[4,72,384]{2,1,0:T(8,128)(2,1)S(1)}, bf16[4,72,384]{2,1,0:T(8,128)(2,1)S(1)}, u32[]{:S(2)}, u32[]{:S(2)}) collective-permute-start(bf16[4,72,384]{2,1,0:T(8,128)(2,1)S(1)} %get-tuple-element.57), channel_id=1, source_target_pairs={{0,1},{1,0},{2,3},{3,2},{4,5},{5,4},{6,7},{7,6},{8,9},{9,8},{10,11... | collective-permute-start | bytes 663560 | tf_op jit(solution)/shard_map/ppermute | solution.py:340
  33.3 6.2 %collective-permute-start.9 = (bf16[4,72,384]{2,1,0:T(8,128)(2,1)S(1)}, bf16[4,72,384]{2,1,0:T(8,128)(2,1)S(1)}, u32[]{:S(2)}, u32[]{:S(2)}) collective-permute-start(bf16[4,72,384]{2,1,0:T(8,128)(2,1)S(1)} %get-tuple-element.54), channel_id=1, source_target_pairs={{1,2},{2,1},{3,4},{4,3},{5,6},{6,5},{9,10},{10,9},{11,12},{12,11},... | collective-permute-start | bytes 663560 | tf_op jit(solution)/shard_map/ppermute | solution.py:339
  34.2 5.4 %collective-permute-start.8 = (bf16[4,72,384]{2,1,0:T(8,128)(2,1)S(1)}, bf16[4,72,384]{2,1,0:T(8,128)(2,1)S(1)}, u32[]{:S(2)}, u32[]{:S(2)}) collective-permute-start(bf16[4,72,384]{2,1,0:T(8,128)(2,1)S(1)} %get-tuple-element.55), channel_id=1, source_target_pairs={{0,1},{1,0},{2,3},{3,2},{4,5},{5,4},{6,7},{7,6},{8,9},{9,8},{10,11... | collective-permute-start | bytes 663560 | tf_op jit(solution)/shard_map/ppermute | solution.py:340
  49.4 6.5 %collective-permute-start.10 = (bf16[72,1024]{1,0:T(8,128)(2,1)S(1)}, bf16[72,1024]{1,0:T(8,128)(2,1)S(1)}, u32[]{:S(2)}, u32[]{:S(2)}) collective-permute-start(bf16[72,1024]{1,0:T(8,128)(2,1)S(1)} %shard_map.85), channel_id=1, source_target_pairs={{0,8},{8,0},{16,24},{24,16},{1,9},{9,1},{17,25},{25,17},{2,10},{10... | collective-permute-start | bytes 442376 | tf_op jit(solution)/shard_map/ppermute | solution.py:331
  51.4 9.7 %collective-permute-start.11 = (bf16[72,1024]{1,0:T(8,128)(2,1)S(1)}, bf16[72,1024]{1,0:T(8,128)(2,1)S(1)}, u32[]{:S(2)}, u32[]{:S(2)}) collective-permute-start(bf16[72,1024]{1,0:T(8,128)(2,1)S(1)} %shard_map.86), channel_id=1, source_target_pairs={{0,16},{8,24},{16,0},{24,8},{1,17},{9,25},{17,1},{25,9},{2,18},{10... | collective-permute-start | bytes 442376 | tf_op jit(solution)/shard_map/ppermute | solution.py:331
  52.9 8.2 %collective-permute-start.12 = (bf16[72,1024]{1,0:T(8,128)(2,1)S(1)}, bf16[72,1024]{1,0:T(8,128)(2,1)S(1)}, u32[]{:S(2)}, u32[]{:S(2)}) collective-permute-start(bf16[72,1024]{1,0:T(8,128)(2,1)S(1)} %shard_map.87), channel_id=1, source_target_pairs={{0,24},{8,16},{16,8},{24,0},{1,25},{9,17},{17,9},{25,1},{2,26},{10... | collective-permute-start | bytes 442376 | tf_op jit(solution)/shard_map/ppermute | solution.py:331

commit v3 on v2

--- a/solution.py
+++ b/solution.py
@@ -205,20 +205,19 @@
     hidden_rows(p, where_ref, taps_ref, w_in, bias_in, act_ref, slope_ref, p.rows - 2, lambda s: s + REACH)
 
 
-def score_kernel(p, where_ref, *refs):
-    n = p.n
-    near, far, targets = refs[0], refs[1], refs[2 : n + 2]
-    w_in, bias_in, w_out, bias_out = refs[n + 2 : n + 6]
-    refs = refs[n + 9 :]
-    taps_ref, act_ref, slope_ref, wide_ref = refs[:4]
-    resids = refs[4 : n + 4]
-    rows_ref, part_ref = refs[n + 4 :]
-    me = where_ref[0]
+def outer_kernel(p, where_ref, near, far, w_in, bias_in, _taps, _act, _slope, taps_ref, act_ref, slope_ref, rows_ref):
     fill_halo(p, where_ref, near, far, rows_ref, taps_ref, False, p.side)
     wrap(p, taps_ref, 0, REACH)
     wrap(p, taps_ref, REACH + p.rows, REACH)
     edge = lambda s: jnp.where(s < REACH, s, s + p.rows - 2)
     hidden_rows(p, where_ref, taps_ref, w_in, bias_in, act_ref, slope_ref, 2 * REACH, edge)
+
+
+def score_kernel(p, where_ref, *refs):
+    n = p.n
+    act_ref, w_out, bias_out = refs[:3]
+    targets, wide_ref, resids, part_ref = refs[3 : n + 3], refs[n + 3], refs[n + 4 : 2 * n + 4], refs[2 * n + 4]
+    me = where_ref[0]
     wide_ref[...] = jnp.zeros_like(wide_ref)
 
     def score_row(row, carry):
@@ -331,13 +330,22 @@
     return lax.ppermute(value, "tm", [(i, i ^ d) for i in range(p.n)])
 
 
+def relay_tm(p, blocks, bit):
+    moving = [d for d in range(p.n) if d & bit]
+    moved = send_tm(p, jnp.stack([blocks[d] for d in moving]), bit)
+    blocks = list(blocks)
+    for at, d in enumerate(moving):
+        blocks[d] = moved[at]
+    return blocks
+
+
 def send_lat(p, even, blocks):
     low = jnp.stack([b[:, : p.msg] for b in blocks])
     high = jnp.stack([b[:, p.cut :] for b in blocks])
     inner = [(i, i ^ 1) for i in range(p.m)]
     outer = [(i, ((i + 1) ^ 1) - 1) for i in range(1, p.m - 1)]
+    near = lax.ppermute(jnp.where(even, high, low), "lat", inner)
     far = lax.ppermute(jnp.where(even, low, high), "lat", outer)
-    near = lax.ppermute(jnp.where(even, high, low), "lat", inner)
     return near, far
 
 
@@ -367,7 +375,8 @@
         16 << 20, 2,
     )
     goal = split(observed, F32)
-    goals = [goal[0]] + [send_tm(p, goal[d], d) for d in range(1, n)]
+    stages = [1 << b for b in range(n.bit_length() - 1)]
+    goals = relay_tm(p, goal, stages[0])
     b_in = bias_in.reshape(1, p.hidden)
     b_out = jnp.pad(bias_out, (0, LANES - p.chans)).reshape(1, LANES)
     near, far = send_lat(p, even, blocks)
@@ -382,15 +391,20 @@
         kernel(inner_kernel, p), [taps_shape, act_shape, slope_shape], [columns],
         [where, *blocks, w_in, b_in], 24 << 20, 6,
     )
+    for bit in stages[1:]:
+        goals = relay_tm(p, goals, bit)
+    _, act, slope = call(
+        kernel(outer_kernel, p), [taps_shape, act_shape, slope_shape], [columns],
+        [where, near, far, w_in, b_in, *inner], 24 << 20, 8, {5: 0, 6: 1, 7: 2},
+    )
     part = scratch((p.total, p.wp + 16, p.packed), F32)
     out = call(
         kernel(score_kernel, p),
-        [taps_shape, act_shape, slope_shape, sds((n, p.posp, LANES), F32)] + [sds((p.cp, p.posp), BF16)] * n,
-        [columns, part],
-        [where, near, far, *goals, w_in, b_in, w_out, b_out, *inner],
-        32 << 20, 12, {n + 7: 0, n + 8: 1, n + 9: 2},
-    )
-    slope, wide, resids = out[2], out[3], out[4:]
+        [sds((n, p.posp, LANES), F32)] + [sds((p.cp, p.posp), BF16)] * n,
+        [part],
+        [where, act, w_out, b_out, *goals], 24 << 20, 4,
+    )
+    wide, resids = out[0], out[1:]
     near, far = send_lat(p, even, resids)
     taps_shape = sds((deep, p.total, p.wp, p.packed), BF16)
     grad_shape = sds((p.rows + 2, around, p.wp, p.hidden), BF16)

time: 63.4 us -> 62.3 us (0.983)
  the two profiles are of different devices: /device:TPU:0 before, /device:TPU:18 now
where the time goes in v3:
time: 62.3 us; the launch traced here: 62.1 us
  Pallas kernels  35 us (56%)
  starting transfers between devices  14.3 us (23%)
  waiting for transfers between devices  10.3 us (17%)
  local copies, waits for them, and re-layouts  1.29 us (2%)
  between operations  0.9 us (1%)
    pallas_call x13, Pallas kernels, call(): pl.pallas_call(kernel, out_shape=outs, in_specs=[SMEM if a.dtype == jnp.i...  35 us
    ppermute x8, starting transfers between devices, send_tm(): return lax.ppermute(value, 'tm', [(i, i ^ d) for i in range(p.n)])  9.03 us
    ppermute x8, waiting for transfers between devices, send_tm(): return lax.ppermute(value, 'tm', [(i, i ^ d) for i in range(p.n)])  7.94 us
    ppermute x2, starting transfers between devices, send_lat(): far = lax.ppermute(jnp.where(even, low, high), 'lat', outer)  4.97 us
    ppermute x2, waiting for transfers between devices, send_lat(): far = lax.ppermute(jnp.where(even, low, high), 'lat', outer)  2.36 us
  transfers between devices with their start and end apart: 12, of which 4 were waited for; matrix products, arithmetic and copies ran while one was open for 0% of the time, Pallas kernels for 36%

profile of v3, /device:TPU:18, one launch (start us, length us, event | category | flops | bytes accessed | tf_op | source)
XLA Modules:
  0.0 62.1 jit_solution(11982423598147704931)
XLA Ops:
  0.6 0.1 pad_add_fusion.where_ref
  0.7 0.0 copy-start.1
  0.7 1.1 %copy-done.1 = f32[2,69,4,256]{3,2,1,0:T(4,128)S(1)} copy-done((f32[2,69,4,256]{3,2,1,0:T(4,128)S(1)}, f32[2,69,4,256]{3,2,1,0:T(4,128)}, u32[]{:S(2)}) %copy-start.1) | copy-done | bytes 565272
  1.8 0.0 copy-start.2
  1.8 1.0 %shard_map.77 = (bf16[72,640]{1,0:T(8,128)(2,1)S(1)}, bf16[72,640]{1,0:T(8,128)(2,1)S(1)}, bf16[72,640]{1,0:T(8,128)(2,1)S(1)}, bf16[72,640]{1,0:T(8,128)(2,1)S(1)}) custom-call(s32[4]{0:T(128)S(1)} %pad_add_fusion.where_ref, f32[2,69,4,256]{3,2,1,0:T(4,128)S(1)} %copy-done.1), custom_call_target="tpu_custom_call" | custom-call | flops 1500000000 | tf_op jit(solution)/shard_map/pallas_call | solution.py:56
  2.8 0.6 collective-permute-start
  3.4 1.5 %collective-permute-start.1 = (bf16[72,640]{1,0:T(8,128)(2,1)S(1)}, bf16[72,640]{1,0:T(8,128)(2,1)S(1)}, u32[]{:S(2)}, u32[]{:S(2)}) collective-permute-start(bf16[72,640]{1,0:T(8,128)(2,1)S(1)} %get-tuple-element.31), channel_id=1, source_target_pairs={{0,16},{8,24},{16,0},{24,8},{1,17},{9,25},{17,1},{25,9},{2,18},{10... | collective-permute-start | bytes 276488 | tf_op jit(solution)/shard_map/ppermute | solution.py:330
  4.9 0.0 copy-start
  4.9 0.0 copy-start.3
  4.9 1.4 %collective-permute-start.2 = (bf16[72,640]{1,0:T(8,128)(2,1)S(1)}, bf16[72,640]{1,0:T(8,128)(2,1)S(1)}, u32[]{:S(2)}, u32[]{:S(2)}) collective-permute-start(bf16[72,640]{1,0:T(8,128)(2,1)S(1)} %get-tuple-element.32), channel_id=1, source_target_pairs={{0,24},{8,16},{16,8},{24,0},{1,25},{9,17},{17,9},{25,1},{2,26},{10... | collective-permute-start | bytes 276488 | tf_op jit(solution)/shard_map/ppermute | solution.py:330
  6.3 0.0 copy-done.2
  6.3 1.0 %shard_map.81 = (f32[72,640]{1,0:T(8,128)S(1)}, f32[72,640]{1,0:T(8,128)S(1)}, f32[72,640]{1,0:T(8,128)S(1)}, f32[72,640]{1,0:T(8,128)S(1)}) custom-call(s32[4]{0:T(128)S(1)} %pad_add_fusion.where_ref, f32[2,69,4,256]{3,2,1,0:T(4,128)S(1)} %copy-done.2), custom_call_target="tpu_custom_call" | custom-call | flops 1500000000 | tf_op jit(solution)/shard_map/pallas_call | solution.py:56
  7.4 0.6 collective-permute-start.5
  8.0 0.0 copy-done
  8.0 0.0 copy-done.3
  8.0 0.0 copy-start.5
  8.0 0.0 copy-start.4
  8.0 0.6 shard_map.78
  8.6 0.1 copy-done.5
  8.7 0.0 collective-permute-done.refs_1_
  8.7 0.0 collective-permute-done.1.refs_2_
  8.7 2.0 %collective-permute-done.2.refs_3_ = bf16[72,640]{1,0:T(8,128)(2,1)S(1)} collective-permute-done((bf16[72,640]{1,0:T(8,128)(2,1)S(1)}, bf16[72,640]{1,0:T(8,128)(2,1)S(1)}, u32[]{:S(2)}, u32[]{:S(2)}) %collective-permute-start.2) | collective-permute-done | bytes 92192 | tf_op jit(solution)/shard_map/ppermute | solution.py:330
  10.7 0.1 broadcast_select_fusion.2
  10.8 0.1 collective-permute-start.3
  10.9 2.4 %collective-permute-start.4 = (bf16[4,72,384]{2,1,0:T(8,128)(2,1)S(1)}, bf16[4,72,384]{2,1,0:T(8,128)(2,1)S(1)}, u32[]{:S(2)}, u32[]{:S(2)}) collective-permute-start(bf16[4,72,384]{2,1,0:T(8,128)(2,1)S(1)} %get-tuple-element.58), channel_id=1, source_target_pairs={{1,2},{2,1},{3,4},{4,3},{5,6},{6,5},{9,10},{10,9},{11,12},{12,11},... | collective-permute-start | bytes 663560 | tf_op jit(solution)/shard_map/ppermute | solution.py:348
  13.3 0.0 copy-done.4
  13.3 4.4 %shard_map.79 = (bf16[8,12,80,256]{3,2,1,0:T(8,128)(2,1)S(1)}, bf16[6,8,80,256]{3,2,1,0:T(8,128)(2,1)S(1)}, f32[6,8,80,256]{3,2,1,0:T(8,128)S(1)}) custom-call(s32[4]{0:T(128)S(1)} %pad_add_fusion.where_ref, bf16[72,640]{1,0:T(8,128)(2,1)S(1)} %get-tuple-element.29.refs_0_, bf16[72,640]{1,0:T(8,128)(2,1)S(1)} %collective-permute-done.refs_1_, ...), custom_call_target="tpu_custom_call" | custom-call | flops 6000000000 | tf_op jit(solution)/shard_map/pallas_call | solution.py:56
  17.8 0.0 collective-permute-done.5
  17.8 1.1 %collective-permute-start.6 = (f32[2,72,640]{2,1,0:T(8,128)S(1)}, f32[2,72,640]{2,1,0:T(8,128)S(1)}, u32[]{:S(2)}, u32[]{:S(2)}) collective-permute-start(f32[2,72,640]{2,1,0:T(8,128)S(1)} %pad_maximum_fusion.1), channel_id=1, source_target_pairs={{0,16},{8,24},{16,0},{24,8},{1,17},{9,25},{17,1},{25,9},{2,18},{10... | collective-permute-start | bytes 1105928 | tf_op jit(solution)/shard_map/ppermute | solution.py:330
  18.9 0.0 collective-permute-done.3.near
  18.9 0.0 collective-permute-done.4.far
  18.9 7.6 %shard_map.80 = (bf16[8,12,80,256]{3,2,1,0:T(8,128)(2,1)S(1)}, bf16[6,8,80,256]{3,2,1,0:T(8,128)(2,1)S(1)}, f32[6,8,80,256]{3,2,1,0:T(8,128)S(1)}) custom-call(s32[4]{0:T(128)S(1)} %pad_add_fusion.where_ref, bf16[4,72,384]{2,1,0:T(8,128)(2,1)S(1)} %collective-permute-done.3.near, ...), custom_call_target="tpu_custom_call", output_to_operand_aliasing={{0}: (5, {}), {1}: (6, {}), {2}: (7, {})} | custom-call | flops 8000000000 | tf_op jit(solution)/shard_map/pallas_call | solution.py:56
  26.5 2.7 %collective-permute-done.6 = f32[2,72,640]{2,1,0:T(8,128)S(1)} collective-permute-done((f32[2,72,640]{2,1,0:T(8,128)S(1)}, f32[2,72,640]{2,1,0:T(8,128)S(1)}, u32[]{:S(2)}, u32[]{:S(2)}) %collective-permute-start.6) | collective-permute-done | bytes 368672 | tf_op jit(solution)/shard_map/ppermute | solution.py:330
  29.2 4.0 %shard_map.82 = (f32[4,640,128]{2,1,0:T(8,128)S(1)}, bf16[72,640]{1,0:T(8,128)(2,1)S(1)}, bf16[72,640]{1,0:T(8,128)(2,1)S(1)}, bf16[72,640]{1,0:T(8,128)(2,1)S(1)}, bf16[72,640]{1,0:T(8,128)(2,1)S(1)}) custom-call(s32[4]{0:T(128)S(1)} %pad_add_fusion.where_ref, bf16[6,8,80,256]{3,2,1,0:T(8,128)(2,1)S(1)} %get-tuple-element.37.refs_0_, ...), custom_call_target="tpu_custom_call" | custom-call | flops 4000000000 | tf_op jit(solution)/shard_map/pallas_call | solution.py:56
  33.3 0.1 broadcast_select_fusion
  33.4 0.2 collective-permute-start.7
  33.6 2.5 %collective-permute-start.8 = (bf16[4,72,384]{2,1,0:T(8,128)(2,1)S(1)}, bf16[4,72,384]{2,1,0:T(8,128)(2,1)S(1)}, u32[]{:S(2)}, u32[]{:S(2)}) collective-permute-start(bf16[4,72,384]{2,1,0:T(8,128)(2,1)S(1)} %get-tuple-element.56), channel_id=1, source_target_pairs={{1,2},{2,1},{3,4},{4,3},{5,6},{6,5},{9,10},{10,9},{11,12},{12,11},... | collective-permute-start | bytes 663560 | tf_op jit(solution)/shard_map/ppermute | solution.py:348
  36.1 2.3 %shard_map.83 = (bf16[8,8,80,256]{3,2,1,0:T(8,128)(2,1)S(1)}, bf16[6,12,80,256]{3,2,1,0:T(8,128)(2,1)S(1)}, f32[72,512]{1,0:T(8,128)S(1)}, bf16[72,512]{1,0:T(8,...) custom-call(s32[4]{0:T(128)S(1)} %pad_add_fusion.where_ref, ...), custom_call_target="tpu_custom_call" | custom-call | flops 4000000000 | tf_op jit(solution)/shard_map/pallas_call | solution.py:56
  38.5 0.0 collective-permute-done.7.near
  38.5 2.4 %collective-permute-done.8.far = bf16[4,72,384]{2,1,0:T(8,128)(2,1)S(1)} collective-permute-done((bf16[4,72,384]{2,1,0:T(8,128)(2,1)S(1)}, bf16[4,72,384]{2,1,0:T(8,128)(2,1)S(1)}, u32[]{:S(2)}, u32[]{:S(2)}) %collective-permute-start.8) | collective-permute-done | bytes 221216 | tf_op jit(solution)/shard_map/ppermute | solution.py:348
  40.8 3.1 %shard_map.84 = (bf16[8,8,80,256]{3,2,1,0:T(8,128)(2,1)S(1)}, bf16[6,12,80,256]{3,2,1,0:T(8,128)(2,1)S(1)}) custom-call(s32[4]{0:T(128)S(1)} %pad_add_fusion.where_ref, bf16[4,72,384]{2,1,0:T(8,128)(2,1)S(1)} %collective-permute-done.7.near, bf16[4,72,384]{2,1,0:T(8,128)(2,1)S(1)} %collective-permute-done.8.far, ...), custom_call_target="tpu_custom_call", output_to_operand_aliasing={{0}: (5, {}), {1}: (6, {})} | custom-call | flops 3000000000 | tf_op jit(solution)/shard_map/pallas_call | solution.py:56
  43.9 2.2 %shard_map.88 = bf16[72,1024]{1,0:T(8,128)(2,1)S(1)} custom-call(s32[4]{0:T(128)S(1)} %pad_add_fusion.where_ref, bf16[6,12,80,256]{3,2,1,0:T(8,128)(2,1)S(1)} %get-tuple-element.51.grad_ref, bf16[15,256,256]{2,1,0:T(8,128)(2,1)S(1)} %get-tuple-element.33.refs_4_.w_in, bf16[72,512]{1,0:T(8,128)(2,1)S(1)} %get-tuple-element.55.scores_ref), custom_call_target="tpu_custom_call" | custom-call | flops 2000000000 | tf_op jit(solution)/shard_map/pallas_call | solution.py:56
  46.2 2.1 %collective-permute-start.11 = (bf16[72,1024]{1,0:T(8,128)(2,1)S(1)}, bf16[72,1024]{1,0:T(8,128)(2,1)S(1)}, u32[]{:S(2)}, u32[]{:S(2)}) collective-permute-start(bf16[72,1024]{1,0:T(8,128)(2,1)S(1)} %shard_map.88), channel_id=1, source_target_pairs={{0,24},{8,16},{16,8},{24,0},{1,25},{9,17},{17,9},{25,1},{2,26},{10... | collective-permute-start | bytes 442376 | tf_op jit(solution)/shard_map/ppermute | solution.py:330
  48.3 2.2 %shard_map.87 = bf16[72,1024]{1,0:T(8,128)(2,1)S(1)} custom-call(s32[4]{0:T(128)S(1)} %pad_add_fusion.where_ref, bf16[6,12,80,256]{3,2,1,0:T(8,128)(2,1)S(1)} %get-tuple-element.51.grad_ref, bf16[15,256,256]{2,1,0:T(8,128)(2,1)S(1)} %get-tuple-element.33.refs_4_.w_in, bf16[72,512]{1,0:T(8,128)(2,1)S(1)} %get-tuple-element.54.scores_ref), custom_call_target="tpu_custom_call" | custom-call | flops 2000000000 | tf_op jit(solution)/shard_map/pallas_call | solution.py:56
  50.5 1.6 %collective-permute-start.10 = (bf16[72,1024]{1,0:T(8,128)(2,1)S(1)}, bf16[72,1024]{1,0:T(8,128)(2,1)S(1)}, u32[]{:S(2)}, u32[]{:S(2)}) collective-permute-start(bf16[72,1024]{1,0:T(8,128)(2,1)S(1)} %shard_map.87), channel_id=1, source_target_pairs={{0,16},{8,24},{16,0},{24,8},{1,17},{9,25},{17,1},{25,9},{2,18},{10... | collective-permute-start | bytes 442376 | tf_op jit(solution)/shard_map/ppermute | solution.py:330
  52.1 2.2 %shard_map.86 = bf16[72,1024]{1,0:T(8,128)(2,1)S(1)} custom-call(s32[4]{0:T(128)S(1)} %pad_add_fusion.where_ref, bf16[6,12,80,256]{3,2,1,0:T(8,128)(2,1)S(1)} %get-tuple-element.51.grad_ref, bf16[15,256,256]{2,1,0:T(8,128)(2,1)S(1)} %get-tuple-element.33.refs_4_.w_in, bf16[72,512]{1,0:T(8,128)(2,1)S(1)} %get-tuple-element.53.scores_ref), custom_call_target="tpu_custom_call" | custom-call | flops 2000000000 | tf_op jit(solution)/shard_map/pallas_call | solution.py:56
  54.3 0.1 collective-permute-start.9
  54.4 2.3 %shard_map.85.refs_0_ = f32[72,1024]{1,0:T(8,128)S(1)} custom-call(s32[4]{0:T(128)S(1)} %pad_add_fusion.where_ref, bf16[6,12,80,256]{3,2,1,0:T(8,128)(2,1)S(1)} %get-tuple-element.51.grad_ref, bf16[15,256,256]{2,1,0:T(8,128)(2,1)S(1)} %get-tuple-element.33.refs_4_.w_in, f32[72,512]{1,0:T(8,128)S(1)} %get-tuple-element.52.scores_ref), custom_call_target="tpu_custom_call" | custom-call | flops 2000000000 | tf_op jit(solution)/shard_map/pallas_call | solution.py:56
  56.6 0.0 collective-permute-done.11.refs_3_
  56.6 0.0 collective-permute-done.10.refs_2_
  56.6 3.3 %collective-permute-done.9.refs_1_ = bf16[72,1024]{1,0:T(8,128)(2,1)S(1)} collective-permute-done((bf16[72,1024]{1,0:T(8,128)(2,1)S(1)}, bf16[72,1024]{1,0:T(8,128)(2,1)S(1)}, u32[]{:S(2)}, u32[]{:S(2)}) %collective-permute-start.9) | collective-permute-done | bytes 147488 | tf_op jit(solution)/shard_map/ppermute | solution.py:330
  59.9 2.2 %shard_map.89 = (f32[2,69,4,256]{3,2,1,0:T(4,128)}, f32[2,69,4,256]{3,2,1,0:T(4,128)}) custom-call(s32[4]{0:T(128)S(1)} %pad_add_fusion.where_ref, f32[72,1024]{1,0:T(8,128)S(1)} %shard_map.85.refs_0_, bf16[72,1024]{1,0:T(8,128)(2,1)S(1)} %collective-permute-done.9.refs_1_, bf16[72,1024]{1,0:T(8,128)(2,1)S(1)} %collective-permute-done.10.refs_2_, ...), custom_call_target="tpu_custom_call" | custom-call | flops 1500000000 | tf_op jit(solution)/shard_map/pallas_call | solution.py:56
  (11 shorter events, 0.2 us)
Async XLA Ops:
  0.7 1.1 %copy-start.1 = (f32[2,69,4,256]{3,2,1,0:T(4,128)S(1)}, f32[2,69,4,256]{3,2,1,0:T(4,128)}, u32[]{:S(2)}) copy-start(f32[2,69,4,256]{3,2,1,0:T(4,128)} %x_ref.2) | copy-start | bytes 1695748
  1.8 4.5 %copy-start.2 = (f32[2,69,4,256]{3,2,1,0:T(4,128)S(1)}, f32[2,69,4,256]{3,2,1,0:T(4,128)}, u32[]{:S(2)}) copy-start(f32[2,69,4,256]{3,2,1,0:T(4,128)} %x_ref.3) | copy-start | bytes 1695748
  2.8 5.9 %collective-permute-start = (bf16[72,640]{1,0:T(8,128)(2,1)S(1)}, bf16[72,640]{1,0:T(8,128)(2,1)S(1)}, u32[]{:S(2)}, u32[]{:S(2)}) collective-permute-start(bf16[72,640]{1,0:T(8,128)(2,1)S(1)} %get-tuple-element.30), channel_id=1, source_target_pairs={{0,8},{8,0},{16,24},{24,16},{1,9},{9,1},{17,25},{25,17},{2,10},{10... | collective-permute-start | bytes 276488 | tf_op jit(solution)/shard_map/ppermute | solution.py:330
  3.4 5.3 %collective-permute-start.1 = (bf16[72,640]{1,0:T(8,128)(2,1)S(1)}, bf16[72,640]{1,0:T(8,128)(2,1)S(1)}, u32[]{:S(2)}, u32[]{:S(2)}) collective-permute-start(bf16[72,640]{1,0:T(8,128)(2,1)S(1)} %get-tuple-element.31), channel_id=1, source_target_pairs={{0,16},{8,24},{16,0},{24,8},{1,17},{9,25},{17,1},{25,9},{2,18},{10... | collective-permute-start | bytes 276488 | tf_op jit(solution)/shard_map/ppermute | solution.py:330
  4.9 3.1 %copy-start = (bf16[3,3,256,345]{2,3,1,0:T(8,128)(2,1)S(1)}, bf16[3,3,256,345]{2,3,1,0:T(8,128)(2,1)}, u32[]{:S(2)}) copy-start(bf16[3,3,256,345]{2,3,1,0:T(8,128)(2,1)} %param.8) | copy-start | bytes 4769284
  4.9 3.1 %copy-start.3 = (bf16[3,3,69,256]{3,2,1,0:T(8,128)(2,1)S(1)}, bf16[3,3,69,256]{3,2,1,0:T(8,128)(2,1)}, u32[]{:S(2)}) copy-start(bf16[3,3,69,256]{3,2,1,0:T(8,128)(2,1)} %k_out.1) | copy-start | bytes 953860
  4.9 5.8 %collective-permute-start.2 = (bf16[72,640]{1,0:T(8,128)(2,1)S(1)}, bf16[72,640]{1,0:T(8,128)(2,1)S(1)}, u32[]{:S(2)}, u32[]{:S(2)}) collective-permute-start(bf16[72,640]{1,0:T(8,128)(2,1)S(1)} %get-tuple-element.32), channel_id=1, source_target_pairs={{0,24},{8,16},{16,8},{24,0},{1,25},{9,17},{17,9},{25,1},{2,26},{10... | collective-permute-start | bytes 276488 | tf_op jit(solution)/shard_map/ppermute | solution.py:330
  7.4 10.4 %collective-permute-start.5 = (f32[2,72,640]{2,1,0:T(8,128)S(1)}, f32[2,72,640]{2,1,0:T(8,128)S(1)}, u32[]{:S(2)}, u32[]{:S(2)}) collective-permute-start(f32[2,72,640]{2,1,0:T(8,128)S(1)} %pad_maximum_fusion), channel_id=1, source_target_pairs={{0,8},{8,0},{16,24},{24,16},{1,9},{9,1},{17,25},{25,17},{2,10},{10... | collective-permute-start | bytes 1105928 | tf_op jit(solution)/shard_map/ppermute | solution.py:330
  8.0 0.7 %copy-start.5 = (f32[69]{0:T(128)S(1)}, f32[69]{0:T(128)}, u32[]{:S(2)}) copy-start(f32[69]{0:T(128)} %param.11) | copy-start | bytes 832
  8.0 5.3 %copy-start.4 = (f32[256]{0:T(256)S(1)}, f32[256]{0:T(256)}, u32[]{:S(2)}) copy-start(f32[256]{0:T(256)} %param.9) | copy-start | bytes 3076
  10.8 8.1 %collective-permute-start.3 = (bf16[4,72,384]{2,1,0:T(8,128)(2,1)S(1)}, bf16[4,72,384]{2,1,0:T(8,128)(2,1)S(1)}, u32[]{:S(2)}, u32[]{:S(2)}) collective-permute-start(bf16[4,72,384]{2,1,0:T(8,128)(2,1)S(1)} %get-tuple-element.59), channel_id=1, source_target_pairs={{0,1},{1,0},{2,3},{3,2},{4,5},{5,4},{6,7},{7,6},{8,9},{9,8},{10,11... | collective-permute-start | bytes 663560 | tf_op jit(solution)/shard_map/ppermute | solution.py:347
  10.9 8.1 %collective-permute-start.4 = (bf16[4,72,384]{2,1,0:T(8,128)(2,1)S(1)}, bf16[4,72,384]{2,1,0:T(8,128)(2,1)S(1)}, u32[]{:S(2)}, u32[]{:S(2)}) collective-permute-start(bf16[4,72,384]{2,1,0:T(8,128)(2,1)S(1)} %get-tuple-element.58), channel_id=1, source_target_pairs={{1,2},{2,1},{3,4},{4,3},{5,6},{6,5},{9,10},{10,9},{11,12},{12,11},... | collective-permute-start | bytes 663560 | tf_op jit(solution)/shard_map/ppermute | solution.py:348
  17.8 11.3 %collective-permute-start.6 = (f32[2,72,640]{2,1,0:T(8,128)S(1)}, f32[2,72,640]{2,1,0:T(8,128)S(1)}, u32[]{:S(2)}, u32[]{:S(2)}) collective-permute-start(f32[2,72,640]{2,1,0:T(8,128)S(1)} %pad_maximum_fusion.1), channel_id=1, source_target_pairs={{0,16},{8,24},{16,0},{24,8},{1,17},{9,25},{17,1},{25,9},{2,18},{10... | collective-permute-start | bytes 1105928 | tf_op jit(solution)/shard_map/ppermute | solution.py:330
  33.4 5.1 %collective-permute-start.7 = (bf16[4,72,384]{2,1,0:T(8,128)(2,1)S(1)}, bf16[4,72,384]{2,1,0:T(8,128)(2,1)S(1)}, u32[]{:S(2)}, u32[]{:S(2)}) collective-permute-start(bf16[4,72,384]{2,1,0:T(8,128)(2,1)S(1)} %get-tuple-element.57), channel_id=1, source_target_pairs={{0,1},{1,0},{2,3},{3,2},{4,5},{5,4},{6,7},{7,6},{8,9},{9,8},{10,11... | collective-permute-start | bytes 663560 | tf_op jit(solution)/shard_map/ppermute | solution.py:347
  33.6 7.2 %collective-permute-start.8 = (bf16[4,72,384]{2,1,0:T(8,128)(2,1)S(1)}, bf16[4,72,384]{2,1,0:T(8,128)(2,1)S(1)}, u32[]{:S(2)}, u32[]{:S(2)}) collective-permute-start(bf16[4,72,384]{2,1,0:T(8,128)(2,1)S(1)} %get-tuple-element.56), channel_id=1, source_target_pairs={{1,2},{2,1},{3,4},{4,3},{5,6},{6,5},{9,10},{10,9},{11,12},{12,11},... | collective-permute-start | bytes 663560 | tf_op jit(solution)/shard_map/ppermute | solution.py:348
  46.2 10.5 %collective-permute-start.11 = (bf16[72,1024]{1,0:T(8,128)(2,1)S(1)}, bf16[72,1024]{1,0:T(8,128)(2,1)S(1)}, u32[]{:S(2)}, u32[]{:S(2)}) collective-permute-start(bf16[72,1024]{1,0:T(8,128)(2,1)S(1)} %shard_map.88), channel_id=1, source_target_pairs={{0,24},{8,16},{16,8},{24,0},{1,25},{9,17},{17,9},{25,1},{2,26},{10... | collective-permute-start | bytes 442376 | tf_op jit(solution)/shard_map/ppermute | solution.py:330
  50.5 6.1 %collective-permute-start.10 = (bf16[72,1024]{1,0:T(8,128)(2,1)S(1)}, bf16[72,1024]{1,0:T(8,128)(2,1)S(1)}, u32[]{:S(2)}, u32[]{:S(2)}) collective-permute-start(bf16[72,1024]{1,0:T(8,128)(2,1)S(1)} %shard_map.87), channel_id=1, source_target_pairs={{0,16},{8,24},{16,0},{24,8},{1,17},{9,25},{17,1},{25,9},{2,18},{10... | collective-permute-start | bytes 442376 | tf_op jit(solution)/shard_map/ppermute | solution.py:330
  54.3 5.7 %collective-permute-start.9 = (bf16[72,1024]{1,0:T(8,128)(2,1)S(1)}, bf16[72,1024]{1,0:T(8,128)(2,1)S(1)}, u32[]{:S(2)}, u32[]{:S(2)}) collective-permute-start(bf16[72,1024]{1,0:T(8,128)(2,1)S(1)} %shard_map.86), channel_id=1, source_target_pairs={{0,8},{8,0},{16,24},{24,16},{1,9},{9,1},{17,25},{25,17},{2,10},{10... | collective-permute-start | bytes 442376 | tf_op jit(solution)/shard_map/ppermute | solution.py:330

commit v4 on v3

--- a/solution.py
+++ b/solution.py
@@ -13,6 +13,7 @@
 LANES = 128
 DEPTH = 4
 REACH = 2
+CODE = 14.0
 VMEM = pl.BlockSpec(memory_space=pltpu.VMEM)
 SMEM = pl.BlockSpec(memory_space=pltpu.SMEM)
 
@@ -43,13 +44,17 @@
         self.msg = max(self.posp - self.cut, up(self.half, LANES))
         self.cut = self.posp - self.msg
         self.shift = self.pos - self.half - self.cut
+        self.halfp = up(self.half, LANES)
         self.out = self.rows * self.local * self.wc
         assert self.taps == 3 and LANES <= 2 * self.chans and 3 * self.chans <= self.packed
         assert self.out % LANES == 0 and LANES % self.wc == 0 and self.wx % 8 == 0
-        assert self.lon % LANES == 0 and self.rows >= 2 * REACH and self.n & (self.n - 1) == 0
+        assert self.lon % LANES == 0 and self.rows == 2 * REACH and self.n & (self.n - 1) == 0
 
     def at(self, row, t):
         return (row * self.local + t) * self.wx
+
+    def paired(self, row, t):
+        return row // REACH * self.halfp + self.at(row % REACH, t)
 
 
 def call(kernel, outs, scratch, args, limit, microseconds, aliases={}):
@@ -69,14 +74,14 @@
     return lax.broadcasted_iota(jnp.int32, shape, len(shape) - 1)
 
 
-def split_kernel(p, where_ref, x_ref, *refs):
+def split_kernel(p, place, coded, where_ref, x_ref, *refs):
     outs, held = refs[: p.n], refs[p.n]
     me = where_ref[0]
     held[...] = jnp.zeros_like(held)
     for r in range(p.rows):
         for t in range(p.local):
             v = x_ref[t, :, r, :]
-            start = p.at(r, t)
+            start = place(r, t)
             base, off = start // LANES * LANES, start % LANES
             width = LANES if off + p.wx <= LANES else 2 * LANES
             lane = lanes_of((p.chans, width))
@@ -86,7 +91,8 @@
                 old = held[q, : p.chans, base : base + width]
                 held[q, : p.chans, base : base + width] = jnp.where(inside, y, old)
     for d in range(p.n):
-        outs[d][...] = held[me ^ d].astype(outs[d].dtype)
+        block = held[me ^ d]
+        outs[d][...] = (jnp.exp(CODE * block) if coded else block).astype(BF16)
 
 
 def weights_kernel(p, k_in, k_out, w_in, w_out, flat_ref, held):
@@ -157,6 +163,15 @@
         for r in range(REACH):
             for t in range(p.local):
                 taps_ref[REACH + p.rows + r, t0 + t] = taps_of(p, rows_ref, p.at(r, t), flip)
+
+
+def fill_pairs(p, where_ref, halves, rows_ref, taps_ref, flip, row):
+    me, even = where_ref[0], where_ref[1] == 1
+    for d in range(p.n):
+        to_columns(jnp.where(even, halves[0][d], halves[1][d]), rows_ref)
+        for r in range(REACH):
+            for t in range(p.local):
+                taps_ref[row + r, (me ^ d) * p.local + t] = taps_of(p, rows_ref, p.at(r, t), flip)
 
 
 def wrap(p, ref, begin, count):
@@ -213,31 +228,34 @@
     hidden_rows(p, where_ref, taps_ref, w_in, bias_in, act_ref, slope_ref, 2 * REACH, edge)
 
 
-def score_kernel(p, where_ref, *refs):
+def score_kernel(p, which, where_ref, *refs):
     n = p.n
     act_ref, w_out, bias_out = refs[:3]
-    targets, wide_ref, resids, part_ref = refs[3 : n + 3], refs[n + 3], refs[n + 4 : 2 * n + 4], refs[2 * n + 4]
+    targets, wide_ref, resid_ref, part_ref = refs[3 : n + 3], refs[n + 3], refs[n + 4], refs[n + 5]
     me = where_ref[0]
+    pair = 1 - where_ref[1] if which == 0 else where_ref[1]
     wide_ref[...] = jnp.zeros_like(wide_ref)
 
-    def score_row(row, carry):
+    def score_row(step, carry):
         total = None
         for i in range(p.taps):
-            term = dot(act_ref[row + i].reshape(p.total * p.wp, p.hidden), w_out[i], True)
+            a = act_ref[pair * REACH + step + i].reshape(p.total * p.wp, p.hidden)
+            term = dot(a, w_out[i], True)
             total = term if total is None else total + term
         part_ref[:, 8 : 8 + p.wp, :] = total.reshape(p.total, p.wp, p.packed)
         for d in range(n):
             for t in range(p.local):
                 s = untap(p, part_ref, (me ^ d) * p.local + t, 8, p.wx, False) + bias_out[...]
-                wide_ref[d, pl.ds(pl.multiple_of((row * p.local + t) * p.wx, 8), p.wx), :] = s
+                wide_ref[d, pl.ds(pl.multiple_of((step * p.local + t) * p.wx, 8), p.wx), :] = s
         return carry
 
-    lax.fori_loop(0, p.rows, score_row, 0)
+    lax.fori_loop(0, REACH, score_row, 0)
     for d in range(n):
-        for m in range(p.posp // LANES):
+        for m in range(p.halfp // LANES):
             cols = slice(m * LANES, (m + 1) * LANES)
             tile = wide_ref[d, cols, :].T[: p.cp]
-            resids[d][:, cols] = (tile - targets[d][:, cols]).astype(BF16)
+            target = targets[d][:, pl.ds(pl.multiple_of(pair * p.halfp + m * LANES, LANES), LANES)]
+            resid_ref[d, :, cols] = (tile - jnp.log(target.astype(F32)) * (1.0 / CODE)).astype(BF16)
 
 
 def gradient_rows(p, taps_ref, w_out, slope_ref, grad_ref, count, row_of):
@@ -257,19 +275,23 @@
 
 def back_inner_kernel(p, where_ref, *refs):
     n = p.n
-    blocks, slope_ref, w_out, wide_ref = refs[:n], refs[n], refs[n + 1], refs[n + 2]
-    taps_ref, grad_ref = refs[n + 3 : n + 5]
-    own_ref, scores = refs[n + 5], refs[n + 6 : 2 * n + 5]
-    rows_ref, thin_ref = refs[2 * n + 5 :]
-    fill_own(p, where_ref, blocks, rows_ref, taps_ref, True, 0)
+    resid, wide, slope_ref, w_out = refs[:2], refs[2:4], refs[4], refs[5]
+    taps_ref, grad_ref = refs[6:8]
+    own_ref, scores = refs[8], refs[9 : n + 8]
+    rows_ref, thin_ref = refs[n + 8 :]
+    even = where_ref[1] == 1
+    fill_pairs(p, where_ref, resid, rows_ref, taps_ref, True, REACH)
+    fill_pairs(p, where_ref, resid[::-1], rows_ref, taps_ref, True, 2 * REACH)
     gradient_rows(p, taps_ref, w_out, slope_ref, grad_ref, p.rows - 2, lambda s: s + REACH)
     wrap(p, grad_ref, REACH, p.rows - 2)
     for d in range(n):
         for r in range(p.rows):
-            for t in range(p.local):
-                start = p.at(r, t) + DEPTH
+            first, second = wide if r < REACH else wide[::-1]
+            for t in range(p.local):
+                start = p.at(r % REACH, t) + DEPTH
                 at = (r * p.local + t) * p.wc
-                thin_ref[at : at + p.wc, :] = wide_ref[d, start : start + p.wc, :]
+                here = slice(start, start + p.wc)
+                thin_ref[at : at + p.wc, :] = jnp.where(even, first[d, here, :], second[d, here, :])
         turn(p, thin_ref, own_ref if d == 0 else scores[d - 1], 0)
 
 
@@ -280,14 +302,16 @@
 
 
 def back_outer_kernel(p, where_ref, near, far, slope_ref, w_out, _taps, _grad, taps_ref, grad_ref, rows_ref):
-    fill_halo(p, where_ref, near, far, rows_ref, taps_ref, True, 0)
+    fill_pairs(p, where_ref, (far, near), rows_ref, taps_ref, True, 0)
+    fill_pairs(p, where_ref, (near, far), rows_ref, taps_ref, True, 3 * REACH)
     edge = lambda s: jnp.where(s < REACH, s, s + p.rows - 2)
     gradient_rows(p, taps_ref, w_out, slope_ref, grad_ref, 2 * REACH, edge)
     wrap(p, grad_ref, 0, REACH)
     wrap(p, grad_ref, p.rows, REACH)
 
 
-def guide_kernel(p, d, where_ref, grad_ref, w_in, scores_ref, out_ref, part_ref, thin_ref):
+def guide_kernel(p, d, where_ref, grad_ref, w_in, *refs):
+    out_ref, part_ref, thin_ref = refs[-3:]
     t0 = (where_ref[0] ^ d) * p.local
     total = None
     for i in range(p.taps):
@@ -299,31 +323,31 @@
     part_ref[:, 8 : 8 + p.wp, :] = total.reshape(p.rows * p.local, p.wp, p.packed)
     for r in range(p.rows * p.local):
         thin_ref[r * p.wc : (r + 1) * p.wc, :] = untap(p, part_ref, r, 8 + DEPTH, p.wc, True)
-    out_ref[:, : p.out] = scores_ref[...]
-    turn(p, thin_ref, out_ref, p.out)
-
-
-def join_kernel(p, where_ref, *refs):
-    ins, outs, held = refs[: p.n], refs[p.n : p.n + 2], refs[p.n + 2]
+    turn(p, thin_ref, out_ref, 0)
+    if len(refs) > 3:
+        out_ref[:, p.out :] = refs[0][...]
+
+
+def join_kernel(p, begins, where_ref, *refs):
+    ins, out_ref, held = refs[: p.n], refs[p.n], refs[p.n + 1]
     me = where_ref[0]
     for d in range(p.n):
-        held[me ^ d] = ins[d][...].astype(F32)
+        held[me ^ d] = ins[d][:, begins[d] : begins[d] + p.out].astype(F32)
     per = LANES // p.wc
     lane = lanes_of((p.chans, LANES))
-    for which in range(2):
-        for r in range(p.rows):
-            for t in range(p.local):
-                start = which * p.out + (r * p.local + t) * p.wc
-                base, off = start // LANES * LANES, start % LANES
-                for m in range(p.lon // LANES):
-                    tile = None
-                    for u in range(per):
-                        piece = held[m * per + u, : p.chans, base : base + LANES]
-                        step = (u * p.wc - off) % LANES
-                        if step:
-                            piece = pltpu.roll(piece, step, 1)
-                        tile = piece if tile is None else jnp.where(lane < u * p.wc, tile, piece)
-                    outs[which][t, :, r, m * LANES : (m + 1) * LANES] = tile
+    for r in range(p.rows):
+        for t in range(p.local):
+            start = (r * p.local + t) * p.wc
+            base, off = start // LANES * LANES, start % LANES
+            for m in range(p.lon // LANES):
+                tile = None
+                for u in range(per):
+                    piece = held[m * per + u, : p.chans, base : base + LANES]
+                    step = (u * p.wc - off) % LANES
+                    if step:
+                        piece = pltpu.roll(piece, step, 1)
+                    tile = piece if tile is None else jnp.where(lane < u * p.wc, tile, piece)
+                out_ref[t, :, r, m * LANES : (m + 1) * LANES] = tile
 
 
 def send_tm(p, value, d):
@@ -339,14 +363,12 @@
     return blocks
 
 
-def send_lat(p, even, blocks):
-    low = jnp.stack([b[:, : p.msg] for b in blocks])
-    high = jnp.stack([b[:, p.cut :] for b in blocks])
-    inner = [(i, i ^ 1) for i in range(p.m)]
-    outer = [(i, ((i + 1) ^ 1) - 1) for i in range(1, p.m - 1)]
-    near = lax.ppermute(jnp.where(even, high, low), "lat", inner)
-    far = lax.ppermute(jnp.where(even, low, high), "lat", outer)
-    return near, far
+def send_near(p, value):
+    return lax.ppermute(value, "lat", [(i, i ^ 1) for i in range(p.m)])
+
+
+def send_far(p, value):
+    return lax.ppermute(value, "lat", [(i, ((i + 1) ^ 1) - 1) for i in range(1, p.m - 1)])
 
 
 def shards(states, observed, conv_in, bias_in, conv_out, bias_out):
@@ -360,12 +382,12 @@
     kernel = functools.partial
     scratch = pltpu.VMEM
 
-    def split(field, dtype):
-        shape = [sds((p.cp, p.posp), dtype)] * n
-        held = [scratch((n, p.cp, p.posp), F32)]
-        return call(kernel(split_kernel, p), shape, held, [where, field], 8 << 20, 1.5)
-
-    mine = split(states, BF16)
+    def split(field, place, coded, width):
+        shape = [sds((p.cp, width), BF16)] * n
+        held = [scratch((n, p.cp, width), F32)]
+        return call(kernel(split_kernel, p, place, coded), shape, held, [where, field], 8 << 20, 1.5)
+
+    mine = split(states, p.at, False, p.posp)
     blocks = [mine[0]] + [send_tm(p, mine[d], d) for d in range(1, n)]
     w_in, w_out = call(
         kernel(weights_kernel, p),
@@ -374,12 +396,15 @@
         [jnp.swapaxes(conv_in, 2, 3), conv_out],
         16 << 20, 2,
     )
-    goal = split(observed, F32)
+    goal = split(observed, p.paired, True, 2 * p.halfp)
     stages = [1 << b for b in range(n.bit_length() - 1)]
     goals = relay_tm(p, goal, stages[0])
     b_in = bias_in.reshape(1, p.hidden)
     b_out = jnp.pad(bias_out, (0, LANES - p.chans)).reshape(1, LANES)
-    near, far = send_lat(p, even, blocks)
+    low = jnp.stack([b[:, : p.msg] for b in blocks])
+    high = jnp.stack([b[:, p.cut :] for b in blocks])
+    near = send_near(p, jnp.where(even, high, low))
+    far = send_far(p, jnp.where(even, low, high))
 
     columns = scratch((p.posp + 32, LANES), F32)
     deep = p.rows + 2 * REACH
@@ -398,40 +423,53 @@
         [where, near, far, w_in, b_in, *inner], 24 << 20, 8, {5: 0, 6: 1, 7: 2},
     )
     part = scratch((p.total, p.wp + 16, p.packed), F32)
-    out = call(
-        kernel(score_kernel, p),
-        [sds((n, p.posp, LANES), F32)] + [sds((p.cp, p.posp), BF16)] * n,
-        [part],
-        [where, act, w_out, b_out, *goals], 24 << 20, 4,
-    )
-    wide, resids = out[0], out[1:]
-    near, far = send_lat(p, even, resids)
+
+    def score(which):
+        return call(
+            kernel(score_kernel, p, which),
+            [sds((n, p.halfp, LANES), F32), sds((n, p.cp, p.halfp), BF16)], [part],
+            [where, act, w_out, b_out, *goals], 24 << 20, 2,
+        )
+
+    wide_far, resid_far = score(0)
+    far = send_far(p, resid_far)
+    wide_near, resid_near = score(1)
+    near = send_near(p, resid_near)
     taps_shape = sds((deep, p.total, p.wp, p.packed), BF16)
     grad_shape = sds((p.rows + 2, around, p.wp, p.hidden), BF16)
+    thin = sds((p.cp, p.out), BF16)
     thin_rows = scratch((p.out, LANES), F32)
     out = call(
         kernel(back_inner_kernel, p),
-        [taps_shape, grad_shape, sds((p.cp, p.out), F32)] + [sds((p.cp, p.out), BF16)] * (n - 1),
+        [taps_shape, grad_shape, sds((p.cp, p.out), F32)] + [thin] * (n - 1),
         [columns, thin_rows],
-        [where, *resids, slope, w_out, wide], 24 << 20, 4,
+        [where, resid_far, resid_near, wide_far, wide_near, slope, w_out], 32 << 20, 2.3,
     )
-    taps, grad, scores = out[0], out[1], out[2:]
+    taps, grad, scores = out[0], out[1], list(out[2:])
+    scores[1] = send_tm(p, scores[1], 1)
     taps, grad = call(
         kernel(back_outer_kernel, p), [taps_shape, grad_shape], [columns],
         [where, near, far, slope, w_out, taps, grad], 24 << 20, 3, {5: 0, 6: 1},
     )
     parts = [None] * n
     for d in [*range(n - 1, 0, -1), 0]:
-        part = scratch((p.rows * p.local, p.wp + 16, p.packed), F32)
+        spread = scratch((p.rows * p.local, p.wp + 16, p.packed), F32)
+        ride = [scores[d]] if d > 1 else []
+        shape = sds((p.cp, (1 + len(ride)) * p.out), BF16 if d else F32)
         parts[d] = call(
-            kernel(guide_kernel, p, d), [sds((p.cp, 2 * p.out), scores[d].dtype)], [part, thin_rows],
-            [where, grad, w_in, scores[d]], 16 << 20, 2,
+            kernel(guide_kernel, p, d), [shape], [spread, thin_rows],
+            [where, grad, w_in, *ride], 16 << 20, 2,
         )[0]
         if d:
             parts[d] = send_tm(p, parts[d], d)
-    shape = [sds((p.local, p.chans, p.rows, p.lon), F32)] * 2
-    held = [scratch((n, p.cp, 2 * p.out), F32)]
-    return tuple(call(kernel(join_kernel, p), shape, held, [where, *parts], 16 << 20, 1.5))
+
+    def join(blocks, begins):
+        shape = [sds((p.local, p.chans, p.rows, p.lon), F32)]
+        held = [scratch((n, p.cp, p.out), F32)]
+        return call(kernel(join_kernel, p, begins), shape, held, [where, *blocks], 8 << 20, 1)[0]
+
+    begins = [0, 0] + [p.out] * (n - 2)
+    return join(scores[:2] + parts[2:], begins), join(parts, [0] * n)
 
 
 def solution(mesh):

time: 62.3 us -> 62.6 us (level)
  the two profiles are of different devices: /device:TPU:18 before, /device:TPU:16 now
where the time goes in v4:
time: 62.6 us; the launch traced here: 62.4 us
  Pallas kernels  37.3 us (60%)
  starting transfers between devices  15 us (24%)
  waiting for transfers between devices  7.62 us (12%)
  local copies, waits for them, and re-layouts  1.22 us (2%)
  between operations  0.91 us (1%)
    pallas_call x15, Pallas kernels, call(): pl.pallas_call(kernel, out_shape=outs, in_specs=[SMEM if a.dtype == jnp.i...  37.3 us
    ppermute x9, starting transfers between devices, send_tm(): return lax.ppermute(value, 'tm', [(i, i ^ d) for i in range(p.n)])  9.42 us
    ppermute x9, waiting for transfers between devices, send_tm(): return lax.ppermute(value, 'tm', [(i, i ^ d) for i in range(p.n)])  5.1 us
    ppermute x2, starting transfers between devices, send_far(): lax.ppermute(value, 'lat', [(i, (i + 1 ^ 1) - 1) for i in range(1, p.m -...  4.6 us
    ppermute x2, waiting for transfers between devices, send_far(): lax.ppermute(value, 'lat', [(i, (i + 1 ^ 1) - 1) for i in range(1, p.m -...  2.51 us
  transfers between devices with their start and end apart: 13, of which 4 were waited for; matrix products, arithmetic and copies ran while one was open for 0% of the time, Pallas kernels for 48%

profile of v4, /device:TPU:16, one launch (start us, length us, event | category | flops | bytes accessed | tf_op | source)
XLA Modules:
  0.0 62.4 jit_solution(9676353600636494648)
XLA Ops:
  0.6 0.1 pad_add_fusion.where_ref
  0.7 0.0 copy-start.1
  0.7 1.1 %copy-done.1 = f32[2,69,4,256]{3,2,1,0:T(4,128)S(1)} copy-done((f32[2,69,4,256]{3,2,1,0:T(4,128)S(1)}, f32[2,69,4,256]{3,2,1,0:T(4,128)}, u32[]{:S(2)}) %copy-start.1) | copy-done | bytes 565272
  1.8 0.0 copy-start.2
  1.8 1.0 %shard_map.77 = (bf16[72,640]{1,0:T(8,128)(2,1)S(1)}, bf16[72,640]{1,0:T(8,128)(2,1)S(1)}, bf16[72,640]{1,0:T(8,128)(2,1)S(1)}, bf16[72,640]{1,0:T(8,128)(2,1)S(1)}) custom-call(s32[4]{0:T(128)S(1)} %pad_add_fusion.where_ref, f32[2,69,4,256]{3,2,1,0:T(4,128)S(1)} %copy-done.1), custom_call_target="tpu_custom_call" | custom-call | flops 1500000000 | tf_op jit(solution)/shard_map/pallas_call | solution.py:61
  2.8 1.6 %collective-permute-start = (bf16[72,640]{1,0:T(8,128)(2,1)S(1)}, bf16[72,640]{1,0:T(8,128)(2,1)S(1)}, u32[]{:S(2)}, u32[]{:S(2)}) collective-permute-start(bf16[72,640]{1,0:T(8,128)(2,1)S(1)} %get-tuple-element.29), channel_id=1, source_target_pairs={{0,8},{8,0},{16,24},{24,16},{1,9},{9,1},{17,25},{25,17},{2,10},{10... | collective-permute-start | bytes 276488 | tf_op jit(solution)/shard_map/ppermute | solution.py:354
  4.3 1.5 %collective-permute-start.1 = (bf16[72,640]{1,0:T(8,128)(2,1)S(1)}, bf16[72,640]{1,0:T(8,128)(2,1)S(1)}, u32[]{:S(2)}, u32[]{:S(2)}) collective-permute-start(bf16[72,640]{1,0:T(8,128)(2,1)S(1)} %get-tuple-element.30), channel_id=1, source_target_pairs={{0,16},{8,24},{16,0},{24,8},{1,17},{9,25},{17,1},{25,9},{2,18},{10... | collective-permute-start | bytes 276488 | tf_op jit(solution)/shard_map/ppermute | solution.py:354
  5.8 0.0 copy-start
  5.8 0.0 copy-start.3
  5.8 0.5 collective-permute-start.2
  6.3 0.0 copy-done.2
  6.3 1.1 %shard_map.81 = (bf16[72,768]{1,0:T(8,128)(2,1)S(1)}, bf16[72,768]{1,0:T(8,128)(2,1)S(1)}, bf16[72,768]{1,0:T(8,128)(2,1)S(1)}, bf16[72,768]{1,0:T(8,128)(2,1)S(1)}) custom-call(s32[4]{0:T(128)S(1)} %pad_add_fusion.where_ref, f32[2,69,4,256]{3,2,1,0:T(4,128)S(1)} %copy-done.2), custom_call_target="tpu_custom_call" | custom-call | flops 1500000000 | tf_op jit(solution)/shard_map/pallas_call | solution.py:61
  7.4 1.6 %collective-permute-start.5 = (bf16[2,72,768]{2,1,0:T(8,128)(2,1)S(1)}, bf16[2,72,768]{2,1,0:T(8,128)(2,1)S(1)}, u32[]{:S(2)}, u32[]{:S(2)}) collective-permute-start(bf16[2,72,768]{2,1,0:T(8,128)(2,1)S(1)} %pad_maximum_fusion.2), channel_id=1, source_target_pairs={{0,8},{8,0},{16,24},{24,16},{1,9},{9,1},{17,25},{25,17},{2,10},{10... | collective-permute-start | bytes 663560 | tf_op jit(solution)/shard_map/ppermute | solution.py:354
  9.0 0.0 copy-done
  9.0 0.0 copy-done.3
  9.0 0.0 copy-start.5
  9.0 0.0 copy-start.4
  9.1 0.6 shard_map.78
  9.6 0.1 copy-done.5
  9.7 0.0 collective-permute-done.refs_1_
  9.7 0.2 collective-permute-done.1.refs_2_
  9.9 2.4 %collective-permute-done.2.refs_3_ = bf16[72,640]{1,0:T(8,128)(2,1)S(1)} collective-permute-done((bf16[72,640]{1,0:T(8,128)(2,1)S(1)}, bf16[72,640]{1,0:T(8,128)(2,1)S(1)}, u32[]{:S(2)}, u32[]{:S(2)}) %collective-permute-start.2) | collective-permute-done | bytes 92192 | tf_op jit(solution)/shard_map/ppermute | solution.py:354
  12.3 0.1 broadcast_select_fusion
  12.4 0.1 collective-permute-start.3
  12.5 2.4 %collective-permute-start.4 = (bf16[4,72,384]{2,1,0:T(8,128)(2,1)S(1)}, bf16[4,72,384]{2,1,0:T(8,128)(2,1)S(1)}, u32[]{:S(2)}, u32[]{:S(2)}) collective-permute-start(bf16[4,72,384]{2,1,0:T(8,128)(2,1)S(1)} %get-tuple-element.54), channel_id=1, source_target_pairs={{1,2},{2,1},{3,4},{4,3},{5,6},{6,5},{9,10},{10,9},{11,12},{12,11},... | collective-permute-start | bytes 663560 | tf_op jit(solution)/shard_map/ppermute | solution.py:371
  14.9 0.0 copy-done.4
  14.9 4.4 %shard_map.79 = (bf16[8,12,80,256]{3,2,1,0:T(8,128)(2,1)S(1)}, bf16[6,8,80,256]{3,2,1,0:T(8,128)(2,1)S(1)}, f32[6,8,80,256]{3,2,1,0:T(8,128)S(1)}) custom-call(s32[4]{0:T(128)S(1)} %pad_add_fusion.where_ref, bf16[72,640]{1,0:T(8,128)(2,1)S(1)} %get-tuple-element.28.refs_0_, bf16[72,640]{1,0:T(8,128)(2,1)S(1)} %collective-permute-done.refs_1_, ...), custom_call_target="tpu_custom_call" | custom-call | flops 6000000000 | tf_op jit(solution)/shard_map/pallas_call | solution.py:61
  19.4 0.0 collective-permute-done.5
  19.4 0.6 collective-permute-start.6
  20.0 0.0 collective-permute-done.3.near
  20.0 0.0 collective-permute-done.4.far
  20.0 7.6 %shard_map.80 = (bf16[8,12,80,256]{3,2,1,0:T(8,128)(2,1)S(1)}, bf16[6,8,80,256]{3,2,1,0:T(8,128)(2,1)S(1)}, f32[6,8,80,256]{3,2,1,0:T(8,128)S(1)}) custom-call(s32[4]{0:T(128)S(1)} %pad_add_fusion.where_ref, bf16[4,72,384]{2,1,0:T(8,128)(2,1)S(1)} %collective-permute-done.3.near, ...), custom_call_target="tpu_custom_call", output_to_operand_aliasing={{0}: (5, {}), {1}: (6, {}), {2}: (7, {})} | custom-call | flops 8000000000 | tf_op jit(solution)/shard_map/pallas_call | solution.py:61
  27.6 0.0 collective-permute-done.6
  27.6 2.3 %shard_map.83 = (f32[4,384,128]{2,1,0:T(8,128)S(1)}, bf16[4,72,384]{2,1,0:T(8,128)(2,1)S(1)}) custom-call(s32[4]{0:T(128)S(1)} %pad_add_fusion.where_ref, bf16[6,8,80,256]{3,2,1,0:T(8,128)(2,1)S(1)} %get-tuple-element.36.refs_0_, bf16[3,256,256]{2,1,0:T(8,128)(2,1)S(1)} %get-tuple-element.37.refs_1_.refs_5_.w_out, f32[1,128]{1,0:T(1,128)S(1)} %pad_bitcast_fusion.refs_2_, ...), custom_call_target="tpu_custom_call" | custom-call | flops 2000000000 | tf_op jit(solution)/shard_map/pallas_call | solution.py:61
  30.0 2.4 %shard_map.82 = (f32[4,384,128]{2,1,0:T(8,128)S(1)}, bf16[4,72,384]{2,1,0:T(8,128)(2,1)S(1)}) custom-call(s32[4]{0:T(128)S(1)} %pad_add_fusion.where_ref, bf16[6,8,80,256]{3,2,1,0:T(8,128)(2,1)S(1)} %get-tuple-element.36.refs_0_, bf16[3,256,256]{2,1,0:T(8,128)(2,1)S(1)} %get-tuple-element.37.refs_1_.refs_5_.w_out, f32[1,128]{1,0:T(1,128)S(1)} %pad_bitcast_fusion.refs_2_, ...), custom_call_target="tpu_custom_call" | custom-call | flops 2000000000 | tf_op jit(solution)/shard_map/pallas_call | solution.py:61
  32.3 0.9 %collective-permute-start.8 = (bf16[4,72,384]{2,1,0:T(8,128)(2,1)S(1)}, bf16[4,72,384]{2,1,0:T(8,128)(2,1)S(1)}, u32[]{:S(2)}, u32[]{:S(2)}) collective-permute-start(bf16[4,72,384]{2,1,0:T(8,128)(2,1)S(1)} %get-tuple-element.43.refs_1_), channel_id=1, source_target_pairs={{0,1},{1,0},{2,3},{3,2},{4,5},{5,4},{6,7},{7,6},{8,9},{9,8},{10,11... | collective-permute-start | bytes 663560 | tf_op jit(solution)/shard_map/ppermute | solution.py:367
  33.3 2.2 %collective-permute-start.9 = (bf16[4,72,384]{2,1,0:T(8,128)(2,1)S(1)}, bf16[4,72,384]{2,1,0:T(8,128)(2,1)S(1)}, u32[]{:S(2)}, u32[]{:S(2)}) collective-permute-start(bf16[4,72,384]{2,1,0:T(8,128)(2,1)S(1)} %get-tuple-element.42.refs_0_), channel_id=1, source_target_pairs={{1,2},{2,1},{3,4},{4,3},{5,6},{6,5},{9,10},{10,9},{11,12},{12,11},... | collective-permute-start | bytes 663560 | tf_op jit(solution)/shard_map/ppermute | solution.py:371
  35.5 2.5 %shard_map.84 = (bf16[8,8,80,256]{3,2,1,0:T(8,128)(2,1)S(1)}, bf16[6,12,80,256]{3,2,1,0:T(8,128)(2,1)S(1)}, f32[72,512]{1,0:T(8,128)S(1)}, bf16[72,512]{1,0:T(8,...) custom-call(s32[4]{0:T(128)S(1)} %pad_add_fusion.where_ref, ...), custom_call_target="tpu_custom_call" | custom-call | flops 2300000000 | tf_op jit(solution)/shard_map/pallas_call | solution.py:61
  37.9 0.1 collective-permute-start.7
  38.0 0.0 collective-permute-done.8.near
  38.0 2.5 %collective-permute-done.9.far = bf16[4,72,384]{2,1,0:T(8,128)(2,1)S(1)} collective-permute-done((bf16[4,72,384]{2,1,0:T(8,128)(2,1)S(1)}, bf16[4,72,384]{2,1,0:T(8,128)(2,1)S(1)}, u32[]{:S(2)}, u32[]{:S(2)}) %collective-permute-start.9) | collective-permute-done | bytes 221216 | tf_op jit(solution)/shard_map/ppermute | solution.py:371
  40.5 3.2 %shard_map.85 = (bf16[8,8,80,256]{3,2,1,0:T(8,128)(2,1)S(1)}, bf16[6,12,80,256]{3,2,1,0:T(8,128)(2,1)S(1)}) custom-call(s32[4]{0:T(128)S(1)} %pad_add_fusion.where_ref, bf16[4,72,384]{2,1,0:T(8,128)(2,1)S(1)} %collective-permute-done.8.near, bf16[4,72,384]{2,1,0:T(8,128)(2,1)S(1)} %collective-permute-done.9.far, ...), custom_call_target="tpu_custom_call", output_to_operand_aliasing={{0}: (5, {}), {1}: (6, {})} | custom-call | flops 3000000000 | tf_op jit(solution)/shard_map/pallas_call | solution.py:61
  43.7 2.2 %shard_map.90 = bf16[72,512]{1,0:T(8,128)(2,1)S(1)} custom-call(s32[4]{0:T(128)S(1)} %pad_add_fusion.where_ref, bf16[6,12,80,256]{3,2,1,0:T(8,128)(2,1)S(1)} %get-tuple-element.51.grad_ref, bf16[15,256,256]{2,1,0:T(8,128)(2,1)S(1)} %get-tuple-element.32.refs_4_.w_in), custom_call_target="tpu_custom_call" | custom-call | flops 2000000000 | tf_op jit(solution)/shard_map/pallas_call | solution.py:61
  45.9 0.1 collective-permute-start.12
  46.0 2.2 %shard_map.87 = bf16[72,1024]{1,0:T(8,128)(2,1)S(1)} custom-call(s32[4]{0:T(128)S(1)} %pad_add_fusion.where_ref, bf16[6,12,80,256]{3,2,1,0:T(8,128)(2,1)S(1)} %get-tuple-element.51.grad_ref, bf16[15,256,256]{2,1,0:T(8,128)(2,1)S(1)} %get-tuple-element.32.refs_4_.w_in, bf16[72,512]{1,0:T(8,128)(2,1)S(1)} %get-tuple-element.53.refs_0_), custom_call_target="tpu_custom_call" | custom-call | flops 2000000000 | tf_op jit(solution)/shard_map/pallas_call | solution.py:61
  48.2 3.0 %collective-permute-start.11 = (bf16[72,1024]{1,0:T(8,128)(2,1)S(1)}, bf16[72,1024]{1,0:T(8,128)(2,1)S(1)}, u32[]{:S(2)}, u32[]{:S(2)}) collective-permute-start(bf16[72,1024]{1,0:T(8,128)(2,1)S(1)} %shard_map.87), channel_id=1, source_target_pairs={{0,24},{8,16},{16,8},{24,0},{1,25},{9,17},{17,9},{25,1},{2,26},{10... | collective-permute-start | bytes 442376 | tf_op jit(solution)/shard_map/ppermute | solution.py:354
  51.2 2.2 %shard_map.86 = bf16[72,1024]{1,0:T(8,128)(2,1)S(1)} custom-call(s32[4]{0:T(128)S(1)} %pad_add_fusion.where_ref, bf16[6,12,80,256]{3,2,1,0:T(8,128)(2,1)S(1)} %get-tuple-element.51.grad_ref, bf16[15,256,256]{2,1,0:T(8,128)(2,1)S(1)} %get-tuple-element.32.refs_4_.w_in, bf16[72,512]{1,0:T(8,128)(2,1)S(1)} %get-tuple-element.52.refs_0_), custom_call_target="tpu_custom_call" | custom-call | flops 2000000000 | tf_op jit(solution)/shard_map/pallas_call | solution.py:61
  53.4 0.6 collective-permute-start.10
  54.0 2.3 %shard_map.89.refs_0_ = f32[72,512]{1,0:T(8,128)S(1)} custom-call(s32[4]{0:T(128)S(1)} %pad_add_fusion.where_ref, bf16[6,12,80,256]{3,2,1,0:T(8,128)(2,1)S(1)} %get-tuple-element.51.grad_ref, bf16[15,256,256]{2,1,0:T(8,128)(2,1)S(1)} %get-tuple-element.32.refs_4_.w_in), custom_call_target="tpu_custom_call" | custom-call | flops 2000000000 | tf_op jit(solution)/shard_map/pallas_call | solution.py:61
  56.2 0.0 collective-permute-done.12.refs_1_
  56.2 0.0 collective-permute-done.11.refs_3_
  56.3 2.5 %collective-permute-done.10.refs_2_ = bf16[72,1024]{1,0:T(8,128)(2,1)S(1)} collective-permute-done((bf16[72,1024]{1,0:T(8,128)(2,1)S(1)}, bf16[72,1024]{1,0:T(8,128)(2,1)S(1)}, u32[]{:S(2)}, u32[]{:S(2)}) %collective-permute-start.10) | collective-permute-done | bytes 147488 | tf_op jit(solution)/shard_map/ppermute | solution.py:354
  58.8 1.8 %shard_map.91 = f32[2,69,4,256]{3,2,1,0:T(4,128)} custom-call(s32[4]{0:T(128)S(1)} %pad_add_fusion.where_ref, f32[72,512]{1,0:T(8,128)S(1)} %shard_map.89.refs_0_, bf16[72,512]{1,0:T(8,128)(2,1)S(1)} %collective-permute-done.12.refs_1_, bf16[72,1024]{1,0:T(8,128)(2,1)S(1)} %collective-permute-done.10.refs_2_, ...), custom_call_target="tpu_custom_call" | custom-call | flops 1000000000 | tf_op jit(solution)/shard_map/pallas_call | solution.py:61
  60.6 0.0 collective-permute-done.7.refs_1_
  60.6 1.8 %shard_map.88 = f32[2,69,4,256]{3,2,1,0:T(4,128)} custom-call(s32[4]{0:T(128)S(1)} %pad_add_fusion.where_ref, f32[72,512]{1,0:T(8,128)S(1)} %get-tuple-element.47.refs_0_, bf16[72,512]{1,0:T(8,128)(2,1)S(1)} %collective-permute-done.7.refs_1_, bf16[72,1024]{1,0:T(8,128)(2,1)S(1)} %collective-permute-done.10.refs_2_, ...), custom_call_target="tpu_custom_call" | custom-call | flops 1000000000 | tf_op jit(solution)/shard_map/pallas_call | solution.py:61
  (9 shorter events, 0.1 us)
Async XLA Ops:
  0.7 1.1 %copy-start.1 = (f32[2,69,4,256]{3,2,1,0:T(4,128)S(1)}, f32[2,69,4,256]{3,2,1,0:T(4,128)}, u32[]{:S(2)}) copy-start(f32[2,69,4,256]{3,2,1,0:T(4,128)} %x_ref.2) | copy-start | bytes 1695748
  1.8 4.5 %copy-start.2 = (f32[2,69,4,256]{3,2,1,0:T(4,128)S(1)}, f32[2,69,4,256]{3,2,1,0:T(4,128)}, u32[]{:S(2)}) copy-start(f32[2,69,4,256]{3,2,1,0:T(4,128)} %x_ref.3) | copy-start | bytes 1695748
  2.8 6.9 %collective-permute-start = (bf16[72,640]{1,0:T(8,128)(2,1)S(1)}, bf16[72,640]{1,0:T(8,128)(2,1)S(1)}, u32[]{:S(2)}, u32[]{:S(2)}) collective-permute-start(bf16[72,640]{1,0:T(8,128)(2,1)S(1)} %get-tuple-element.29), channel_id=1, source_target_pairs={{0,8},{8,0},{16,24},{24,16},{1,9},{9,1},{17,25},{25,17},{2,10},{10... | collective-permute-start | bytes 276488 | tf_op jit(solution)/shard_map/ppermute | solution.py:354
  4.3 5.5 %collective-permute-start.1 = (bf16[72,640]{1,0:T(8,128)(2,1)S(1)}, bf16[72,640]{1,0:T(8,128)(2,1)S(1)}, u32[]{:S(2)}, u32[]{:S(2)}) collective-permute-start(bf16[72,640]{1,0:T(8,128)(2,1)S(1)} %get-tuple-element.30), channel_id=1, source_target_pairs={{0,16},{8,24},{16,0},{24,8},{1,17},{9,25},{17,1},{25,9},{2,18},{10... | collective-permute-start | bytes 276488 | tf_op jit(solution)/shard_map/ppermute | solution.py:354
  5.8 3.2 %copy-start = (bf16[3,3,256,345]{2,3,1,0:T(8,128)(2,1)S(1)}, bf16[3,3,256,345]{2,3,1,0:T(8,128)(2,1)}, u32[]{:S(2)}) copy-start(bf16[3,3,256,345]{2,3,1,0:T(8,128)(2,1)} %param.8) | copy-start | bytes 4769284
  5.8 3.2 %copy-start.3 = (bf16[3,3,69,256]{3,2,1,0:T(8,128)(2,1)S(1)}, bf16[3,3,69,256]{3,2,1,0:T(8,128)(2,1)}, u32[]{:S(2)}) copy-start(bf16[3,3,69,256]{3,2,1,0:T(8,128)(2,1)} %k_out.1) | copy-start | bytes 953860
  5.8 6.4 %collective-permute-start.2 = (bf16[72,640]{1,0:T(8,128)(2,1)S(1)}, bf16[72,640]{1,0:T(8,128)(2,1)S(1)}, u32[]{:S(2)}, u32[]{:S(2)}) collective-permute-start(bf16[72,640]{1,0:T(8,128)(2,1)S(1)} %get-tuple-element.31), channel_id=1, source_target_pairs={{0,24},{8,16},{16,8},{24,0},{1,25},{9,17},{17,9},{25,1},{2,26},{10... | collective-permute-start | bytes 276488 | tf_op jit(solution)/shard_map/ppermute | solution.py:354
  7.4 11.9 %collective-permute-start.5 = (bf16[2,72,768]{2,1,0:T(8,128)(2,1)S(1)}, bf16[2,72,768]{2,1,0:T(8,128)(2,1)S(1)}, u32[]{:S(2)}, u32[]{:S(2)}) collective-permute-start(bf16[2,72,768]{2,1,0:T(8,128)(2,1)S(1)} %pad_maximum_fusion.2), channel_id=1, source_target_pairs={{0,8},{8,0},{16,24},{24,16},{1,9},{9,1},{17,25},{25,17},{2,10},{10... | collective-permute-start | bytes 663560 | tf_op jit(solution)/shard_map/ppermute | solution.py:354
  9.0 0.7 %copy-start.5 = (f32[69]{0:T(128)S(1)}, f32[69]{0:T(128)}, u32[]{:S(2)}) copy-start(f32[69]{0:T(128)} %param.11) | copy-start | bytes 832
  9.0 5.9 %copy-start.4 = (f32[256]{0:T(256)S(1)}, f32[256]{0:T(256)}, u32[]{:S(2)}) copy-start(f32[256]{0:T(256)} %param.9) | copy-start | bytes 3076
  12.4 7.6 %collective-permute-start.3 = (bf16[4,72,384]{2,1,0:T(8,128)(2,1)S(1)}, bf16[4,72,384]{2,1,0:T(8,128)(2,1)S(1)}, u32[]{:S(2)}, u32[]{:S(2)}) collective-permute-start(bf16[4,72,384]{2,1,0:T(8,128)(2,1)S(1)} %get-tuple-element.55), channel_id=1, source_target_pairs={{0,1},{1,0},{2,3},{3,2},{4,5},{5,4},{6,7},{7,6},{8,9},{9,8},{10,11... | collective-permute-start | bytes 663560 | tf_op jit(solution)/shard_map/ppermute | solution.py:367
  12.5 7.5 %collective-permute-start.4 = (bf16[4,72,384]{2,1,0:T(8,128)(2,1)S(1)}, bf16[4,72,384]{2,1,0:T(8,128)(2,1)S(1)}, u32[]{:S(2)}, u32[]{:S(2)}) collective-permute-start(bf16[4,72,384]{2,1,0:T(8,128)(2,1)S(1)} %get-tuple-element.54), channel_id=1, source_target_pairs={{1,2},{2,1},{3,4},{4,3},{5,6},{6,5},{9,10},{10,9},{11,12},{12,11},... | collective-permute-start | bytes 663560 | tf_op jit(solution)/shard_map/ppermute | solution.py:371
  19.4 8.2 %collective-permute-start.6 = (bf16[2,72,768]{2,1,0:T(8,128)(2,1)S(1)}, bf16[2,72,768]{2,1,0:T(8,128)(2,1)S(1)}, u32[]{:S(2)}, u32[]{:S(2)}) collective-permute-start(bf16[2,72,768]{2,1,0:T(8,128)(2,1)S(1)} %pad_maximum_fusion.3), channel_id=1, source_target_pairs={{0,16},{8,24},{16,0},{24,8},{1,17},{9,25},{17,1},{25,9},{2,18},{10... | collective-permute-start | bytes 663560 | tf_op jit(solution)/shard_map/ppermute | solution.py:354
  32.3 5.7 %collective-permute-start.8 = (bf16[4,72,384]{2,1,0:T(8,128)(2,1)S(1)}, bf16[4,72,384]{2,1,0:T(8,128)(2,1)S(1)}, u32[]{:S(2)}, u32[]{:S(2)}) collective-permute-start(bf16[4,72,384]{2,1,0:T(8,128)(2,1)S(1)} %get-tuple-element.43.refs_1_), channel_id=1, source_target_pairs={{0,1},{1,0},{2,3},{3,2},{4,5},{5,4},{6,7},{7,6},{8,9},{9,8},{10,11... | collective-permute-start | bytes 663560 | tf_op jit(solution)/shard_map/ppermute | solution.py:367
  33.3 7.2 %collective-permute-start.9 = (bf16[4,72,384]{2,1,0:T(8,128)(2,1)S(1)}, bf16[4,72,384]{2,1,0:T(8,128)(2,1)S(1)}, u32[]{:S(2)}, u32[]{:S(2)}) collective-permute-start(bf16[4,72,384]{2,1,0:T(8,128)(2,1)S(1)} %get-tuple-element.42.refs_0_), channel_id=1, source_target_pairs={{1,2},{2,1},{3,4},{4,3},{5,6},{6,5},{9,10},{10,9},{11,12},{12,11},... | collective-permute-start | bytes 663560 | tf_op jit(solution)/shard_map/ppermute | solution.py:371
  37.9 22.6 %collective-permute-start.7 = (bf16[72,512]{1,0:T(8,128)(2,1)S(1)}, bf16[72,512]{1,0:T(8,128)(2,1)S(1)}, u32[]{:S(2)}, u32[]{:S(2)}) collective-permute-start(bf16[72,512]{1,0:T(8,128)(2,1)S(1)} %get-tuple-element.48), channel_id=1, source_target_pairs={{0,8},{8,0},{16,24},{24,16},{1,9},{9,1},{17,25},{25,17},{2,10},{10... | collective-permute-start | bytes 221192 | tf_op jit(solution)/shard_map/ppermute | solution.py:354
  45.9 10.3 %collective-permute-start.12 = (bf16[72,512]{1,0:T(8,128)(2,1)S(1)}, bf16[72,512]{1,0:T(8,128)(2,1)S(1)}, u32[]{:S(2)}, u32[]{:S(2)}) collective-permute-start(bf16[72,512]{1,0:T(8,128)(2,1)S(1)} %shard_map.90), channel_id=1, source_target_pairs={{0,8},{8,0},{16,24},{24,16},{1,9},{9,1},{17,25},{25,17},{2,10},{10... | collective-permute-start | bytes 221192 | tf_op jit(solution)/shard_map/ppermute | solution.py:354
  48.2 8.1 %collective-permute-start.11 = (bf16[72,1024]{1,0:T(8,128)(2,1)S(1)}, bf16[72,1024]{1,0:T(8,128)(2,1)S(1)}, u32[]{:S(2)}, u32[]{:S(2)}) collective-permute-start(bf16[72,1024]{1,0:T(8,128)(2,1)S(1)} %shard_map.87), channel_id=1, source_target_pairs={{0,24},{8,16},{16,8},{24,0},{1,25},{9,17},{17,9},{25,1},{2,26},{10... | collective-permute-start | bytes 442376 | tf_op jit(solution)/shard_map/ppermute | solution.py:354
  53.4 5.4 %collective-permute-start.10 = (bf16[72,1024]{1,0:T(8,128)(2,1)S(1)}, bf16[72,1024]{1,0:T(8,128)(2,1)S(1)}, u32[]{:S(2)}, u32[]{:S(2)}) collective-permute-start(bf16[72,1024]{1,0:T(8,128)(2,1)S(1)} %shard_map.86), channel_id=1, source_target_pairs={{0,16},{8,24},{16,0},{24,8},{1,17},{9,25},{17,1},{25,9},{2,18},{10... | collective-permute-start | bytes 442376 | tf_op jit(solution)/shard_map/ppermute | solution.py:354

commit v5 on v4

--- a/solution.py
+++ b/solution.py
@@ -15,7 +15,6 @@
 REACH = 2
 CODE = 14.0
 VMEM = pl.BlockSpec(memory_space=pltpu.VMEM)
-SMEM = pl.BlockSpec(memory_space=pltpu.SMEM)
 
 
 def up(value, step):
@@ -57,11 +56,17 @@
         return row // REACH * self.halfp + self.at(row % REACH, t)
 
 
+def here():
+    row = lax.axis_index("lat")
+    flags = [row % 2 == 0, row == 0, row == lax.axis_size("lat") - 1]
+    return [lax.axis_index("tm")] + [flag.astype(jnp.int32) for flag in flags]
+
+
 def call(kernel, outs, scratch, args, limit, microseconds, aliases={}):
     return pl.pallas_call(
-        kernel,
+        lambda *refs: kernel(here(), *refs),
         out_shape=outs,
-        in_specs=[SMEM if a.dtype == jnp.int32 else VMEM for a in args],
+        in_specs=[VMEM] * len(args),
         out_specs=[VMEM] * len(outs),
         scratch_shapes=scratch,
         input_output_aliases=aliases,
@@ -74,9 +79,9 @@
     return lax.broadcasted_iota(jnp.int32, shape, len(shape) - 1)
 
 
-def split_kernel(p, place, coded, where_ref, x_ref, *refs):
+def split_kernel(p, place, coded, where, x_ref, *refs):
     outs, held = refs[: p.n], refs[p.n]
-    me = where_ref[0]
+    me = where[0]
     held[...] = jnp.zeros_like(held)
     for r in range(p.rows):
         for t in range(p.local):
@@ -95,7 +100,7 @@
         outs[d][...] = (jnp.exp(CODE * block) if coded else block).astype(BF16)
 
 
-def weights_kernel(p, k_in, k_out, w_in, w_out, flat_ref, held):
+def weights_kernel(p, where, k_in, k_out, w_in, w_out, flat_ref, held):
     held[...] = jnp.zeros_like(held)
     c = p.chans
     for i in range(p.taps):
@@ -129,20 +134,25 @@
     return jnp.concatenate([low, high], axis=1).astype(BF16)
 
 
-def untap(p, ref, lead, start, count, flip):
+def spread(p, total, parts):
+    lead = total.shape[0] // p.wp
+    for tile, ref in enumerate(parts):
+        ref[:, 8 : 8 + p.wp, :] = total[:, tile * LANES : (tile + 1) * LANES].reshape(lead, p.wp, LANES)
+
+
+def untap(p, parts, lead, start, count, flip):
     before, after = (1, -1) if flip else (-1, 1)
-    s = start
-    first = ref[lead, s + before : s + before + count, :LANES]
-    low = pltpu.roll(ref[lead, s : s + count, :LANES], LANES - p.chans, 1)
-    high = pltpu.roll(ref[lead, s : s + count, LANES:], LANES - p.chans, 1)
+    first = parts[0][lead, start + before : start + before + count, :]
+    low = pltpu.roll(parts[0][lead, start : start + count, :], LANES - p.chans, 1)
+    high = pltpu.roll(parts[1][lead, start : start + count, :], LANES - p.chans, 1)
     lane = lanes_of((count, LANES))
     middle = jnp.where(lane < LANES - p.chans, low, high)
-    last = pltpu.roll(ref[lead, s + after : s + after + count, LANES:], 2 * LANES - 2 * p.chans, 1)
+    last = pltpu.roll(parts[1][lead, start + after : start + after + count, :], 2 * LANES - 2 * p.chans, 1)
     return jnp.where(lane < p.chans, first + middle + last, 0.0)
 
 
-def fill_own(p, where_ref, blocks, rows_ref, taps_ref, flip, base):
-    me = where_ref[0]
+def fill_own(p, where, blocks, rows_ref, taps_ref, flip, base):
+    me = where[0]
     for d in range(p.n):
         t0 = (me ^ d) * p.local + base
         to_columns(blocks[d][...], rows_ref)
@@ -151,8 +161,8 @@
                 taps_ref[REACH + r, t0 + t] = taps_of(p, rows_ref, p.at(r, t), flip)
 
 
-def fill_halo(p, where_ref, near, far, rows_ref, taps_ref, flip, base):
-    me, even = where_ref[0], where_ref[1] == 1
+def fill_halo(p, where, near, far, rows_ref, taps_ref, flip, base):
+    me, even = where[0], where[1] == 1
     for d in range(p.n):
         t0 = (me ^ d) * p.local + base
         to_columns(jnp.where(even, far[d], near[d]), rows_ref)
@@ -165,8 +175,8 @@
                 taps_ref[REACH + p.rows + r, t0 + t] = taps_of(p, rows_ref, p.at(r, t), flip)
 
 
-def fill_pairs(p, where_ref, halves, rows_ref, taps_ref, flip, row):
-    me, even = where_ref[0], where_ref[1] == 1
+def fill_pairs(p, where, halves, rows_ref, taps_ref, flip, row):
+    me, even = where[0], where[1] == 1
     for d in range(p.n):
         to_columns(jnp.where(even, halves[0][d], halves[1][d]), rows_ref)
         for r in range(REACH):
@@ -181,8 +191,8 @@
             ref[row, p.total + p.side + e] = ref[row, p.side + e]
 
 
-def row_mask(p, where_ref, row):
-    outside = ((row == 0) & (where_ref[2] == 1)) | ((row == p.rows + 1) & (where_ref[3] == 1))
+def row_mask(p, where, row):
+    outside = ((row == 0) & (where[2] == 1)) | ((row == p.rows + 1) & (where[3] == 1))
     return jnp.where(outside, 0.0, 1.0)
 
 
@@ -191,7 +201,7 @@
     return lax.dot_general(a, b, dims, preferred_element_type=F32)
 
 
-def hidden_rows(p, where_ref, taps_ref, w_in, bias_in, act_ref, slope_ref, count, row_of):
+def hidden_rows(p, where, taps_ref, w_in, bias_in, act_ref, slope_ref, count, row_of):
     def body(step, carry):
         row = row_of(step)
         total = None
@@ -204,7 +214,7 @@
         sig = 0.5 * jnp.tanh(0.5 * pre) + 0.5
         act = pre * sig
         slope = sig + act * (1.0 - sig)
-        mask = row_mask(p, where_ref, row)
+        mask = row_mask(p, where, row)
         act_ref[row] = (act * mask).astype(BF16).reshape(p.total, p.wp, p.hidden)
         slope_ref[row] = (slope * mask).reshape(p.total, p.wp, p.hidden)
         return carry
@@ -212,28 +222,28 @@
     lax.fori_loop(0, count, body, 0)
 
 
-def inner_kernel(p, where_ref, *refs):
+def inner_kernel(p, where, *refs):
     blocks, w_in, bias_in = refs[: p.n], refs[p.n], refs[p.n + 1]
     taps_ref, act_ref, slope_ref, rows_ref = refs[p.n + 2 :]
-    fill_own(p, where_ref, blocks, rows_ref, taps_ref, False, p.side)
+    fill_own(p, where, blocks, rows_ref, taps_ref, False, p.side)
     wrap(p, taps_ref, REACH, p.rows)
-    hidden_rows(p, where_ref, taps_ref, w_in, bias_in, act_ref, slope_ref, p.rows - 2, lambda s: s + REACH)
-
-
-def outer_kernel(p, where_ref, near, far, w_in, bias_in, _taps, _act, _slope, taps_ref, act_ref, slope_ref, rows_ref):
-    fill_halo(p, where_ref, near, far, rows_ref, taps_ref, False, p.side)
+    hidden_rows(p, where, taps_ref, w_in, bias_in, act_ref, slope_ref, p.rows - 2, lambda s: s + REACH)
+
+
+def outer_kernel(p, where, near, far, w_in, bias_in, _taps, _act, _slope, taps_ref, act_ref, slope_ref, rows_ref):
+    fill_halo(p, where, near, far, rows_ref, taps_ref, False, p.side)
     wrap(p, taps_ref, 0, REACH)
     wrap(p, taps_ref, REACH + p.rows, REACH)
     edge = lambda s: jnp.where(s < REACH, s, s + p.rows - 2)
-    hidden_rows(p, where_ref, taps_ref, w_in, bias_in, act_ref, slope_ref, 2 * REACH, edge)
-
-
-def score_kernel(p, which, where_ref, *refs):
+    hidden_rows(p, where, taps_ref, w_in, bias_in, act_ref, slope_ref, 2 * REACH, edge)
+
+
+def score_kernel(p, which, where, *refs):
     n = p.n
     act_ref, w_out, bias_out = refs[:3]
-    targets, wide_ref, resid_ref, part_ref = refs[3 : n + 3], refs[n + 3], refs[n + 4], refs[n + 5]
-    me = where_ref[0]
-    pair = 1 - where_ref[1] if which == 0 else where_ref[1]
+    targets, wide_ref, resid_ref, parts = refs[3 : n + 3], refs[n + 3], refs[n + 4], refs[n + 5 :]
+    me = where[0]
+    pair = 1 - where[1] if which == 0 else where[1]
     wide_ref[...] = jnp.zeros_like(wide_ref)
 
     def score_row(step, carry):
@@ -242,10 +252,10 @@
             a = act_ref[pair * REACH + step + i].reshape(p.total * p.wp, p.hidden)
             term = dot(a, w_out[i], True)
             total = term if total is None else total + term
-        part_ref[:, 8 : 8 + p.wp, :] = total.reshape(p.total, p.wp, p.packed)
+        spread(p, total, parts)
         for d in range(n):
             for t in range(p.local):
-                s = untap(p, part_ref, (me ^ d) * p.local + t, 8, p.wx, False) + bias_out[...]
+                s = untap(p, parts, (me ^ d) * p.local + t, 8, p.wx, False) + bias_out[...]
                 wide_ref[d, pl.ds(pl.multiple_of((step * p.local + t) * p.wx, 8), p.wx), :] = s
         return carry
 
@@ -273,15 +283,15 @@
     lax.fori_loop(0, count, body, 0)
 
 
-def back_inner_kernel(p, where_ref, *refs):
+def back_inner_kernel(p, where, *refs):
     n = p.n
     resid, wide, slope_ref, w_out = refs[:2], refs[2:4], refs[4], refs[5]
     taps_ref, grad_ref = refs[6:8]
     own_ref, scores = refs[8], refs[9 : n + 8]
     rows_ref, thin_ref = refs[n + 8 :]
-    even = where_ref[1] == 1
-    fill_pairs(p, where_ref, resid, rows_ref, taps_ref, True, REACH)
-    fill_pairs(p, where_ref, resid[::-1], rows_ref, taps_ref, True, 2 * REACH)
+    even = where[1] == 1
+    fill_pairs(p, where, resid, rows_ref, taps_ref, True, REACH)
+    fill_pairs(p, where, resid[::-1], rows_ref, taps_ref, True, 2 * REACH)
     gradient_rows(p, taps_ref, w_out, slope_ref, grad_ref, p.rows - 2, lambda s: s + REACH)
     wrap(p, grad_ref, REACH, p.rows - 2)
     for d in range(n):
@@ -301,18 +311,18 @@
         out_ref[:, begin + m * LANES : begin + (m + 1) * LANES] = tile.astype(out_ref.dtype)
 
 
-def back_outer_kernel(p, where_ref, near, far, slope_ref, w_out, _taps, _grad, taps_ref, grad_ref, rows_ref):
-    fill_pairs(p, where_ref, (far, near), rows_ref, taps_ref, True, 0)
-    fill_pairs(p, where_ref, (near, far), rows_ref, taps_ref, True, 3 * REACH)
+def back_outer_kernel(p, where, near, far, slope_ref, w_out, _taps, _grad, taps_ref, grad_ref, rows_ref):
+    fill_pairs(p, where, (far, near), rows_ref, taps_ref, True, 0)
+    fill_pairs(p, where, (near, far), rows_ref, taps_ref, True, 3 * REACH)
     edge = lambda s: jnp.where(s < REACH, s, s + p.rows - 2)
     gradient_rows(p, taps_ref, w_out, slope_ref, grad_ref, 2 * REACH, edge)
     wrap(p, grad_ref, 0, REACH)
     wrap(p, grad_ref, p.rows, REACH)
 
 
-def guide_kernel(p, d, where_ref, grad_ref, w_in, *refs):
-    out_ref, part_ref, thin_ref = refs[-3:]
-    t0 = (where_ref[0] ^ d) * p.local
+def guide_kernel(p, d, where, grad_ref, w_in, *refs):
+    out_ref, thin_ref, parts = refs[-4], refs[-3], refs[-2:]
+    t0 = (where[0] ^ d) * p.local
     total = None
     for i in range(p.taps):
         for k in range(p.window):
@@ -320,17 +330,17 @@
             a = a.reshape(p.rows * p.local * p.wp, p.hidden)
             term = dot(a, w_in[i * p.window + k], True)
             total = term if total is None else total + term
-    part_ref[:, 8 : 8 + p.wp, :] = total.reshape(p.rows * p.local, p.wp, p.packed)
+    spread(p, total, parts)
     for r in range(p.rows * p.local):
-        thin_ref[r * p.wc : (r + 1) * p.wc, :] = untap(p, part_ref, r, 8 + DEPTH, p.wc, True)
+        thin_ref[r * p.wc : (r + 1) * p.wc, :] = untap(p, parts, r, 8 + DEPTH, p.wc, True)
     turn(p, thin_ref, out_ref, 0)
-    if len(refs) > 3:
+    if len(refs) > 4:
         out_ref[:, p.out :] = refs[0][...]
 
 
-def join_kernel(p, begins, where_ref, *refs):
+def join_kernel(p, begins, where, *refs):
     ins, out_ref, held = refs[: p.n], refs[p.n], refs[p.n + 1]
-    me = where_ref[0]
+    me = where[0]
     for d in range(p.n):
         held[me ^ d] = ins[d][:, begins[d] : begins[d] + p.out].astype(F32)
     per = LANES // p.wc
@@ -374,10 +384,7 @@
 def shards(states, observed, conv_in, bias_in, conv_out, bias_out):
     p = Plan(states, conv_in)
     n = p.n
-    me, row = lax.axis_index("tm"), lax.axis_index("lat")
-    even = row % 2 == 0
-    where = jnp.stack([me, even.astype(jnp.int32), (row == 0).astype(jnp.int32), (row == p.m - 1).astype(jnp.int32)])
-    where = where.astype(jnp.int32)
+    even = lax.axis_index("lat") % 2 == 0
     sds = jax.ShapeDtypeStruct
     kernel = functools.partial
     scratch = pltpu.VMEM
@@ -385,7 +392,7 @@
     def split(field, place, coded, width):
         shape = [sds((p.cp, width), BF16)] * n
         held = [scratch((n, p.cp, width), F32)]
-        return call(kernel(split_kernel, p, place, coded), shape, held, [where, field], 8 << 20, 1.5)
+        return call(kernel(split_kernel, p, place, coded), shape, held, [field], 8 << 20, 1.5)
 
     mine = split(states, p.at, False, p.posp)
     blocks = [mine[0]] + [send_tm(p, mine[d], d) for d in range(1, n)]
@@ -414,21 +421,21 @@
     slope_shape = sds((p.rows + 2, p.total, p.wp, p.hidden), F32)
     inner = call(
         kernel(inner_kernel, p), [taps_shape, act_shape, slope_shape], [columns],
-        [where, *blocks, w_in, b_in], 24 << 20, 6,
+        [*blocks, w_in, b_in], 24 << 20, 6,
     )
     for bit in stages[1:]:
         goals = relay_tm(p, goals, bit)
     _, act, slope = call(
         kernel(outer_kernel, p), [taps_shape, act_shape, slope_shape], [columns],
-        [where, near, far, w_in, b_in, *inner], 24 << 20, 8, {5: 0, 6: 1, 7: 2},
+        [near, far, w_in, b_in, *inner], 24 << 20, 8, {4: 0, 5: 1, 6: 2},
     )
-    part = scratch((p.total, p.wp + 16, p.packed), F32)
+    part = [scratch((p.total, p.wp + 16, LANES), F32)] * 2
 
     def score(which):
         return call(
             kernel(score_kernel, p, which),
-            [sds((n, p.halfp, LANES), F32), sds((n, p.cp, p.halfp), BF16)], [part],
-            [where, act, w_out, b_out, *goals], 24 << 20, 2,
+            [sds((n, p.halfp, LANES), F32), sds((n, p.cp, p.halfp), BF16)], part,
+            [act, w_out, b_out, *goals], 24 << 20, 2,
         )
 
     wide_far, resid_far = score(0)
@@ -443,22 +450,22 @@
         kernel(back_inner_kernel, p),
         [taps_shape, grad_shape, sds((p.cp, p.out), F32)] + [thin] * (n - 1),
         [columns, thin_rows],
-        [where, resid_far, resid_near, wide_far, wide_near, slope, w_out], 32 << 20, 2.3,
+        [resid_far, resid_near, wide_far, wide_near, slope, w_out], 32 << 20, 2.3,
     )
     taps, grad, scores = out[0], out[1], list(out[2:])
     scores[1] = send_tm(p, scores[1], 1)
     taps, grad = call(
         kernel(back_outer_kernel, p), [taps_shape, grad_shape], [columns],
-        [where, near, far, slope, w_out, taps, grad], 24 << 20, 3, {5: 0, 6: 1},
+        [near, far, slope, w_out, taps, grad], 24 << 20, 3, {4: 0, 5: 1},
     )
     parts = [None] * n
     for d in [*range(n - 1, 0, -1), 0]:
-        spread = scratch((p.rows * p.local, p.wp + 16, p.packed), F32)
+        part = [scratch((p.rows * p.local, p.wp + 16, LANES), F32)] * 2
         ride = [scores[d]] if d > 1 else []
         shape = sds((p.cp, (1 + len(ride)) * p.out), BF16 if d else F32)
         parts[d] = call(
-            kernel(guide_kernel, p, d), [shape], [spread, thin_rows],
-            [where, grad, w_in, *ride], 16 << 20, 2,
+            kernel(guide_kernel, p, d), [shape], [thin_rows, *part],
+            [grad, w_in, *ride], 16 << 20, 2,
         )[0]
         if d:
             parts[d] = send_tm(p, parts[d], d)
@@ -466,7 +473,7 @@
     def join(blocks, begins):
         shape = [sds((p.local, p.chans, p.rows, p.lon), F32)]
         held = [scratch((n, p.cp, p.out), F32)]
-        return call(kernel(join_kernel, p, begins), shape, held, [where, *blocks], 8 << 20, 1)[0]
+        return call(kernel(join_kernel, p, begins), shape, held, [*blocks], 8 << 20, 1)[0]
 
     begins = [0, 0] + [p.out] * (n - 2)
     return join(scores[:2] + parts[2:], begins), join(parts, [0] * n)

time: 62.6 us -> 56.8 us (0.907)
  the two profiles are of different devices: /device:TPU:16 before, /device:TPU:21 now
where the time goes in v5:
time: 56.8 us; the launch traced here: 56 us
  Pallas kernels  29.8 us (52%)
  starting transfers between devices  17.7 us (31%)
  waiting for transfers between devices  6.32 us (11%)
  local copies, waits for them, and re-layouts  1.21 us (2%)
  between operations  0.88 us (2%)
    pallas_call x15, Pallas kernels, call(): pl.pallas_call(lambda *refs: kernel(here(), *refs), out_shape=outs, in_sp...  29.8 us
    ppermute x9, starting transfers between devices, send_tm(): return lax.ppermute(value, 'tm', [(i, i ^ d) for i in range(p.n)])  8.26 us
    ppermute x2, starting transfers between devices, send_far(): lax.ppermute(value, 'lat', [(i, (i + 1 ^ 1) - 1) for i in range(1, p.m -...  6.02 us
    ppermute x9, waiting for transfers between devices, send_tm(): return lax.ppermute(value, 'tm', [(i, i ^ d) for i in range(p.n)])  3.97 us
    ppermute x2, starting transfers between devices, send_near(): return lax.ppermute(value, 'lat', [(i, i ^ 1) for i in range(p.m)])  3.44 us
    ppermute x2, waiting for transfers between devices, send_far(): lax.ppermute(value, 'lat', [(i, (i + 1 ^ 1) - 1) for i in range(1, p.m -...  2.34 us
  transfers between devices with their start and end apart: 13, of which 3 were waited for; matrix products, arithmetic and copies ran while one was open for 0% of the time, Pallas kernels for 44%

profile of v5, /device:TPU:21, one launch (start us, length us, event | category | flops | bytes accessed | tf_op | source)
XLA Modules:
  0.0 56.0 jit_solution(7743056305277613510)
XLA Ops:
  0.6 0.0 copy-start.1
  0.6 1.0 %copy-done.1 = f32[2,69,4,256]{3,2,1,0:T(4,128)S(1)} copy-done((f32[2,69,4,256]{3,2,1,0:T(4,128)S(1)}, f32[2,69,4,256]{3,2,1,0:T(4,128)}, u32[]{:S(2)}) %copy-start.1) | copy-done | bytes 565272
  1.7 0.0 copy-start.2
  1.7 0.5 shard_map.77
  2.1 1.3 %collective-permute-start = (bf16[72,640]{1,0:T(8,128)(2,1)S(1)}, bf16[72,640]{1,0:T(8,128)(2,1)S(1)}, u32[]{:S(2)}, u32[]{:S(2)}) collective-permute-start(bf16[72,640]{1,0:T(8,128)(2,1)S(1)} %get-tuple-element.29), channel_id=1, source_target_pairs={{0,8},{8,0},{16,24},{24,16},{1,9},{9,1},{17,25},{25,17},{2,10},{10... | collective-permute-start | bytes 276488 | tf_op jit(solution)/shard_map/ppermute | solution.py:364
  3.4 0.2 collective-permute-start.1
  3.7 0.0 copy-start
  3.7 0.0 copy-start.3
  3.7 1.2 %collective-permute-start.2 = (bf16[72,640]{1,0:T(8,128)(2,1)S(1)}, bf16[72,640]{1,0:T(8,128)(2,1)S(1)}, u32[]{:S(2)}, u32[]{:S(2)}) collective-permute-start(bf16[72,640]{1,0:T(8,128)(2,1)S(1)} %get-tuple-element.31), channel_id=1, source_target_pairs={{0,24},{8,16},{16,8},{24,0},{1,25},{9,17},{17,9},{25,1},{2,26},{10... | collective-permute-start | bytes 276488 | tf_op jit(solution)/shard_map/ppermute | solution.py:364
  4.9 0.0 copy-done.2
  4.9 0.6 %shard_map.81 = (bf16[72,768]{1,0:T(8,128)(2,1)S(1)}, bf16[72,768]{1,0:T(8,128)(2,1)S(1)}, bf16[72,768]{1,0:T(8,128)(2,1)S(1)}, bf16[72,768]{1,0:T(8,128)(2,1)S(1)}) custom-call(f32[2,69,4,256]{3,2,1,0:T(4,128)S(1)} %copy-done.2), custom_call_target="tpu_custom_call" | custom-call | flops 1500000000 | tf_op jit(solution)/shard_map/pallas_call | solution.py:66
  5.5 1.3 %collective-permute-start.5 = (bf16[2,72,768]{2,1,0:T(8,128)(2,1)S(1)}, bf16[2,72,768]{2,1,0:T(8,128)(2,1)S(1)}, u32[]{:S(2)}, u32[]{:S(2)}) collective-permute-start(bf16[2,72,768]{2,1,0:T(8,128)(2,1)S(1)} %pad_maximum_fusion.2), channel_id=1, source_target_pairs={{0,8},{8,0},{16,24},{24,16},{1,9},{9,1},{17,25},{25,17},{2,10},{10... | collective-permute-start | bytes 663560 | tf_op jit(solution)/shard_map/ppermute | solution.py:364
  6.8 0.0 copy-done
  6.8 0.0 copy-done.3
  6.8 0.0 copy-start.5
  6.8 0.0 copy-start.4
  6.8 0.6 %shard_map.78 = (bf16[15,256,256]{2,1,0:T(8,128)(2,1)S(1)}, bf16[3,256,256]{2,1,0:T(8,128)(2,1)S(1)}) custom-call(bf16[3,3,345,256]{3,2,1,0:T(8,128)(2,1)S(1)} %bitcast.32, bf16[3,3,69,256]{3,2,1,0:T(8,128)(2,1)S(1)} %copy-done.3), custom_call_target="tpu_custom_call" | custom-call | flops 2000000000 | tf_op jit(solution)/shard_map/pallas_call | solution.py:66
  7.4 0.1 copy-done.5
  7.5 0.0 collective-permute-done.refs_1_
  7.5 0.0 collective-permute-done.1.refs_2_
  7.5 0.5 collective-permute-done.2.refs_3_
  8.0 0.1 broadcast_select_fusion
  8.1 3.4 %collective-permute-start.3 = (bf16[4,72,384]{2,1,0:T(8,128)(2,1)S(1)}, bf16[4,72,384]{2,1,0:T(8,128)(2,1)S(1)}, u32[]{:S(2)}, u32[]{:S(2)}) collective-permute-start(bf16[4,72,384]{2,1,0:T(8,128)(2,1)S(1)} %get-tuple-element.55), channel_id=1, source_target_pairs={{0,1},{1,0},{2,3},{3,2},{4,5},{5,4},{6,7},{7,6},{8,9},{9,8},{10,11... | collective-permute-start | bytes 663560 | tf_op jit(solution)/shard_map/ppermute | solution.py:377
  11.5 3.1 %collective-permute-start.4 = (bf16[4,72,384]{2,1,0:T(8,128)(2,1)S(1)}, bf16[4,72,384]{2,1,0:T(8,128)(2,1)S(1)}, u32[]{:S(2)}, u32[]{:S(2)}) collective-permute-start(bf16[4,72,384]{2,1,0:T(8,128)(2,1)S(1)} %get-tuple-element.54), channel_id=1, source_target_pairs={{1,2},{2,1},{3,4},{4,3},{5,6},{6,5},{9,10},{10,9},{11,12},{12,11},... | collective-permute-start | bytes 663560 | tf_op jit(solution)/shard_map/ppermute | solution.py:381
  14.6 0.0 copy-done.4
  14.6 3.9 %shard_map.79 = (bf16[8,12,80,256]{3,2,1,0:T(8,128)(2,1)S(1)}, bf16[6,8,80,256]{3,2,1,0:T(8,128)(2,1)S(1)}, f32[6,8,80,256]{3,2,1,0:T(8,128)S(1)}) custom-call(bf16[72,640]{1,0:T(8,128)(2,1)S(1)} %get-tuple-element.28.refs_0_, bf16[72,640]{1,0:T(8,128)(2,1)S(1)} %collective-permute-done.refs_1_, bf16[72,640]{1,0:T(8,128)(2,1)S(1)} %collective-permute-done.1.refs_2_, ...), custom_call_target="tpu_custom_call" | custom-call | flops 6000000000 | tf_op jit(solution)/shard_map/pallas_call | solution.py:66
  18.5 0.0 collective-permute-done.5
  18.6 1.3 %collective-permute-start.6 = (bf16[2,72,768]{2,1,0:T(8,128)(2,1)S(1)}, bf16[2,72,768]{2,1,0:T(8,128)(2,1)S(1)}, u32[]{:S(2)}, u32[]{:S(2)}) collective-permute-start(bf16[2,72,768]{2,1,0:T(8,128)(2,1)S(1)} %pad_maximum_fusion.3), channel_id=1, source_target_pairs={{0,16},{8,24},{16,0},{24,8},{1,17},{9,25},{17,1},{25,9},{2,18},{10... | collective-permute-start | bytes 663560 | tf_op jit(solution)/shard_map/ppermute | solution.py:364
  19.9 0.0 collective-permute-done.3.refs_0_
  19.9 0.0 collective-permute-done.4.refs_1_
  19.9 7.0 %shard_map.80 = (bf16[8,12,80,256]{3,2,1,0:T(8,128)(2,1)S(1)}, bf16[6,8,80,256]{3,2,1,0:T(8,128)(2,1)S(1)}, f32[6,8,80,256]{3,2,1,0:T(8,128)S(1)}) custom-call(bf16[4,72,384]{2,1,0:T(8,128)(2,1)S(1)} %collective-permute-done.3.refs_0_, ...), custom_call_target="tpu_custom_call", output_to_operand_aliasing={{0}: (4, {}), {1}: (5, {}), {2}: (6, {})} | custom-call | flops 8000000000 | tf_op jit(solution)/shard_map/pallas_call | solution.py:66
  26.9 0.0 collective-permute-done.6
  26.9 1.7 %shard_map.83 = (f32[4,384,128]{2,1,0:T(8,128)S(1)}, bf16[4,72,384]{2,1,0:T(8,128)(2,1)S(1)}) custom-call(bf16[6,8,80,256]{3,2,1,0:T(8,128)(2,1)S(1)} %get-tuple-element.36.refs_0_, bf16[3,256,256]{2,1,0:T(8,128)(2,1)S(1)} %get-tuple-element.37.refs_1_.refs_5_.refs_3_, f32[1,128]{1,0:T(1,128)S(1)} %pad_bitcast_fusion.refs_2_, ...), custom_call_target="tpu_custom_call" | custom-call | flops 2000000000 | tf_op jit(solution)/shard_map/pallas_call | solution.py:66
  28.7 1.7 %shard_map.82 = (f32[4,384,128]{2,1,0:T(8,128)S(1)}, bf16[4,72,384]{2,1,0:T(8,128)(2,1)S(1)}) custom-call(bf16[6,8,80,256]{3,2,1,0:T(8,128)(2,1)S(1)} %get-tuple-element.36.refs_0_, bf16[3,256,256]{2,1,0:T(8,128)(2,1)S(1)} %get-tuple-element.37.refs_1_.refs_5_.refs_3_, f32[1,128]{1,0:T(1,128)S(1)} %pad_bitcast_fusion.refs_2_, ...), custom_call_target="tpu_custom_call" | custom-call | flops 2000000000 | tf_op jit(solution)/shard_map/pallas_call | solution.py:66
  30.5 0.1 collective-permute-start.8
  30.5 2.9 %collective-permute-start.9 = (bf16[4,72,384]{2,1,0:T(8,128)(2,1)S(1)}, bf16[4,72,384]{2,1,0:T(8,128)(2,1)S(1)}, u32[]{:S(2)}, u32[]{:S(2)}) collective-permute-start(bf16[4,72,384]{2,1,0:T(8,128)(2,1)S(1)} %get-tuple-element.42.refs_0_), channel_id=1, source_target_pairs={{1,2},{2,1},{3,4},{4,3},{5,6},{6,5},{9,10},{10,9},{11,12},{12,11},... | collective-permute-start | bytes 663560 | tf_op jit(solution)/shard_map/ppermute | solution.py:381
  33.5 2.0 %shard_map.84 = (bf16[8,8,80,256]{3,2,1,0:T(8,128)(2,1)S(1)}, bf16[6,12,80,256]{3,2,1,0:T(8,128)(2,1)S(1)}, f32[72,512]{1,0:T(8,128)S(1)}, bf16[72,512]{1,0:T(8,...) custom-call(bf16[4,72,384]{2,1,0:T(8,128)(2,1)S(1)} %get-tuple-element.42.refs_0_, ...), custom_call_target="tpu_custom_call" | custom-call | flops 2300000000 | tf_op jit(solution)/shard_map/pallas_call | solution.py:66
  35.4 0.1 collective-permute-start.7
  35.5 0.0 collective-permute-done.8.refs_0_
  35.5 2.3 %collective-permute-done.9.refs_1_ = bf16[4,72,384]{2,1,0:T(8,128)(2,1)S(1)} collective-permute-done((bf16[4,72,384]{2,1,0:T(8,128)(2,1)S(1)}, bf16[4,72,384]{2,1,0:T(8,128)(2,1)S(1)}, u32[]{:S(2)}, u32[]{:S(2)}) %collective-permute-start.9) | collective-permute-done | bytes 221216 | tf_op jit(solution)/shard_map/ppermute | solution.py:381
  37.9 2.6 %shard_map.85 = (bf16[8,8,80,256]{3,2,1,0:T(8,128)(2,1)S(1)}, bf16[6,12,80,256]{3,2,1,0:T(8,128)(2,1)S(1)}) custom-call(bf16[4,72,384]{2,1,0:T(8,128)(2,1)S(1)} %collective-permute-done.8.refs_0_, bf16[4,72,384]{2,1,0:T(8,128)(2,1)S(1)} %collective-permute-done.9.refs_1_, ...), custom_call_target="tpu_custom_call", output_to_operand_aliasing={{0}: (4, {}), {1}: (5, {})} | custom-call | flops 3000000000 | tf_op jit(solution)/shard_map/pallas_call | solution.py:66
  40.5 1.7 %shard_map.90 = bf16[72,512]{1,0:T(8,128)(2,1)S(1)} custom-call(bf16[6,12,80,256]{3,2,1,0:T(8,128)(2,1)S(1)} %get-tuple-element.51.refs_0_, bf16[15,256,256]{2,1,0:T(8,128)(2,1)S(1)} %get-tuple-element.32.refs_4_.refs_2_.refs_1_), custom_call_target="tpu_custom_call" | custom-call | flops 2000000000 | tf_op jit(solution)/shard_map/pallas_call | solution.py:66
  42.2 0.1 collective-permute-start.12
  42.3 1.7 %shard_map.87 = bf16[72,1024]{1,0:T(8,128)(2,1)S(1)} custom-call(bf16[6,12,80,256]{3,2,1,0:T(8,128)(2,1)S(1)} %get-tuple-element.51.refs_0_, bf16[15,256,256]{2,1,0:T(8,128)(2,1)S(1)} %get-tuple-element.32.refs_4_.refs_2_.refs_1_, bf16[72,512]{1,0:T(8,128)(2,1)S(1)} %get-tuple-element.53.refs_2_), custom_call_target="tpu_custom_call" | custom-call | flops 2000000000 | tf_op jit(solution)/shard_map/pallas_call | solution.py:66
  44.0 1.5 %collective-permute-start.11 = (bf16[72,1024]{1,0:T(8,128)(2,1)S(1)}, bf16[72,1024]{1,0:T(8,128)(2,1)S(1)}, u32[]{:S(2)}, u32[]{:S(2)}) collective-permute-start(bf16[72,1024]{1,0:T(8,128)(2,1)S(1)} %shard_map.87), channel_id=1, source_target_pairs={{0,24},{8,16},{16,8},{24,0},{1,25},{9,17},{17,9},{25,1},{2,26},{10... | collective-permute-start | bytes 442376 | tf_op jit(solution)/shard_map/ppermute | solution.py:364
  45.4 1.7 %shard_map.86 = bf16[72,1024]{1,0:T(8,128)(2,1)S(1)} custom-call(bf16[6,12,80,256]{3,2,1,0:T(8,128)(2,1)S(1)} %get-tuple-element.51.refs_0_, bf16[15,256,256]{2,1,0:T(8,128)(2,1)S(1)} %get-tuple-element.32.refs_4_.refs_2_.refs_1_, bf16[72,512]{1,0:T(8,128)(2,1)S(1)} %get-tuple-element.52.refs_2_), custom_call_target="tpu_custom_call" | custom-call | flops 2000000000 | tf_op jit(solution)/shard_map/pallas_call | solution.py:66
  47.1 1.2 %collective-permute-start.10 = (bf16[72,1024]{1,0:T(8,128)(2,1)S(1)}, bf16[72,1024]{1,0:T(8,128)(2,1)S(1)}, u32[]{:S(2)}, u32[]{:S(2)}) collective-permute-start(bf16[72,1024]{1,0:T(8,128)(2,1)S(1)} %shard_map.86), channel_id=1, source_target_pairs={{0,16},{8,24},{16,0},{24,8},{1,17},{9,25},{17,1},{25,9},{2,18},{10... | collective-permute-start | bytes 442376 | tf_op jit(solution)/shard_map/ppermute | solution.py:364
  48.3 1.7 %shard_map.89.refs_0_ = f32[72,512]{1,0:T(8,128)S(1)} custom-call(bf16[6,12,80,256]{3,2,1,0:T(8,128)(2,1)S(1)} %get-tuple-element.51.refs_0_, bf16[15,256,256]{2,1,0:T(8,128)(2,1)S(1)} %get-tuple-element.32.refs_4_.refs_2_.refs_1_), custom_call_target="tpu_custom_call" | custom-call | flops 2000000000 | tf_op jit(solution)/shard_map/pallas_call | solution.py:66
  50.0 0.0 collective-permute-done.12.refs_1_
  50.1 0.0 collective-permute-done.11.refs_3_
  50.1 3.4 %collective-permute-done.10.refs_2_ = bf16[72,1024]{1,0:T(8,128)(2,1)S(1)} collective-permute-done((bf16[72,1024]{1,0:T(8,128)(2,1)S(1)}, bf16[72,1024]{1,0:T(8,128)(2,1)S(1)}, u32[]{:S(2)}, u32[]{:S(2)}) %collective-permute-start.10) | collective-permute-done | bytes 147488 | tf_op jit(solution)/shard_map/ppermute | solution.py:364
  53.5 1.3 %shard_map.91 = f32[2,69,4,256]{3,2,1,0:T(4,128)} custom-call(f32[72,512]{1,0:T(8,128)S(1)} %shard_map.89.refs_0_, bf16[72,512]{1,0:T(8,128)(2,1)S(1)} %collective-permute-done.12.refs_1_, bf16[72,1024]{1,0:T(8,128)(2,1)S(1)} %collective-permute-done.10.refs_2_, bf16[72,1024]{1,0:T(8,128)(2,1)S(1)} %collective-permute-done.11.refs_3_), custom_call_target="tpu_custom_call" | custom-call | flops 1000000000 | tf_op jit(solution)/shard_map/pallas_call | solution.py:66
  54.8 0.0 collective-permute-done.7.refs_1_
  54.8 1.3 %shard_map.88 = f32[2,69,4,256]{3,2,1,0:T(4,128)} custom-call(f32[72,512]{1,0:T(8,128)S(1)} %get-tuple-element.47.refs_0_, bf16[72,512]{1,0:T(8,128)(2,1)S(1)} %collective-permute-done.7.refs_1_, bf16[72,1024]{1,0:T(8,128)(2,1)S(1)} %collective-permute-done.10.refs_2_, bf16[72,1024]{1,0:T(8,128)(2,1)S(1)} %collective-permute-done.11.refs_3_), custom_call_target="tpu_custom_call" | custom-call | flops 1000000000 | tf_op jit(solution)/shard_map/pallas_call | solution.py:66
  (9 shorter events, 0.1 us)
Async XLA Ops:
  0.6 1.1 %copy-start.1 = (f32[2,69,4,256]{3,2,1,0:T(4,128)S(1)}, f32[2,69,4,256]{3,2,1,0:T(4,128)}, u32[]{:S(2)}) copy-start(f32[2,69,4,256]{3,2,1,0:T(4,128)} %refs_0_.2) | copy-start | bytes 1695748
  1.7 3.2 %copy-start.2 = (f32[2,69,4,256]{3,2,1,0:T(4,128)S(1)}, f32[2,69,4,256]{3,2,1,0:T(4,128)}, u32[]{:S(2)}) copy-start(f32[2,69,4,256]{3,2,1,0:T(4,128)} %refs_0_.3) | copy-start | bytes 1695748
  2.1 5.3 %collective-permute-start = (bf16[72,640]{1,0:T(8,128)(2,1)S(1)}, bf16[72,640]{1,0:T(8,128)(2,1)S(1)}, u32[]{:S(2)}, u32[]{:S(2)}) collective-permute-start(bf16[72,640]{1,0:T(8,128)(2,1)S(1)} %get-tuple-element.29), channel_id=1, source_target_pairs={{0,8},{8,0},{16,24},{24,16},{1,9},{9,1},{17,25},{25,17},{2,10},{10... | collective-permute-start | bytes 276488 | tf_op jit(solution)/shard_map/ppermute | solution.py:364
  3.4 4.1 %collective-permute-start.1 = (bf16[72,640]{1,0:T(8,128)(2,1)S(1)}, bf16[72,640]{1,0:T(8,128)(2,1)S(1)}, u32[]{:S(2)}, u32[]{:S(2)}) collective-permute-start(bf16[72,640]{1,0:T(8,128)(2,1)S(1)} %get-tuple-element.30), channel_id=1, source_target_pairs={{0,16},{8,24},{16,0},{24,8},{1,17},{9,25},{17,1},{25,9},{2,18},{10... | collective-permute-start | bytes 276488 | tf_op jit(solution)/shard_map/ppermute | solution.py:364
  3.7 3.1 %copy-start = (bf16[3,3,256,345]{2,3,1,0:T(8,128)(2,1)S(1)}, bf16[3,3,256,345]{2,3,1,0:T(8,128)(2,1)}, u32[]{:S(2)}) copy-start(bf16[3,3,256,345]{2,3,1,0:T(8,128)(2,1)} %param.8) | copy-start | bytes 4769284
  3.7 3.1 %copy-start.3 = (bf16[3,3,69,256]{3,2,1,0:T(8,128)(2,1)S(1)}, bf16[3,3,69,256]{3,2,1,0:T(8,128)(2,1)}, u32[]{:S(2)}) copy-start(bf16[3,3,69,256]{3,2,1,0:T(8,128)(2,1)} %refs_1_.1) | copy-start | bytes 953860
  3.7 4.4 %collective-permute-start.2 = (bf16[72,640]{1,0:T(8,128)(2,1)S(1)}, bf16[72,640]{1,0:T(8,128)(2,1)S(1)}, u32[]{:S(2)}, u32[]{:S(2)}) collective-permute-start(bf16[72,640]{1,0:T(8,128)(2,1)S(1)} %get-tuple-element.31), channel_id=1, source_target_pairs={{0,24},{8,16},{16,8},{24,0},{1,25},{9,17},{17,9},{25,1},{2,26},{10... | collective-permute-start | bytes 276488 | tf_op jit(solution)/shard_map/ppermute | solution.py:364
  5.5 13.0 %collective-permute-start.5 = (bf16[2,72,768]{2,1,0:T(8,128)(2,1)S(1)}, bf16[2,72,768]{2,1,0:T(8,128)(2,1)S(1)}, u32[]{:S(2)}, u32[]{:S(2)}) collective-permute-start(bf16[2,72,768]{2,1,0:T(8,128)(2,1)S(1)} %pad_maximum_fusion.2), channel_id=1, source_target_pairs={{0,8},{8,0},{16,24},{24,16},{1,9},{9,1},{17,25},{25,17},{2,10},{10... | collective-permute-start | bytes 663560 | tf_op jit(solution)/shard_map/ppermute | solution.py:364
  6.8 0.7 %copy-start.5 = (f32[69]{0:T(128)S(1)}, f32[69]{0:T(128)}, u32[]{:S(2)}) copy-start(f32[69]{0:T(128)} %param.11) | copy-start | bytes 832
  6.8 7.8 %copy-start.4 = (f32[256]{0:T(256)S(1)}, f32[256]{0:T(256)}, u32[]{:S(2)}) copy-start(f32[256]{0:T(256)} %param.9) | copy-start | bytes 3076
  8.1 11.7 %collective-permute-start.3 = (bf16[4,72,384]{2,1,0:T(8,128)(2,1)S(1)}, bf16[4,72,384]{2,1,0:T(8,128)(2,1)S(1)}, u32[]{:S(2)}, u32[]{:S(2)}) collective-permute-start(bf16[4,72,384]{2,1,0:T(8,128)(2,1)S(1)} %get-tuple-element.55), channel_id=1, source_target_pairs={{0,1},{1,0},{2,3},{3,2},{4,5},{5,4},{6,7},{7,6},{8,9},{9,8},{10,11... | collective-permute-start | bytes 663560 | tf_op jit(solution)/shard_map/ppermute | solution.py:377
  11.5 8.4 %collective-permute-start.4 = (bf16[4,72,384]{2,1,0:T(8,128)(2,1)S(1)}, bf16[4,72,384]{2,1,0:T(8,128)(2,1)S(1)}, u32[]{:S(2)}, u32[]{:S(2)}) collective-permute-start(bf16[4,72,384]{2,1,0:T(8,128)(2,1)S(1)} %get-tuple-element.54), channel_id=1, source_target_pairs={{1,2},{2,1},{3,4},{4,3},{5,6},{6,5},{9,10},{10,9},{11,12},{12,11},... | collective-permute-start | bytes 663560 | tf_op jit(solution)/shard_map/ppermute | solution.py:381
  18.6 8.4 %collective-permute-start.6 = (bf16[2,72,768]{2,1,0:T(8,128)(2,1)S(1)}, bf16[2,72,768]{2,1,0:T(8,128)(2,1)S(1)}, u32[]{:S(2)}, u32[]{:S(2)}) collective-permute-start(bf16[2,72,768]{2,1,0:T(8,128)(2,1)S(1)} %pad_maximum_fusion.3), channel_id=1, source_target_pairs={{0,16},{8,24},{16,0},{24,8},{1,17},{9,25},{17,1},{25,9},{2,18},{10... | collective-permute-start | bytes 663560 | tf_op jit(solution)/shard_map/ppermute | solution.py:364
  30.5 5.1 %collective-permute-start.8 = (bf16[4,72,384]{2,1,0:T(8,128)(2,1)S(1)}, bf16[4,72,384]{2,1,0:T(8,128)(2,1)S(1)}, u32[]{:S(2)}, u32[]{:S(2)}) collective-permute-start(bf16[4,72,384]{2,1,0:T(8,128)(2,1)S(1)} %get-tuple-element.43.refs_1_), channel_id=1, source_target_pairs={{0,1},{1,0},{2,3},{3,2},{4,5},{5,4},{6,7},{7,6},{8,9},{9,8},{10,11... | collective-permute-start | bytes 663560 | tf_op jit(solution)/shard_map/ppermute | solution.py:377
  30.5 7.3 %collective-permute-start.9 = (bf16[4,72,384]{2,1,0:T(8,128)(2,1)S(1)}, bf16[4,72,384]{2,1,0:T(8,128)(2,1)S(1)}, u32[]{:S(2)}, u32[]{:S(2)}) collective-permute-start(bf16[4,72,384]{2,1,0:T(8,128)(2,1)S(1)} %get-tuple-element.42.refs_0_), channel_id=1, source_target_pairs={{1,2},{2,1},{3,4},{4,3},{5,6},{6,5},{9,10},{10,9},{11,12},{12,11},... | collective-permute-start | bytes 663560 | tf_op jit(solution)/shard_map/ppermute | solution.py:381
  35.4 19.3 %collective-permute-start.7 = (bf16[72,512]{1,0:T(8,128)(2,1)S(1)}, bf16[72,512]{1,0:T(8,128)(2,1)S(1)}, u32[]{:S(2)}, u32[]{:S(2)}) collective-permute-start(bf16[72,512]{1,0:T(8,128)(2,1)S(1)} %get-tuple-element.48), channel_id=1, source_target_pairs={{0,8},{8,0},{16,24},{24,16},{1,9},{9,1},{17,25},{25,17},{2,10},{10... | collective-permute-start | bytes 221192 | tf_op jit(solution)/shard_map/ppermute | solution.py:364
  42.2 7.9 %collective-permute-start.12 = (bf16[72,512]{1,0:T(8,128)(2,1)S(1)}, bf16[72,512]{1,0:T(8,128)(2,1)S(1)}, u32[]{:S(2)}, u32[]{:S(2)}) collective-permute-start(bf16[72,512]{1,0:T(8,128)(2,1)S(1)} %shard_map.90), channel_id=1, source_target_pairs={{0,8},{8,0},{16,24},{24,16},{1,9},{9,1},{17,25},{25,17},{2,10},{10... | collective-permute-start | bytes 221192 | tf_op jit(solution)/shard_map/ppermute | solution.py:364
  44.0 6.1 %collective-permute-start.11 = (bf16[72,1024]{1,0:T(8,128)(2,1)S(1)}, bf16[72,1024]{1,0:T(8,128)(2,1)S(1)}, u32[]{:S(2)}, u32[]{:S(2)}) collective-permute-start(bf16[72,1024]{1,0:T(8,128)(2,1)S(1)} %shard_map.87), channel_id=1, source_target_pairs={{0,24},{8,16},{16,8},{24,0},{1,25},{9,17},{17,9},{25,1},{2,26},{10... | collective-permute-start | bytes 442376 | tf_op jit(solution)/shard_map/ppermute | solution.py:364
  47.1 6.4 %collective-permute-start.10 = (bf16[72,1024]{1,0:T(8,128)(2,1)S(1)}, bf16[72,1024]{1,0:T(8,128)(2,1)S(1)}, u32[]{:S(2)}, u32[]{:S(2)}) collective-permute-start(bf16[72,1024]{1,0:T(8,128)(2,1)S(1)} %shard_map.86), channel_id=1, source_target_pairs={{0,16},{8,24},{16,0},{24,8},{1,17},{9,25},{17,1},{25,9},{2,18},{10... | collective-permute-start | bytes 442376 | tf_op jit(solution)/shard_map/ppermute | solution.py:364

commit v6 on v5

--- a/solution.py
+++ b/solution.py
@@ -62,12 +62,16 @@
     return [lax.axis_index("tm")] + [flag.astype(jnp.int32) for flag in flags]
 
 
-def call(kernel, outs, scratch, args, limit, microseconds, aliases={}):
+def call(kernel, outs, scratch, args, limit, microseconds, aliases={}, states=0, ins_by=False, outs_by=False):
+    def one(shape):
+        return pl.BlockSpec((1,) + tuple(shape[1:]), lambda t: (t,) + (0,) * (len(shape) - 1))
+
     return pl.pallas_call(
         lambda *refs: kernel(here(), *refs),
+        grid=(states,) if states else (),
         out_shape=outs,
-        in_specs=[VMEM] * len(args),
-        out_specs=[VMEM] * len(outs),
+        in_specs=[one(a.shape) if ins_by else VMEM for a in args],
+        out_specs=[one(a.shape) if outs_by else VMEM for a in outs],
         scratch_shapes=scratch,
         input_output_aliases=aliases,
         compiler_params=pltpu.CompilerParams(vmem_limit_bytes=limit),
@@ -81,11 +85,14 @@
 
 def split_kernel(p, place, coded, where, x_ref, *refs):
     outs, held = refs[: p.n], refs[p.n]
-    me = where[0]
-    held[...] = jnp.zeros_like(held)
-    for r in range(p.rows):
-        for t in range(p.local):
-            v = x_ref[t, :, r, :]
+
+    @pl.when(pl.program_id(0) == 0)
+    def _():
+        held[...] = jnp.zeros_like(held)
+
+    def place_state(t):
+        for r in range(p.rows):
+            v = x_ref[0, :, r, :]
             start = place(r, t)
             base, off = start // LANES * LANES, start % LANES
             width = LANES if off + p.wx <= LANES else 2 * LANES
@@ -95,9 +102,15 @@
                 y = pltpu.roll(v, (off + DEPTH - p.wc * q) % p.lon, 1)[:, :width]
                 old = held[q, : p.chans, base : base + width]
                 held[q, : p.chans, base : base + width] = jnp.where(inside, y, old)
-    for d in range(p.n):
-        block = held[me ^ d]
-        outs[d][...] = (jnp.exp(CODE * block) if coded else block).astype(BF16)
+
+    for t in range(p.local):
+        pl.when(pl.program_id(0) == t)(functools.partial(place_state, t))
+
+    @pl.when(pl.program_id(0) == p.local - 1)
+    def _():
+        for d in range(p.n):
+            block = held[where[0] ^ d]
+            outs[d][...] = (jnp.exp(CODE * block) if coded else block).astype(BF16)
 
 
 def weights_kernel(p, where, k_in, k_out, w_in, w_out, flat_ref, held):
@@ -118,20 +131,20 @@
 def to_columns(block, rows_ref):
     depth, width = block.shape
     for m in range(width // LANES):
-        tile = block[:, m * LANES : (m + 1) * LANES].astype(F32)
-        tile = jnp.concatenate([tile, jnp.zeros((LANES - depth, LANES), F32)], axis=0)
-        rows_ref[8 + m * LANES : 8 + (m + 1) * LANES, :] = tile.T
+        tile = block[:, m * LANES : (m + 1) * LANES]
+        tile = jnp.concatenate([tile, jnp.zeros((LANES - depth, LANES), BF16)], axis=0)
+        rows_ref[8 + m * LANES : 8 + (m + 1) * LANES, :] = tile.T.astype(F32)
 
 
 def taps_of(p, rows_ref, start, flip):
-    v = [rows_ref[8 + start + j : 8 + start + j + p.wp, :] for j in (-1, 0, 1)]
+    v = [rows_ref[8 + start + j : 8 + start + j + p.wp, :].astype(BF16) for j in (-1, 0, 1)]
     if flip:
         v = v[::-1]
     lane = lanes_of((p.wp, LANES))
     middle = pltpu.roll(v[1], p.chans, 1)
     low = jnp.where(lane < p.chans, v[0], middle)
     high = jnp.where(lane < 2 * p.chans - LANES, middle, pltpu.roll(v[2], 2 * p.chans - LANES, 1))
-    return jnp.concatenate([low, high], axis=1).astype(BF16)
+    return jnp.concatenate([low, high], axis=1)
 
 
 def spread(p, total, parts):
@@ -153,9 +166,9 @@
 
 def fill_own(p, where, blocks, rows_ref, taps_ref, flip, base):
     me = where[0]
-    for d in range(p.n):
+    for d, block in blocks.items():
         t0 = (me ^ d) * p.local + base
-        to_columns(blocks[d][...], rows_ref)
+        to_columns(block[...], rows_ref)
         for r in range(p.rows):
             for t in range(p.local):
                 taps_ref[REACH + r, t0 + t] = taps_of(p, rows_ref, p.at(r, t), flip)
@@ -222,10 +235,13 @@
     lax.fori_loop(0, count, body, 0)
 
 
-def inner_kernel(p, where, *refs):
-    blocks, w_in, bias_in = refs[: p.n], refs[p.n], refs[p.n + 1]
-    taps_ref, act_ref, slope_ref, rows_ref = refs[p.n + 2 :]
-    fill_own(p, where, blocks, rows_ref, taps_ref, False, p.side)
+def early_kernel(p, where, *refs):
+    blocks, taps_ref, rows_ref = refs[: p.n - 1], refs[p.n - 1], refs[p.n]
+    fill_own(p, where, dict(enumerate(blocks)), rows_ref, taps_ref, False, p.side)
+
+
+def inner_kernel(p, where, block, w_in, bias_in, _taps, taps_ref, act_ref, slope_ref, rows_ref):
+    fill_own(p, where, {p.n - 1: block}, rows_ref, taps_ref, False, p.side)
     wrap(p, taps_ref, REACH, p.rows)
     hidden_rows(p, where, taps_ref, w_in, bias_in, act_ref, slope_ref, p.rows - 2, lambda s: s + REACH)
 
@@ -339,25 +355,35 @@
 
 
 def join_kernel(p, begins, where, *refs):
-    ins, out_ref, held = refs[: p.n], refs[p.n], refs[p.n + 1]
-    me = where[0]
-    for d in range(p.n):
-        held[me ^ d] = ins[d][:, begins[d] : begins[d] + p.out].astype(F32)
+    fields = len(begins)
+    ins, outs, held = refs[: p.n * fields], refs[p.n * fields : -1], refs[-1]
     per = LANES // p.wc
     lane = lanes_of((p.chans, LANES))
-    for r in range(p.rows):
-        for t in range(p.local):
-            start = (r * p.local + t) * p.wc
-            base, off = start // LANES * LANES, start % LANES
-            for m in range(p.lon // LANES):
-                tile = None
-                for u in range(per):
-                    piece = held[m * per + u, : p.chans, base : base + LANES]
-                    step = (u * p.wc - off) % LANES
-                    if step:
-                        piece = pltpu.roll(piece, step, 1)
-                    tile = piece if tile is None else jnp.where(lane < u * p.wc, tile, piece)
-                out_ref[t, :, r, m * LANES : (m + 1) * LANES] = tile
+
+    @pl.when(pl.program_id(0) == 0)
+    def _():
+        for f in range(fields):
+            for d in range(p.n):
+                block = ins[f * p.n + d][:, begins[f][d] : begins[f][d] + p.out]
+                held[f, where[0] ^ d] = block.astype(F32)
+
+    def join_state(t):
+        for f in range(fields):
+            for r in range(p.rows):
+                start = (r * p.local + t) * p.wc
+                base, off = start // LANES * LANES, start % LANES
+                for m in range(p.lon // LANES):
+                    tile = None
+                    for u in range(per):
+                        piece = held[f, m * per + u, : p.chans, base : base + LANES]
+                        step = (u * p.wc - off) % LANES
+                        if step:
+                            piece = pltpu.roll(piece, step, 1)
+                        tile = piece if tile is None else jnp.where(lane < u * p.wc, tile, piece)
+                    outs[f][0, :, r, m * LANES : (m + 1) * LANES] = tile
+
+    for t in range(p.local):
+        pl.when(pl.program_id(0) == t)(functools.partial(join_state, t))
 
 
 def send_tm(p, value, d):
@@ -392,10 +418,14 @@
     def split(field, place, coded, width):
         shape = [sds((p.cp, width), BF16)] * n
         held = [scratch((n, p.cp, width), F32)]
-        return call(kernel(split_kernel, p, place, coded), shape, held, [field], 8 << 20, 1.5)
+        return call(
+            kernel(split_kernel, p, place, coded), shape, held, [field], 8 << 20, 1.5, states=p.local, ins_by=True
+        )
 
     mine = split(states, p.at, False, p.posp)
-    blocks = [mine[0]] + [send_tm(p, mine[d], d) for d in range(1, n)]
+    blocks = [mine[0]]
+    for d in range(1, n):
+        blocks.append(send_tm(p, mine[d], d))
     w_in, w_out = call(
         kernel(weights_kernel, p),
         [sds((p.taps * p.window, p.packed, p.hidden), BF16), sds((p.taps, p.packed, p.hidden), BF16)],
@@ -419,9 +449,10 @@
     taps_shape = sds((deep, around, p.wp, p.packed), BF16)
     act_shape = sds((p.rows + 2, p.total, p.wp, p.hidden), BF16)
     slope_shape = sds((p.rows + 2, p.total, p.wp, p.hidden), F32)
+    taps = call(kernel(early_kernel, p), [taps_shape], [columns], blocks[:-1], 16 << 20, 1)[0]
     inner = call(
         kernel(inner_kernel, p), [taps_shape, act_shape, slope_shape], [columns],
-        [*blocks, w_in, b_in], 24 << 20, 6,
+        [blocks[-1], w_in, b_in, taps], 24 << 20, 5, {3: 0},
     )
     for bit in stages[1:]:
         goals = relay_tm(p, goals, bit)
@@ -470,13 +501,15 @@
         if d:
             parts[d] = send_tm(p, parts[d], d)
 
-    def join(blocks, begins):
-        shape = [sds((p.local, p.chans, p.rows, p.lon), F32)]
-        held = [scratch((n, p.cp, p.out), F32)]
-        return call(kernel(join_kernel, p, begins), shape, held, [*blocks], 8 << 20, 1)[0]
-
-    begins = [0, 0] + [p.out] * (n - 2)
-    return join(scores[:2] + parts[2:], begins), join(parts, [0] * n)
+    begins = [[0, 0] + [p.out] * (n - 2), [0] * n]
+    shape = [sds((p.local, p.chans, p.rows, p.lon), F32)] * 2
+    held = [scratch((2, n, p.cp, p.out), F32)]
+    return tuple(
+        call(
+            kernel(join_kernel, p, begins), shape, held, scores[:2] + parts[2:] + parts, 16 << 20, 1.5,
+            states=p.local, outs_by=True,
+        )
+    )
 
 
 def solution(mesh):

time: 56.8 us -> 56.3 us (level)
  the two profiles are of different devices: /device:TPU:21 before, /device:TPU:11 now
where the time goes in v6:
time: 56.3 us; the launch traced here: 56.1 us
  Pallas kernels  28.9 us (51%)
  starting transfers between devices  17.2 us (31%)
  waiting for transfers between devices  7.77 us (14%)
  local copies, waits for them, and re-layouts  1.22 us (2%)
  between operations  0.88 us (2%)
    pallas_call x15, Pallas kernels, call(): pl.pallas_call(lambda *refs: kernel(here(), *refs), grid=(states,) if sta...  28.9 us
    ppermute x9, starting transfers between devices, send_tm(): return lax.ppermute(value, 'tm', [(i, i ^ d) for i in range(p.n)])  7.86 us
    ppermute x9, waiting for transfers between devices, send_tm(): return lax.ppermute(value, 'tm', [(i, i ^ d) for i in range(p.n)])  7.2 us
    ppermute x2, starting transfers between devices, send_far(): lax.ppermute(value, 'lat', [(i, (i + 1 ^ 1) - 1) for i in range(1, p.m -...  6.61 us
    ppermute x2, starting transfers between devices, send_near(): return lax.ppermute(value, 'lat', [(i, i ^ 1) for i in range(p.m)])  2.75 us
    unnamed x12, local copies, waits for them, and re-layouts  1.14 us
  transfers between devices with their start and end apart: 13, of which 4 were waited for; matrix products, arithmetic and copies ran while one was open for 0% of the time, Pallas kernels for 41%

profile of v6, /device:TPU:11, one launch (start us, length us, event | category | flops | bytes accessed | tf_op | source)
XLA Modules:
  0.0 56.1 jit_solution(17312583723434112927)
XLA Ops:
  0.6 0.0 copy-start.1
  0.6 1.0 %copy-done.1 = f32[2,69,4,256]{3,2,1,0:T(4,128)S(1)} copy-done((f32[2,69,4,256]{3,2,1,0:T(4,128)S(1)}, f32[2,69,4,256]{3,2,1,0:T(4,128)}, u32[]{:S(2)}) %copy-start.1) | copy-done | bytes 565272
  1.7 0.0 copy-start.2
  1.7 0.6 %shard_map.77 = (bf16[72,640]{1,0:T(8,128)(2,1)S(1)}, bf16[72,640]{1,0:T(8,128)(2,1)S(1)}, bf16[72,640]{1,0:T(8,128)(2,1)S(1)}, bf16[72,640]{1,0:T(8,128)(2,1)S(1)}) custom-call(f32[2,69,4,256]{3,2,1,0:T(4,128)S(1)} %copy-done.1), custom_call_target="tpu_custom_call" | custom-call | flops 1500000000 | tf_op jit(solution)/shard_map/pallas_call | solution.py:69
  2.3 0.3 collective-permute-start
  2.6 1.2 %collective-permute-start.1 = (bf16[72,640]{1,0:T(8,128)(2,1)S(1)}, bf16[72,640]{1,0:T(8,128)(2,1)S(1)}, u32[]{:S(2)}, u32[]{:S(2)}) collective-permute-start(bf16[72,640]{1,0:T(8,128)(2,1)S(1)} %get-tuple-element.30), channel_id=1, source_target_pairs={{0,16},{8,24},{16,0},{24,8},{1,17},{9,25},{17,1},{25,9},{2,18},{10... | collective-permute-start | bytes 276488 | tf_op jit(solution)/shard_map/ppermute | solution.py:390
  3.8 0.0 copy-start
  3.8 0.0 copy-start.3
  3.8 1.2 %collective-permute-start.2 = (bf16[72,640]{1,0:T(8,128)(2,1)S(1)}, bf16[72,640]{1,0:T(8,128)(2,1)S(1)}, u32[]{:S(2)}, u32[]{:S(2)}) collective-permute-start(bf16[72,640]{1,0:T(8,128)(2,1)S(1)} %get-tuple-element.31), channel_id=1, source_target_pairs={{0,24},{8,16},{16,8},{24,0},{1,25},{9,17},{17,9},{25,1},{2,26},{10... | collective-permute-start | bytes 276488 | tf_op jit(solution)/shard_map/ppermute | solution.py:390
  5.0 0.0 copy-done.2
  5.0 0.7 %shard_map.82 = (bf16[72,768]{1,0:T(8,128)(2,1)S(1)}, bf16[72,768]{1,0:T(8,128)(2,1)S(1)}, bf16[72,768]{1,0:T(8,128)(2,1)S(1)}, bf16[72,768]{1,0:T(8,128)(2,1)S(1)}) custom-call(f32[2,69,4,256]{3,2,1,0:T(4,128)S(1)} %copy-done.2), custom_call_target="tpu_custom_call" | custom-call | flops 1500000000 | tf_op jit(solution)/shard_map/pallas_call | solution.py:69
  5.7 0.3 collective-permute-start.5
  6.0 0.0 copy-done
  6.1 0.0 copy-done.3
  6.1 0.0 copy-start.5
  6.1 0.6 %shard_map.78 = (bf16[15,256,256]{2,1,0:T(8,128)(2,1)S(1)}, bf16[3,256,256]{2,1,0:T(8,128)(2,1)S(1)}) custom-call(bf16[3,3,345,256]{3,2,1,0:T(8,128)(2,1)S(1)} %bitcast.32, bf16[3,3,69,256]{3,2,1,0:T(8,128)(2,1)S(1)} %copy-done.3), custom_call_target="tpu_custom_call" | custom-call | flops 2000000000 | tf_op jit(solution)/shard_map/pallas_call | solution.py:69
  6.7 0.1 copy-done.5
  6.7 0.0 copy-start.4
  6.7 0.0 collective-permute-done.refs_1_
  6.8 0.0 collective-permute-done.1.refs_2_
  6.8 2.0 %collective-permute-done.2.refs_0_ = bf16[72,640]{1,0:T(8,128)(2,1)S(1)} collective-permute-done((bf16[72,640]{1,0:T(8,128)(2,1)S(1)}, bf16[72,640]{1,0:T(8,128)(2,1)S(1)}, u32[]{:S(2)}, u32[]{:S(2)}) %collective-permute-start.2) | collective-permute-done | bytes 92192 | tf_op jit(solution)/shard_map/ppermute | solution.py:390
  8.8 0.1 broadcast_select_fusion
  8.9 2.4 %collective-permute-start.3 = (bf16[4,72,384]{2,1,0:T(8,128)(2,1)S(1)}, bf16[4,72,384]{2,1,0:T(8,128)(2,1)S(1)}, u32[]{:S(2)}, u32[]{:S(2)}) collective-permute-start(bf16[4,72,384]{2,1,0:T(8,128)(2,1)S(1)} %get-tuple-element.55), channel_id=1, source_target_pairs={{0,1},{1,0},{2,3},{3,2},{4,5},{5,4},{6,7},{7,6},{8,9},{9,8},{10,11... | collective-permute-start | bytes 663560 | tf_op jit(solution)/shard_map/ppermute | solution.py:403
  11.3 3.1 %collective-permute-start.4 = (bf16[4,72,384]{2,1,0:T(8,128)(2,1)S(1)}, bf16[4,72,384]{2,1,0:T(8,128)(2,1)S(1)}, u32[]{:S(2)}, u32[]{:S(2)}) collective-permute-start(bf16[4,72,384]{2,1,0:T(8,128)(2,1)S(1)} %get-tuple-element.54), channel_id=1, source_target_pairs={{1,2},{2,1},{3,4},{4,3},{5,6},{6,5},{9,10},{10,9},{11,12},{12,11},... | collective-permute-start | bytes 663560 | tf_op jit(solution)/shard_map/ppermute | solution.py:407
  14.5 0.5 shard_map.79.refs_3_
  15.0 0.0 copy-done.4
  15.0 3.4 %shard_map.80 = (bf16[8,12,80,256]{3,2,1,0:T(8,128)(2,1)S(1)}, bf16[6,8,80,256]{3,2,1,0:T(8,128)(2,1)S(1)}, f32[6,8,80,256]{3,2,1,0:T(8,128)S(1)}) custom-call(bf16[72,640]{1,0:T(8,128)(2,1)S(1)} %collective-permute-done.2.refs_0_, bf16[15,256,256]{2,1,0:T(8,128)(2,1)S(1)} %get-tuple-element.32.refs_1_.refs_2_, ...), custom_call_target="tpu_custom_call", output_to_operand_aliasing={{0}: (3, {})} | custom-call | flops 5000000000 | tf_op jit(solution)/shard_map/pallas_call | solution.py:69
  18.3 0.0 collective-permute-done.5
  18.4 0.3 collective-permute-start.6
  18.7 0.0 collective-permute-done.3.refs_0_
  18.7 0.0 collective-permute-done.4.refs_1_
  18.7 7.0 %shard_map.81 = (bf16[8,12,80,256]{3,2,1,0:T(8,128)(2,1)S(1)}, bf16[6,8,80,256]{3,2,1,0:T(8,128)(2,1)S(1)}, f32[6,8,80,256]{3,2,1,0:T(8,128)S(1)}) custom-call(bf16[4,72,384]{2,1,0:T(8,128)(2,1)S(1)} %collective-permute-done.3.refs_0_, ...), custom_call_target="tpu_custom_call", output_to_operand_aliasing={{0}: (4, {}), {1}: (5, {}), {2}: (6, {})} | custom-call | flops 8000000000 | tf_op jit(solution)/shard_map/pallas_call | solution.py:69
  25.7 0.0 collective-permute-done.6
  25.7 1.8 %shard_map.84 = (f32[4,384,128]{2,1,0:T(8,128)S(1)}, bf16[4,72,384]{2,1,0:T(8,128)(2,1)S(1)}) custom-call(bf16[6,8,80,256]{3,2,1,0:T(8,128)(2,1)S(1)} %get-tuple-element.36.refs_0_, bf16[3,256,256]{2,1,0:T(8,128)(2,1)S(1)} %get-tuple-element.37.refs_1_.refs_5_.refs_3_, f32[1,128]{1,0:T(1,128)S(1)} %pad_bitcast_fusion.refs_2_, ...), custom_call_target="tpu_custom_call" | custom-call | flops 2000000000 | tf_op jit(solution)/shard_map/pallas_call | solution.py:69
  27.5 1.8 %shard_map.83 = (f32[4,384,128]{2,1,0:T(8,128)S(1)}, bf16[4,72,384]{2,1,0:T(8,128)(2,1)S(1)}) custom-call(bf16[6,8,80,256]{3,2,1,0:T(8,128)(2,1)S(1)} %get-tuple-element.36.refs_0_, bf16[3,256,256]{2,1,0:T(8,128)(2,1)S(1)} %get-tuple-element.37.refs_1_.refs_5_.refs_3_, f32[1,128]{1,0:T(1,128)S(1)} %pad_bitcast_fusion.refs_2_, ...), custom_call_target="tpu_custom_call" | custom-call | flops 2000000000 | tf_op jit(solution)/shard_map/pallas_call | solution.py:69
  29.2 0.3 collective-permute-start.8
  29.6 3.5 %collective-permute-start.9 = (bf16[4,72,384]{2,1,0:T(8,128)(2,1)S(1)}, bf16[4,72,384]{2,1,0:T(8,128)(2,1)S(1)}, u32[]{:S(2)}, u32[]{:S(2)}) collective-permute-start(bf16[4,72,384]{2,1,0:T(8,128)(2,1)S(1)} %get-tuple-element.42.refs_0_), channel_id=1, source_target_pairs={{1,2},{2,1},{3,4},{4,3},{5,6},{6,5},{9,10},{10,9},{11,12},{12,11},... | collective-permute-start | bytes 663560 | tf_op jit(solution)/shard_map/ppermute | solution.py:407
  33.1 1.8 %shard_map.85 = (bf16[8,8,80,256]{3,2,1,0:T(8,128)(2,1)S(1)}, bf16[6,12,80,256]{3,2,1,0:T(8,128)(2,1)S(1)}, f32[72,512]{1,0:T(8,128)S(1)}, bf16[72,512]{1,0:T(8,...) custom-call(bf16[4,72,384]{2,1,0:T(8,128)(2,1)S(1)} %get-tuple-element.42.refs_0_, ...), custom_call_target="tpu_custom_call" | custom-call | flops 2300000000 | tf_op jit(solution)/shard_map/pallas_call | solution.py:69
  34.9 1.6 %collective-permute-start.7 = (bf16[72,512]{1,0:T(8,128)(2,1)S(1)}, bf16[72,512]{1,0:T(8,128)(2,1)S(1)}, u32[]{:S(2)}, u32[]{:S(2)}) collective-permute-start(bf16[72,512]{1,0:T(8,128)(2,1)S(1)} %get-tuple-element.48), channel_id=1, source_target_pairs={{0,8},{8,0},{16,24},{24,16},{1,9},{9,1},{17,25},{25,17},{2,10},{10... | collective-permute-start | bytes 221192 | tf_op jit(solution)/shard_map/ppermute | solution.py:390
  36.5 0.0 collective-permute-done.8.refs_0_
  36.5 0.6 %collective-permute-done.9.refs_1_ = bf16[4,72,384]{2,1,0:T(8,128)(2,1)S(1)} collective-permute-done((bf16[4,72,384]{2,1,0:T(8,128)(2,1)S(1)}, bf16[4,72,384]{2,1,0:T(8,128)(2,1)S(1)}, u32[]{:S(2)}, u32[]{:S(2)}) %collective-permute-start.9) | collective-permute-done | bytes 221216 | tf_op jit(solution)/shard_map/ppermute | solution.py:407
  37.1 2.5 %shard_map.86 = (bf16[8,8,80,256]{3,2,1,0:T(8,128)(2,1)S(1)}, bf16[6,12,80,256]{3,2,1,0:T(8,128)(2,1)S(1)}) custom-call(bf16[4,72,384]{2,1,0:T(8,128)(2,1)S(1)} %collective-permute-done.8.refs_0_, bf16[4,72,384]{2,1,0:T(8,128)(2,1)S(1)} %collective-permute-done.9.refs_1_, ...), custom_call_target="tpu_custom_call", output_to_operand_aliasing={{0}: (4, {}), {1}: (5, {})} | custom-call | flops 3000000000 | tf_op jit(solution)/shard_map/pallas_call | solution.py:69
  39.6 1.7 %shard_map.90 = bf16[72,512]{1,0:T(8,128)(2,1)S(1)} custom-call(bf16[6,12,80,256]{3,2,1,0:T(8,128)(2,1)S(1)} %get-tuple-element.51.refs_0_, bf16[15,256,256]{2,1,0:T(8,128)(2,1)S(1)} %get-tuple-element.32.refs_1_.refs_2_), custom_call_target="tpu_custom_call" | custom-call | flops 2000000000 | tf_op jit(solution)/shard_map/pallas_call | solution.py:69
  41.3 1.6 %collective-permute-start.12 = (bf16[72,512]{1,0:T(8,128)(2,1)S(1)}, bf16[72,512]{1,0:T(8,128)(2,1)S(1)}, u32[]{:S(2)}, u32[]{:S(2)}) collective-permute-start(bf16[72,512]{1,0:T(8,128)(2,1)S(1)} %shard_map.90), channel_id=1, source_target_pairs={{0,8},{8,0},{16,24},{24,16},{1,9},{9,1},{17,25},{25,17},{2,10},{10... | collective-permute-start | bytes 221192 | tf_op jit(solution)/shard_map/ppermute | solution.py:390
  42.9 1.7 %shard_map.88 = bf16[72,1024]{1,0:T(8,128)(2,1)S(1)} custom-call(bf16[6,12,80,256]{3,2,1,0:T(8,128)(2,1)S(1)} %get-tuple-element.51.refs_0_, bf16[15,256,256]{2,1,0:T(8,128)(2,1)S(1)} %get-tuple-element.32.refs_1_.refs_2_, bf16[72,512]{1,0:T(8,128)(2,1)S(1)} %get-tuple-element.53.refs_2_), custom_call_target="tpu_custom_call" | custom-call | flops 2000000000 | tf_op jit(solution)/shard_map/pallas_call | solution.py:69
  44.5 0.6 %collective-permute-start.11 = (bf16[72,1024]{1,0:T(8,128)(2,1)S(1)}, bf16[72,1024]{1,0:T(8,128)(2,1)S(1)}, u32[]{:S(2)}, u32[]{:S(2)}) collective-permute-start(bf16[72,1024]{1,0:T(8,128)(2,1)S(1)} %shard_map.88), channel_id=1, source_target_pairs={{0,24},{8,16},{16,8},{24,0},{1,25},{9,17},{17,9},{25,1},{2,26},{10... | collective-permute-start | bytes 442376 | tf_op jit(solution)/shard_map/ppermute | solution.py:390
  45.1 1.7 %shard_map.87 = bf16[72,1024]{1,0:T(8,128)(2,1)S(1)} custom-call(bf16[6,12,80,256]{3,2,1,0:T(8,128)(2,1)S(1)} %get-tuple-element.51.refs_0_, bf16[15,256,256]{2,1,0:T(8,128)(2,1)S(1)} %get-tuple-element.32.refs_1_.refs_2_, bf16[72,512]{1,0:T(8,128)(2,1)S(1)} %get-tuple-element.52.refs_2_), custom_call_target="tpu_custom_call" | custom-call | flops 2000000000 | tf_op jit(solution)/shard_map/pallas_call | solution.py:69
  46.8 0.7 %collective-permute-start.10 = (bf16[72,1024]{1,0:T(8,128)(2,1)S(1)}, bf16[72,1024]{1,0:T(8,128)(2,1)S(1)}, u32[]{:S(2)}, u32[]{:S(2)}) collective-permute-start(bf16[72,1024]{1,0:T(8,128)(2,1)S(1)} %shard_map.87), channel_id=1, source_target_pairs={{0,16},{8,24},{16,0},{24,8},{1,17},{9,25},{17,1},{25,9},{2,18},{10... | collective-permute-start | bytes 442376 | tf_op jit(solution)/shard_map/ppermute | solution.py:390
  47.5 1.7 %shard_map.89.refs_4_ = f32[72,512]{1,0:T(8,128)S(1)} custom-call(bf16[6,12,80,256]{3,2,1,0:T(8,128)(2,1)S(1)} %get-tuple-element.51.refs_0_, bf16[15,256,256]{2,1,0:T(8,128)(2,1)S(1)} %get-tuple-element.32.refs_1_.refs_2_), custom_call_target="tpu_custom_call" | custom-call | flops 2000000000 | tf_op jit(solution)/shard_map/pallas_call | solution.py:69
  49.2 0.0 collective-permute-done.7.refs_1_
  49.2 0.0 collective-permute-done.12.refs_5_
  49.3 1.4 %collective-permute-done.11.refs_3_.refs_7_ = bf16[72,1024]{1,0:T(8,128)(2,1)S(1)} collective-permute-done((bf16[72,1024]{1,0:T(8,128)(2,1)S(1)}, bf16[72,1024]{1,0:T(8,128)(2,1)S(1)}, u32[]{:S(2)}, u32[]{:S(2)}) %collective-permute-start.11) | collective-permute-done | bytes 147488 | tf_op jit(solution)/shard_map/ppermute | solution.py:390
  50.7 3.8 %collective-permute-done.10.refs_2_.refs_6_ = bf16[72,1024]{1,0:T(8,128)(2,1)S(1)} collective-permute-done((bf16[72,1024]{1,0:T(8,128)(2,1)S(1)}, bf16[72,1024]{1,0:T(8,128)(2,1)S(1)}, u32[]{:S(2)}, u32[]{:S(2)}) %collective-permute-start.10) | collective-permute-done | bytes 147488 | tf_op jit(solution)/shard_map/ppermute | solution.py:390
  54.4 1.7 %shard_map.91 = (f32[2,69,4,256]{3,2,1,0:T(4,128)}, f32[2,69,4,256]{3,2,1,0:T(4,128)}) custom-call(f32[72,512]{1,0:T(8,128)S(1)} %get-tuple-element.47.refs_0_, bf16[72,512]{1,0:T(8,128)(2,1)S(1)} %collective-permute-done.7.refs_1_, bf16[72,1024]{1,0:T(8,128)(2,1)S(1)} %collective-permute-done.10.refs_2_.refs_6_, ...), custom_call_target="tpu_custom_call" | custom-call | flops 1500000000 | tf_op jit(solution)/shard_map/pallas_call | solution.py:69
  (9 shorter events, 0.1 us)
Async XLA Ops:
  0.6 1.1 %copy-start.1 = (f32[2,69,4,256]{3,2,1,0:T(4,128)S(1)}, f32[2,69,4,256]{3,2,1,0:T(4,128)}, u32[]{:S(2)}) copy-start(f32[2,69,4,256]{3,2,1,0:T(4,128)} %refs_0_.2) | copy-start | bytes 1695748
  1.7 3.3 %copy-start.2 = (f32[2,69,4,256]{3,2,1,0:T(4,128)S(1)}, f32[2,69,4,256]{3,2,1,0:T(4,128)}, u32[]{:S(2)}) copy-start(f32[2,69,4,256]{3,2,1,0:T(4,128)} %refs_0_.3) | copy-start | bytes 1695748
  2.3 4.5 %collective-permute-start = (bf16[72,640]{1,0:T(8,128)(2,1)S(1)}, bf16[72,640]{1,0:T(8,128)(2,1)S(1)}, u32[]{:S(2)}, u32[]{:S(2)}) collective-permute-start(bf16[72,640]{1,0:T(8,128)(2,1)S(1)} %get-tuple-element.29), channel_id=1, source_target_pairs={{0,8},{8,0},{16,24},{24,16},{1,9},{9,1},{17,25},{25,17},{2,10},{10... | collective-permute-start | bytes 276488 | tf_op jit(solution)/shard_map/ppermute | solution.py:390
  2.6 4.2 %collective-permute-start.1 = (bf16[72,640]{1,0:T(8,128)(2,1)S(1)}, bf16[72,640]{1,0:T(8,128)(2,1)S(1)}, u32[]{:S(2)}, u32[]{:S(2)}) collective-permute-start(bf16[72,640]{1,0:T(8,128)(2,1)S(1)} %get-tuple-element.30), channel_id=1, source_target_pairs={{0,16},{8,24},{16,0},{24,8},{1,17},{9,25},{17,1},{25,9},{2,18},{10... | collective-permute-start | bytes 276488 | tf_op jit(solution)/shard_map/ppermute | solution.py:390
  3.8 2.2 %copy-start = (bf16[3,3,256,345]{2,3,1,0:T(8,128)(2,1)S(1)}, bf16[3,3,256,345]{2,3,1,0:T(8,128)(2,1)}, u32[]{:S(2)}) copy-start(bf16[3,3,256,345]{2,3,1,0:T(8,128)(2,1)} %param.8) | copy-start | bytes 4769284
  3.8 2.2 %copy-start.3 = (bf16[3,3,69,256]{3,2,1,0:T(8,128)(2,1)S(1)}, bf16[3,3,69,256]{3,2,1,0:T(8,128)(2,1)}, u32[]{:S(2)}) copy-start(bf16[3,3,69,256]{3,2,1,0:T(8,128)(2,1)} %refs_1_.1) | copy-start | bytes 953860
  3.8 5.0 %collective-permute-start.2 = (bf16[72,640]{1,0:T(8,128)(2,1)S(1)}, bf16[72,640]{1,0:T(8,128)(2,1)S(1)}, u32[]{:S(2)}, u32[]{:S(2)}) collective-permute-start(bf16[72,640]{1,0:T(8,128)(2,1)S(1)} %get-tuple-element.31), channel_id=1, source_target_pairs={{0,24},{8,16},{16,8},{24,0},{1,25},{9,17},{17,9},{25,1},{2,26},{10... | collective-permute-start | bytes 276488 | tf_op jit(solution)/shard_map/ppermute | solution.py:390
  5.7 12.6 %collective-permute-start.5 = (bf16[2,72,768]{2,1,0:T(8,128)(2,1)S(1)}, bf16[2,72,768]{2,1,0:T(8,128)(2,1)S(1)}, u32[]{:S(2)}, u32[]{:S(2)}) collective-permute-start(bf16[2,72,768]{2,1,0:T(8,128)(2,1)S(1)} %pad_maximum_fusion.2), channel_id=1, source_target_pairs={{0,8},{8,0},{16,24},{24,16},{1,9},{9,1},{17,25},{25,17},{2,10},{10... | collective-permute-start | bytes 663560 | tf_op jit(solution)/shard_map/ppermute | solution.py:390
  6.1 0.7 %copy-start.5 = (f32[69]{0:T(128)S(1)}, f32[69]{0:T(128)}, u32[]{:S(2)}) copy-start(f32[69]{0:T(128)} %param.11) | copy-start | bytes 832
  6.7 8.2 %copy-start.4 = (f32[256]{0:T(256)S(1)}, f32[256]{0:T(256)}, u32[]{:S(2)}) copy-start(f32[256]{0:T(256)} %param.9) | copy-start | bytes 3076
  8.9 9.8 %collective-permute-start.3 = (bf16[4,72,384]{2,1,0:T(8,128)(2,1)S(1)}, bf16[4,72,384]{2,1,0:T(8,128)(2,1)S(1)}, u32[]{:S(2)}, u32[]{:S(2)}) collective-permute-start(bf16[4,72,384]{2,1,0:T(8,128)(2,1)S(1)} %get-tuple-element.55), channel_id=1, source_target_pairs={{0,1},{1,0},{2,3},{3,2},{4,5},{5,4},{6,7},{7,6},{8,9},{9,8},{10,11... | collective-permute-start | bytes 663560 | tf_op jit(solution)/shard_map/ppermute | solution.py:403
  11.3 7.4 %collective-permute-start.4 = (bf16[4,72,384]{2,1,0:T(8,128)(2,1)S(1)}, bf16[4,72,384]{2,1,0:T(8,128)(2,1)S(1)}, u32[]{:S(2)}, u32[]{:S(2)}) collective-permute-start(bf16[4,72,384]{2,1,0:T(8,128)(2,1)S(1)} %get-tuple-element.54), channel_id=1, source_target_pairs={{1,2},{2,1},{3,4},{4,3},{5,6},{6,5},{9,10},{10,9},{11,12},{12,11},... | collective-permute-start | bytes 663560 | tf_op jit(solution)/shard_map/ppermute | solution.py:407
  18.4 7.3 %collective-permute-start.6 = (bf16[2,72,768]{2,1,0:T(8,128)(2,1)S(1)}, bf16[2,72,768]{2,1,0:T(8,128)(2,1)S(1)}, u32[]{:S(2)}, u32[]{:S(2)}) collective-permute-start(bf16[2,72,768]{2,1,0:T(8,128)(2,1)S(1)} %pad_maximum_fusion.3), channel_id=1, source_target_pairs={{0,16},{8,24},{16,0},{24,8},{1,17},{9,25},{17,1},{25,9},{2,18},{10... | collective-permute-start | bytes 663560 | tf_op jit(solution)/shard_map/ppermute | solution.py:390
  29.2 7.3 %collective-permute-start.8 = (bf16[4,72,384]{2,1,0:T(8,128)(2,1)S(1)}, bf16[4,72,384]{2,1,0:T(8,128)(2,1)S(1)}, u32[]{:S(2)}, u32[]{:S(2)}) collective-permute-start(bf16[4,72,384]{2,1,0:T(8,128)(2,1)S(1)} %get-tuple-element.43.refs_1_), channel_id=1, source_target_pairs={{0,1},{1,0},{2,3},{3,2},{4,5},{5,4},{6,7},{7,6},{8,9},{9,8},{10,11... | collective-permute-start | bytes 663560 | tf_op jit(solution)/shard_map/ppermute | solution.py:403
  29.6 7.5 %collective-permute-start.9 = (bf16[4,72,384]{2,1,0:T(8,128)(2,1)S(1)}, bf16[4,72,384]{2,1,0:T(8,128)(2,1)S(1)}, u32[]{:S(2)}, u32[]{:S(2)}) collective-permute-start(bf16[4,72,384]{2,1,0:T(8,128)(2,1)S(1)} %get-tuple-element.42.refs_0_), channel_id=1, source_target_pairs={{1,2},{2,1},{3,4},{4,3},{5,6},{6,5},{9,10},{10,9},{11,12},{12,11},... | collective-permute-start | bytes 663560 | tf_op jit(solution)/shard_map/ppermute | solution.py:407
  34.9 14.3 %collective-permute-start.7 = (bf16[72,512]{1,0:T(8,128)(2,1)S(1)}, bf16[72,512]{1,0:T(8,128)(2,1)S(1)}, u32[]{:S(2)}, u32[]{:S(2)}) collective-permute-start(bf16[72,512]{1,0:T(8,128)(2,1)S(1)} %get-tuple-element.48), channel_id=1, source_target_pairs={{0,8},{8,0},{16,24},{24,16},{1,9},{9,1},{17,25},{25,17},{2,10},{10... | collective-permute-start | bytes 221192 | tf_op jit(solution)/shard_map/ppermute | solution.py:390
  41.3 8.0 %collective-permute-start.12 = (bf16[72,512]{1,0:T(8,128)(2,1)S(1)}, bf16[72,512]{1,0:T(8,128)(2,1)S(1)}, u32[]{:S(2)}, u32[]{:S(2)}) collective-permute-start(bf16[72,512]{1,0:T(8,128)(2,1)S(1)} %shard_map.90), channel_id=1, source_target_pairs={{0,8},{8,0},{16,24},{24,16},{1,9},{9,1},{17,25},{25,17},{2,10},{10... | collective-permute-start | bytes 221192 | tf_op jit(solution)/shard_map/ppermute | solution.py:390
  44.5 6.1 %collective-permute-start.11 = (bf16[72,1024]{1,0:T(8,128)(2,1)S(1)}, bf16[72,1024]{1,0:T(8,128)(2,1)S(1)}, u32[]{:S(2)}, u32[]{:S(2)}) collective-permute-start(bf16[72,1024]{1,0:T(8,128)(2,1)S(1)} %shard_map.88), channel_id=1, source_target_pairs={{0,24},{8,16},{16,8},{24,0},{1,25},{9,17},{17,9},{25,1},{2,26},{10... | collective-permute-start | bytes 442376 | tf_op jit(solution)/shard_map/ppermute | solution.py:390
  46.8 7.6 %collective-permute-start.10 = (bf16[72,1024]{1,0:T(8,128)(2,1)S(1)}, bf16[72,1024]{1,0:T(8,128)(2,1)S(1)}, u32[]{:S(2)}, u32[]{:S(2)}) collective-permute-start(bf16[72,1024]{1,0:T(8,128)(2,1)S(1)} %shard_map.87), channel_id=1, source_target_pairs={{0,16},{8,24},{16,0},{24,8},{1,17},{9,25},{17,1},{25,9},{2,18},{10... | collective-permute-start | bytes 442376 | tf_op jit(solution)/shard_map/ppermute | solution.py:390

commit v7 on v6

--- a/solution.py
+++ b/solution.py
@@ -171,21 +171,18 @@
         to_columns(block[...], rows_ref)
         for r in range(p.rows):
             for t in range(p.local):
-                taps_ref[REACH + r, t0 + t] = taps_of(p, rows_ref, p.at(r, t), flip)
-
-
-def fill_halo(p, where, near, far, rows_ref, taps_ref, flip, base):
+                taps_ref[r, t0 + t] = taps_of(p, rows_ref, p.at(r, t), flip)
+
+
+def fill_halo(p, where, blocks, begin, rows_ref, taps_ref):
     me, even = where[0], where[1] == 1
     for d in range(p.n):
-        t0 = (me ^ d) * p.local + base
-        to_columns(jnp.where(even, far[d], near[d]), rows_ref)
+        t0 = (me ^ d) * p.local + p.side
+        to_columns(jnp.where(even, blocks[0][d], blocks[1][d]), rows_ref)
         for r in range(REACH):
             for t in range(p.local):
-                taps_ref[r, t0 + t] = taps_of(p, rows_ref, p.shift + p.at(r, t), flip)
-        to_columns(jnp.where(even, near[d], far[d]), rows_ref)
-        for r in range(REACH):
-            for t in range(p.local):
-                taps_ref[REACH + p.rows + r, t0 + t] = taps_of(p, rows_ref, p.at(r, t), flip)
+                taps_ref[r, t0 + t] = taps_of(p, rows_ref, begin + p.at(r, t), False)
+    wrap(p, taps_ref, 0, REACH)
 
 
 def fill_pairs(p, where, halves, rows_ref, taps_ref, flip, row):
@@ -214,25 +211,21 @@
     return lax.dot_general(a, b, dims, preferred_element_type=F32)
 
 
-def hidden_rows(p, where, taps_ref, w_in, bias_in, act_ref, slope_ref, count, row_of):
-    def body(step, carry):
-        row = row_of(step)
-        total = None
-        for i in range(p.taps):
-            for k in range(p.window):
-                a = taps_ref[row + i, k : k + p.total].reshape(p.total * p.wp, p.packed)
-                term = dot(a, w_in[i * p.window + k], False)
-                total = term if total is None else total + term
-        pre = total + bias_in[...]
-        sig = 0.5 * jnp.tanh(0.5 * pre) + 0.5
-        act = pre * sig
-        slope = sig + act * (1.0 - sig)
-        mask = row_mask(p, where, row)
-        act_ref[row] = (act * mask).astype(BF16).reshape(p.total, p.wp, p.hidden)
-        slope_ref[row] = (slope * mask).reshape(p.total, p.wp, p.hidden)
-        return carry
-
-    lax.fori_loop(0, count, body, 0)
+def hidden_row(p, where, row, taps, w_in, bias_in, act_ref, slope_ref):
+    total = None
+    for i in range(p.taps):
+        ref, at = taps[i]
+        for k in range(p.window):
+            a = ref[at, k : k + p.total].reshape(p.total * p.wp, p.packed)
+            term = dot(a, w_in[i * p.window + k], False)
+            total = term if total is None else total + term
+    pre = total + bias_in[...]
+    sig = 0.5 * jnp.tanh(0.5 * pre) + 0.5
+    act = pre * sig
+    slope = sig + act * (1.0 - sig)
+    mask = row_mask(p, where, row)
+    act_ref[row] = (act * mask).astype(BF16).reshape(p.total, p.wp, p.hidden)
+    slope_ref[row] = (slope * mask).reshape(p.total, p.wp, p.hidden)
 
 
 def early_kernel(p, where, *refs):
@@ -242,16 +235,29 @@
 
 def inner_kernel(p, where, block, w_in, bias_in, _taps, taps_ref, act_ref, slope_ref, rows_ref):
     fill_own(p, where, {p.n - 1: block}, rows_ref, taps_ref, False, p.side)
-    wrap(p, taps_ref, REACH, p.rows)
-    hidden_rows(p, where, taps_ref, w_in, bias_in, act_ref, slope_ref, p.rows - 2, lambda s: s + REACH)
-
-
-def outer_kernel(p, where, near, far, w_in, bias_in, _taps, _act, _slope, taps_ref, act_ref, slope_ref, rows_ref):
-    fill_halo(p, where, near, far, rows_ref, taps_ref, False, p.side)
-    wrap(p, taps_ref, 0, REACH)
-    wrap(p, taps_ref, REACH + p.rows, REACH)
-    edge = lambda s: jnp.where(s < REACH, s, s + p.rows - 2)
-    hidden_rows(p, where, taps_ref, w_in, bias_in, act_ref, slope_ref, 2 * REACH, edge)
+    wrap(p, taps_ref, 0, p.rows)
+
+    for step in range(p.rows - 2):
+        taps = [(taps_ref, step + i) for i in range(p.taps)]
+        hidden_row(p, where, step + REACH, taps, w_in, bias_in, act_ref, slope_ref)
+
+
+def outer_kernel(p, where, near, far, w_in, bias_in, taps_ref, _act, _slope, act_ref, slope_ref, *scratch):
+    below, above, rows_below, rows_above = scratch
+
+    def row_at(row):
+        taps = []
+        for at in range(row - REACH, row - REACH + p.taps):
+            ref = below if at < 0 else above if at >= p.rows else taps_ref
+            taps.append((ref, at % p.rows if ref is above else at + REACH if ref is below else at))
+        hidden_row(p, where, row, taps, w_in, bias_in, act_ref, slope_ref)
+
+    fill_halo(p, where, (far, near), p.shift, rows_below, below)
+    row_at(1)
+    fill_halo(p, where, (near, far), 0, rows_above, above)
+    row_at(0)
+    row_at(p.rows)
+    row_at(p.rows + 1)
 
 
 def score_kernel(p, which, where, *refs):
@@ -260,22 +266,20 @@
     targets, wide_ref, resid_ref, parts = refs[3 : n + 3], refs[n + 3], refs[n + 4], refs[n + 5 :]
     me = where[0]
     pair = 1 - where[1] if which == 0 else where[1]
-    wide_ref[...] = jnp.zeros_like(wide_ref)
-
-    def score_row(step, carry):
+    for d in range(n):
+        wide_ref[d, p.half :, :] = jnp.zeros((p.halfp - p.half, LANES), F32)
+    for step in range(REACH):
         total = None
         for i in range(p.taps):
             a = act_ref[pair * REACH + step + i].reshape(p.total * p.wp, p.hidden)
             term = dot(a, w_out[i], True)
             total = term if total is None else total + term
-        spread(p, total, parts)
+        here = parts[2 * step : 2 * step + 2]
+        spread(p, total, here)
         for d in range(n):
             for t in range(p.local):
-                s = untap(p, parts, (me ^ d) * p.local + t, 8, p.wx, False) + bias_out[...]
-                wide_ref[d, pl.ds(pl.multiple_of((step * p.local + t) * p.wx, 8), p.wx), :] = s
-        return carry
-
-    lax.fori_loop(0, REACH, score_row, 0)
+                s = untap(p, here, (me ^ d) * p.local + t, 8, p.wx, False) + bias_out[...]
+                wide_ref[d, p.at(step, t) : p.at(step, t) + p.wx, :] = s
     for d in range(n):
         for m in range(p.halfp // LANES):
             cols = slice(m * LANES, (m + 1) * LANES)
@@ -284,19 +288,15 @@
             resid_ref[d, :, cols] = (tile - jnp.log(target.astype(F32)) * (1.0 / CODE)).astype(BF16)
 
 
-def gradient_rows(p, taps_ref, w_out, slope_ref, grad_ref, count, row_of):
-    def body(step, carry):
-        row = row_of(step)
-        total = None
-        for i in range(p.taps):
-            a = taps_ref[row + 2 - i].reshape(p.total * p.wp, p.packed)
-            term = dot(a, w_out[i], False)
-            total = term if total is None else total + term
-        grad = total.reshape(p.total, p.wp, p.hidden) * slope_ref[row]
-        grad_ref[row, p.side : p.side + p.total] = grad.astype(BF16)
-        return carry
-
-    lax.fori_loop(0, count, body, 0)
+def gradient_row(p, row, taps, w_out, slope_ref, grad_ref):
+    total = None
+    for i in range(p.taps):
+        ref, at = taps[i]
+        term = dot(ref[at].reshape(p.total * p.wp, p.packed), w_out[i], False)
+        total = term if total is None else total + term
+    grad = total.reshape(p.total, p.wp, p.hidden) * slope_ref[row]
+    grad_ref[row, p.side : p.side + p.total] = grad.astype(BF16)
+    wrap(p, grad_ref, row, 1)
 
 
 def back_inner_kernel(p, where, *refs):
@@ -306,10 +306,11 @@
     own_ref, scores = refs[8], refs[9 : n + 8]
     rows_ref, thin_ref = refs[n + 8 :]
     even = where[1] == 1
-    fill_pairs(p, where, resid, rows_ref, taps_ref, True, REACH)
-    fill_pairs(p, where, resid[::-1], rows_ref, taps_ref, True, 2 * REACH)
-    gradient_rows(p, taps_ref, w_out, slope_ref, grad_ref, p.rows - 2, lambda s: s + REACH)
-    wrap(p, grad_ref, REACH, p.rows - 2)
+    fill_pairs(p, where, resid, rows_ref, taps_ref, True, 0)
+    fill_pairs(p, where, resid[::-1], rows_ref, taps_ref, True, REACH)
+    for row in range(REACH, p.rows):
+        taps = [(taps_ref, row - i) for i in range(p.taps)]
+        gradient_row(p, row, taps, w_out, slope_ref, grad_ref)
     for d in range(n):
         for r in range(p.rows):
             first, second = wide if r < REACH else wide[::-1]
@@ -321,19 +322,28 @@
         turn(p, thin_ref, own_ref if d == 0 else scores[d - 1], 0)
 
 
+def back_outer_kernel(p, where, near, far, slope_ref, w_out, taps_ref, _grad, grad_ref, *scratch):
+    below, above, rows_below, rows_above = scratch
+
+    def row_at(row):
+        taps = []
+        for at in range(row, row - p.taps, -1):
+            ref = below if at < 0 else above if at >= p.rows else taps_ref
+            taps.append((ref, at % p.rows if ref is above else at + REACH if ref is below else at))
+        gradient_row(p, row, taps, w_out, slope_ref, grad_ref)
+
+    fill_pairs(p, where, (far, near), rows_below, below, True, 0)
+    row_at(1)
+    fill_pairs(p, where, (near, far), rows_above, above, True, 0)
+    row_at(0)
+    row_at(p.rows)
+    row_at(p.rows + 1)
+
+
 def turn(p, thin_ref, out_ref, begin):
     for m in range(p.out // LANES):
         tile = thin_ref[m * LANES : (m + 1) * LANES, :].T[: p.cp]
         out_ref[:, begin + m * LANES : begin + (m + 1) * LANES] = tile.astype(out_ref.dtype)
-
-
-def back_outer_kernel(p, where, near, far, slope_ref, w_out, _taps, _grad, taps_ref, grad_ref, rows_ref):
-    fill_pairs(p, where, (far, near), rows_ref, taps_ref, True, 0)
-    fill_pairs(p, where, (near, far), rows_ref, taps_ref, True, 3 * REACH)
-    edge = lambda s: jnp.where(s < REACH, s, s + p.rows - 2)
-    gradient_rows(p, taps_ref, w_out, slope_ref, grad_ref, 2 * REACH, edge)
-    wrap(p, grad_ref, 0, REACH)
-    wrap(p, grad_ref, p.rows, REACH)
 
 
 def guide_kernel(p, d, where, grad_ref, w_in, *refs):
@@ -444,9 +454,8 @@
     far = send_far(p, jnp.where(even, low, high))
 
     columns = scratch((p.posp + 32, LANES), F32)
-    deep = p.rows + 2 * REACH
     around = p.total + 2 * p.side
-    taps_shape = sds((deep, around, p.wp, p.packed), BF16)
+    taps_shape = sds((p.rows, around, p.wp, p.packed), BF16)
     act_shape = sds((p.rows + 2, p.total, p.wp, p.hidden), BF16)
     slope_shape = sds((p.rows + 2, p.total, p.wp, p.hidden), F32)
     taps = call(kernel(early_kernel, p), [taps_shape], [columns], blocks[:-1], 16 << 20, 1)[0]
@@ -456,11 +465,12 @@
     )
     for bit in stages[1:]:
         goals = relay_tm(p, goals, bit)
-    _, act, slope = call(
-        kernel(outer_kernel, p), [taps_shape, act_shape, slope_shape], [columns],
-        [near, far, w_in, b_in, *inner], 24 << 20, 8, {4: 0, 5: 1, 6: 2},
+    edge = scratch((REACH, around, p.wp, p.packed), BF16)
+    act, slope = call(
+        kernel(outer_kernel, p), [act_shape, slope_shape], [edge, edge, columns, columns],
+        [near, far, w_in, b_in, *inner], 24 << 20, 7, {5: 0, 6: 1},
     )
-    part = [scratch((p.total, p.wp + 16, LANES), F32)] * 2
+    part = [scratch((p.total, p.wp + 16, LANES), F32)] * (2 * REACH)
 
     def score(which):
         return call(
@@ -473,7 +483,7 @@
     far = send_far(p, resid_far)
     wide_near, resid_near = score(1)
     near = send_near(p, resid_near)
-    taps_shape = sds((deep, p.total, p.wp, p.packed), BF16)
+    taps_shape = sds((p.rows, p.total, p.wp, p.packed), BF16)
     grad_shape = sds((p.rows + 2, around, p.wp, p.hidden), BF16)
     thin = sds((p.cp, p.out), BF16)
     thin_rows = scratch((p.out, LANES), F32)
@@ -485,10 +495,11 @@
     )
     taps, grad, scores = out[0], out[1], list(out[2:])
     scores[1] = send_tm(p, scores[1], 1)
-    taps, grad = call(
-        kernel(back_outer_kernel, p), [taps_shape, grad_shape], [columns],
-        [near, far, slope, w_out, taps, grad], 24 << 20, 3, {4: 0, 5: 1},
-    )
+    edge = scratch((REACH, p.total, p.wp, p.packed), BF16)
+    grad = call(
+        kernel(back_outer_kernel, p), [grad_shape], [edge, edge, columns, columns],
+        [near, far, slope, w_out, taps, grad], 24 << 20, 2, {5: 0},
+    )[0]
     parts = [None] * n
     for d in [*range(n - 1, 0, -1), 0]:
         part = [scratch((p.rows * p.local, p.wp + 16, LANES), F32)] * 2
@@ -501,15 +512,13 @@
         if d:
             parts[d] = send_tm(p, parts[d], d)
 
-    begins = [[0, 0] + [p.out] * (n - 2), [0] * n]
-    shape = [sds((p.local, p.chans, p.rows, p.lon), F32)] * 2
-    held = [scratch((2, n, p.cp, p.out), F32)]
-    return tuple(
-        call(
-            kernel(join_kernel, p, begins), shape, held, scores[:2] + parts[2:] + parts, 16 << 20, 1.5,
-            states=p.local, outs_by=True,
-        )
-    )
+    def join(blocks, begins):
+        shape = [sds((p.local, p.chans, p.rows, p.lon), F32)]
+        held = [scratch((1, n, p.cp, p.out), F32)]
+        return call(kernel(join_kernel, p, [begins]), shape, held, blocks, 8 << 20, 1, states=p.local, outs_by=True)[0]
+
+    begins = [0, 0] + [p.out] * (n - 2)
+    return join(scores[:2] + parts[2:], begins), join(parts, [0] * n)
 
 
 def solution(mesh):

time: 56.3 us -> 55.3 us (0.982)
  the two profiles are of different devices: /device:TPU:11 before, /device:TPU:19 now
where the time goes in v7:
time: 55.3 us; the launch traced here: 55.2 us
  Pallas kernels  26.7 us (48%)
  starting transfers between devices  16.3 us (29%)
  waiting for transfers between devices  9.88 us (18%)
  local copies, waits for them, and re-layouts  1.22 us (2%)
  between operations  0.86 us (2%)
    pallas_call x16, Pallas kernels, call(): pl.pallas_call(lambda *refs: kernel(here(), *refs), grid=(states,) if sta...  26.7 us
    ppermute x9, starting transfers between devices, send_tm(): return lax.ppermute(value, 'tm', [(i, i ^ d) for i in range(p.n)])  7.89 us
    ppermute x9, waiting for transfers between devices, send_tm(): return lax.ppermute(value, 'tm', [(i, i ^ d) for i in range(p.n)])  7.73 us
    ppermute x2, starting transfers between devices, send_far(): lax.ppermute(value, 'lat', [(i, (i + 1 ^ 1) - 1) for i in range(1, p.m -...  5.54 us
    ppermute x2, starting transfers between devices, send_near(): return lax.ppermute(value, 'lat', [(i, i ^ 1) for i in range(p.m)])  2.88 us
    ppermute x2, waiting for transfers between devices, send_far(): lax.ppermute(value, 'lat', [(i, (i + 1 ^ 1) - 1) for i in range(1, p.m -...  2.15 us
    unnamed x12, local copies, waits for them, and re-layouts  1.14 us
  transfers between devices with their start and end apart: 13, of which 6 were waited for; matrix products, arithmetic and copies ran while one was open for 0% of the time, Pallas kernels for 40%

profile of v7, /device:TPU:19, one launch (start us, length us, event | category | flops | bytes accessed | tf_op | source)
XLA Modules:
  0.0 55.2 jit_solution(6451576251487006865)
XLA Ops:
  0.6 0.0 copy-start.1
  0.6 1.0 %copy-done.1 = f32[2,69,4,256]{3,2,1,0:T(4,128)S(1)} copy-done((f32[2,69,4,256]{3,2,1,0:T(4,128)S(1)}, f32[2,69,4,256]{3,2,1,0:T(4,128)}, u32[]{:S(2)}) %copy-start.1) | copy-done | bytes 565272
  1.7 0.0 copy-start.2
  1.7 0.6 %shard_map.77 = (bf16[72,640]{1,0:T(8,128)(2,1)S(1)}, bf16[72,640]{1,0:T(8,128)(2,1)S(1)}, bf16[72,640]{1,0:T(8,128)(2,1)S(1)}, bf16[72,640]{1,0:T(8,128)(2,1)S(1)}) custom-call(f32[2,69,4,256]{3,2,1,0:T(4,128)S(1)} %copy-done.1), custom_call_target="tpu_custom_call" | custom-call | flops 1500000000 | tf_op jit(solution)/shard_map/pallas_call | solution.py:69
  2.3 0.3 collective-permute-start
  2.6 1.2 %collective-permute-start.1 = (bf16[72,640]{1,0:T(8,128)(2,1)S(1)}, bf16[72,640]{1,0:T(8,128)(2,1)S(1)}, u32[]{:S(2)}, u32[]{:S(2)}) collective-permute-start(bf16[72,640]{1,0:T(8,128)(2,1)S(1)} %get-tuple-element.29), channel_id=1, source_target_pairs={{0,16},{8,24},{16,0},{24,8},{1,17},{9,25},{17,1},{25,9},{2,18},{10... | collective-permute-start | bytes 276488 | tf_op jit(solution)/shard_map/ppermute | solution.py:400
  3.8 0.0 copy-start
  3.8 0.0 copy-start.3
  3.8 1.2 %collective-permute-start.2 = (bf16[72,640]{1,0:T(8,128)(2,1)S(1)}, bf16[72,640]{1,0:T(8,128)(2,1)S(1)}, u32[]{:S(2)}, u32[]{:S(2)}) collective-permute-start(bf16[72,640]{1,0:T(8,128)(2,1)S(1)} %get-tuple-element.30), channel_id=1, source_target_pairs={{0,24},{8,16},{16,8},{24,0},{1,25},{9,17},{17,9},{25,1},{2,26},{10... | collective-permute-start | bytes 276488 | tf_op jit(solution)/shard_map/ppermute | solution.py:400
  5.0 0.0 copy-done.2
  5.0 0.7 %shard_map.82 = (bf16[72,768]{1,0:T(8,128)(2,1)S(1)}, bf16[72,768]{1,0:T(8,128)(2,1)S(1)}, bf16[72,768]{1,0:T(8,128)(2,1)S(1)}, bf16[72,768]{1,0:T(8,128)(2,1)S(1)}) custom-call(f32[2,69,4,256]{3,2,1,0:T(4,128)S(1)} %copy-done.2), custom_call_target="tpu_custom_call" | custom-call | flops 1500000000 | tf_op jit(solution)/shard_map/pallas_call | solution.py:69
  5.7 0.3 collective-permute-start.5
  6.0 0.0 copy-done
  6.1 0.0 copy-done.3
  6.1 0.0 copy-start.5
  6.1 0.6 %shard_map.78 = (bf16[15,256,256]{2,1,0:T(8,128)(2,1)S(1)}, bf16[3,256,256]{2,1,0:T(8,128)(2,1)S(1)}) custom-call(bf16[3,3,345,256]{3,2,1,0:T(8,128)(2,1)S(1)} %bitcast.32, bf16[3,3,69,256]{3,2,1,0:T(8,128)(2,1)S(1)} %copy-done.3), custom_call_target="tpu_custom_call" | custom-call | flops 2000000000 | tf_op jit(solution)/shard_map/pallas_call | solution.py:69
  6.7 0.1 copy-done.5
  6.7 0.0 collective-permute-done.refs_1_
  6.8 0.0 collective-permute-done.1.refs_2_
  6.8 2.0 %collective-permute-done.2.refs_0_ = bf16[72,640]{1,0:T(8,128)(2,1)S(1)} collective-permute-done((bf16[72,640]{1,0:T(8,128)(2,1)S(1)}, bf16[72,640]{1,0:T(8,128)(2,1)S(1)}, u32[]{:S(2)}, u32[]{:S(2)}) %collective-permute-start.2) | collective-permute-done | bytes 92192 | tf_op jit(solution)/shard_map/ppermute | solution.py:400
  8.8 0.1 broadcast_select_fusion
  8.9 0.0 copy-start.4
  8.9 2.4 %collective-permute-start.3 = (bf16[4,72,384]{2,1,0:T(8,128)(2,1)S(1)}, bf16[4,72,384]{2,1,0:T(8,128)(2,1)S(1)}, u32[]{:S(2)}, u32[]{:S(2)}) collective-permute-start(bf16[4,72,384]{2,1,0:T(8,128)(2,1)S(1)} %get-tuple-element.53), channel_id=1, source_target_pairs={{0,1},{1,0},{2,3},{3,2},{4,5},{5,4},{6,7},{7,6},{8,9},{9,8},{10,11... | collective-permute-start | bytes 663560 | tf_op jit(solution)/shard_map/ppermute | solution.py:413
  11.4 3.1 %collective-permute-start.4 = (bf16[4,72,384]{2,1,0:T(8,128)(2,1)S(1)}, bf16[4,72,384]{2,1,0:T(8,128)(2,1)S(1)}, u32[]{:S(2)}, u32[]{:S(2)}) collective-permute-start(bf16[4,72,384]{2,1,0:T(8,128)(2,1)S(1)} %get-tuple-element.52), channel_id=1, source_target_pairs={{1,2},{2,1},{3,4},{4,3},{5,6},{6,5},{9,10},{10,9},{11,12},{12,11},... | collective-permute-start | bytes 663560 | tf_op jit(solution)/shard_map/ppermute | solution.py:417
  14.5 0.5 shard_map.79.refs_3_
  15.0 0.0 copy-done.4
  15.0 3.2 %shard_map.80 = (bf16[4,12,80,256]{3,2,1,0:T(8,128)(2,1)S(1)}, bf16[6,8,80,256]{3,2,1,0:T(8,128)(2,1)S(1)}, f32[6,8,80,256]{3,2,1,0:T(8,128)S(1)}) custom-call(bf16[72,640]{1,0:T(8,128)(2,1)S(1)} %collective-permute-done.2.refs_0_, bf16[15,256,256]{2,1,0:T(8,128)(2,1)S(1)} %get-tuple-element.31.refs_1_.refs_2_, ...), custom_call_target="tpu_custom_call", output_to_operand_aliasing={{0}: (3, {})} | custom-call | flops 5000000000 | tf_op jit(solution)/shard_map/pallas_call | solution.py:69
  18.1 0.0 collective-permute-done.5
  18.2 0.3 collective-permute-start.6
  18.5 0.0 collective-permute-done.3.refs_0_
  18.5 0.1 collective-permute-done.4.refs_1_
  18.6 6.2 %shard_map.81 = (bf16[6,8,80,256]{3,2,1,0:T(8,128)(2,1)S(1)}, f32[6,8,80,256]{3,2,1,0:T(8,128)S(1)}) custom-call(bf16[4,72,384]{2,1,0:T(8,128)(2,1)S(1)} %collective-permute-done.3.refs_0_, bf16[4,72,384]{2,1,0:T(8,128)(2,1)S(1)} %collective-permute-done.4.refs_1_, ...), custom_call_target="tpu_custom_call", output_to_operand_aliasing={{0}: (5, {}), {1}: (6, {})} | custom-call | flops 7000000000 | tf_op jit(solution)/shard_map/pallas_call | solution.py:69
  24.8 0.5 collective-permute-done.6
  25.4 1.4 %shard_map.84 = (f32[4,384,128]{2,1,0:T(8,128)S(1)}, bf16[4,72,384]{2,1,0:T(8,128)(2,1)S(1)}) custom-call(bf16[6,8,80,256]{3,2,1,0:T(8,128)(2,1)S(1)} %get-tuple-element.35.refs_0_, bf16[3,256,256]{2,1,0:T(8,128)(2,1)S(1)} %get-tuple-element.36.refs_1_.refs_5_.refs_3_, f32[1,128]{1,0:T(1,128)S(1)} %pad_bitcast_fusion.refs_2_, ...), custom_call_target="tpu_custom_call" | custom-call | flops 2000000000 | tf_op jit(solution)/shard_map/pallas_call | solution.py:69
  26.8 1.4 %shard_map.83 = (f32[4,384,128]{2,1,0:T(8,128)S(1)}, bf16[4,72,384]{2,1,0:T(8,128)(2,1)S(1)}) custom-call(bf16[6,8,80,256]{3,2,1,0:T(8,128)(2,1)S(1)} %get-tuple-element.35.refs_0_, bf16[3,256,256]{2,1,0:T(8,128)(2,1)S(1)} %get-tuple-element.36.refs_1_.refs_5_.refs_3_, f32[1,128]{1,0:T(1,128)S(1)} %pad_bitcast_fusion.refs_2_, ...), custom_call_target="tpu_custom_call" | custom-call | flops 2000000000 | tf_op jit(solution)/shard_map/pallas_call | solution.py:69
  28.2 0.5 collective-permute-start.8
  28.6 2.4 %collective-permute-start.9 = (bf16[4,72,384]{2,1,0:T(8,128)(2,1)S(1)}, bf16[4,72,384]{2,1,0:T(8,128)(2,1)S(1)}, u32[]{:S(2)}, u32[]{:S(2)}) collective-permute-start(bf16[4,72,384]{2,1,0:T(8,128)(2,1)S(1)} %get-tuple-element.41.refs_0_), channel_id=1, source_target_pairs={{1,2},{2,1},{3,4},{4,3},{5,6},{6,5},{9,10},{10,9},{11,12},{12,11},... | collective-permute-start | bytes 663560 | tf_op jit(solution)/shard_map/ppermute | solution.py:417
  31.1 1.4 %shard_map.85 = (bf16[4,8,80,256]{3,2,1,0:T(8,128)(2,1)S(1)}, bf16[6,12,80,256]{3,2,1,0:T(8,128)(2,1)S(1)}, f32[72,512]{1,0:T(8,128)S(1)}, bf16[72,512]{1,0:T(8,...) custom-call(bf16[4,72,384]{2,1,0:T(8,128)(2,1)S(1)} %get-tuple-element.41.refs_0_, ...), custom_call_target="tpu_custom_call" | custom-call | flops 2300000000 | tf_op jit(solution)/shard_map/pallas_call | solution.py:69
  32.5 1.6 %collective-permute-start.7 = (bf16[72,512]{1,0:T(8,128)(2,1)S(1)}, bf16[72,512]{1,0:T(8,128)(2,1)S(1)}, u32[]{:S(2)}, u32[]{:S(2)}) collective-permute-start(bf16[72,512]{1,0:T(8,128)(2,1)S(1)} %get-tuple-element.47), channel_id=1, source_target_pairs={{0,8},{8,0},{16,24},{24,16},{1,9},{9,1},{17,25},{25,17},{2,10},{10... | collective-permute-start | bytes 221192 | tf_op jit(solution)/shard_map/ppermute | solution.py:400
  34.1 0.0 collective-permute-done.8.refs_0_
  34.1 2.0 %collective-permute-done.9.refs_1_ = bf16[4,72,384]{2,1,0:T(8,128)(2,1)S(1)} collective-permute-done((bf16[4,72,384]{2,1,0:T(8,128)(2,1)S(1)}, bf16[4,72,384]{2,1,0:T(8,128)(2,1)S(1)}, u32[]{:S(2)}, u32[]{:S(2)}) %collective-permute-start.9) | collective-permute-done | bytes 221216 | tf_op jit(solution)/shard_map/ppermute | solution.py:417
  36.2 1.6 %shard_map.86.refs_0_ = bf16[6,12,80,256]{3,2,1,0:T(8,128)(2,1)S(1)} custom-call(bf16[4,72,384]{2,1,0:T(8,128)(2,1)S(1)} %collective-permute-done.8.refs_0_, bf16[4,72,384]{2,1,0:T(8,128)(2,1)S(1)} %collective-permute-done.9.refs_1_, f32[6,8,80,256]{3,2,1,0:T(8,128)S(1)} %get-tuple-element.45.refs_4_.refs_2_, ...), custom_call_target="tpu_custom_call", output_to_operand_aliasing={{}: (5, {})} | custom-call | flops 2000000000 | tf_op jit(solution)/shard_map/pallas_call | solution.py:69
  37.8 1.7 %shard_map.91 = bf16[72,512]{1,0:T(8,128)(2,1)S(1)} custom-call(bf16[6,12,80,256]{3,2,1,0:T(8,128)(2,1)S(1)} %shard_map.86.refs_0_, bf16[15,256,256]{2,1,0:T(8,128)(2,1)S(1)} %get-tuple-element.31.refs_1_.refs_2_), custom_call_target="tpu_custom_call" | custom-call | flops 2000000000 | tf_op jit(solution)/shard_map/pallas_call | solution.py:69
  39.5 1.6 %collective-permute-start.12 = (bf16[72,512]{1,0:T(8,128)(2,1)S(1)}, bf16[72,512]{1,0:T(8,128)(2,1)S(1)}, u32[]{:S(2)}, u32[]{:S(2)}) collective-permute-start(bf16[72,512]{1,0:T(8,128)(2,1)S(1)} %shard_map.91), channel_id=1, source_target_pairs={{0,8},{8,0},{16,24},{24,16},{1,9},{9,1},{17,25},{25,17},{2,10},{10... | collective-permute-start | bytes 221192 | tf_op jit(solution)/shard_map/ppermute | solution.py:400
  41.1 1.7 %shard_map.88 = bf16[72,1024]{1,0:T(8,128)(2,1)S(1)} custom-call(bf16[6,12,80,256]{3,2,1,0:T(8,128)(2,1)S(1)} %shard_map.86.refs_0_, bf16[15,256,256]{2,1,0:T(8,128)(2,1)S(1)} %get-tuple-element.31.refs_1_.refs_2_, bf16[72,512]{1,0:T(8,128)(2,1)S(1)} %get-tuple-element.51.refs_2_), custom_call_target="tpu_custom_call" | custom-call | flops 2000000000 | tf_op jit(solution)/shard_map/pallas_call | solution.py:69
  42.8 0.1 collective-permute-start.11
  42.8 1.7 %shard_map.87 = bf16[72,1024]{1,0:T(8,128)(2,1)S(1)} custom-call(bf16[6,12,80,256]{3,2,1,0:T(8,128)(2,1)S(1)} %shard_map.86.refs_0_, bf16[15,256,256]{2,1,0:T(8,128)(2,1)S(1)} %get-tuple-element.31.refs_1_.refs_2_, bf16[72,512]{1,0:T(8,128)(2,1)S(1)} %get-tuple-element.50.refs_2_), custom_call_target="tpu_custom_call" | custom-call | flops 2000000000 | tf_op jit(solution)/shard_map/pallas_call | solution.py:69
  44.5 1.2 %collective-permute-start.10 = (bf16[72,1024]{1,0:T(8,128)(2,1)S(1)}, bf16[72,1024]{1,0:T(8,128)(2,1)S(1)}, u32[]{:S(2)}, u32[]{:S(2)}) collective-permute-start(bf16[72,1024]{1,0:T(8,128)(2,1)S(1)} %shard_map.87), channel_id=1, source_target_pairs={{0,16},{8,24},{16,0},{24,8},{1,17},{9,25},{17,1},{25,9},{2,18},{10... | collective-permute-start | bytes 442376 | tf_op jit(solution)/shard_map/ppermute | solution.py:400
  45.8 1.7 %shard_map.90.refs_0_ = f32[72,512]{1,0:T(8,128)S(1)} custom-call(bf16[6,12,80,256]{3,2,1,0:T(8,128)(2,1)S(1)} %shard_map.86.refs_0_, bf16[15,256,256]{2,1,0:T(8,128)(2,1)S(1)} %get-tuple-element.31.refs_1_.refs_2_), custom_call_target="tpu_custom_call" | custom-call | flops 2000000000 | tf_op jit(solution)/shard_map/pallas_call | solution.py:69
  47.5 0.0 collective-permute-done.12.refs_1_
  47.5 1.6 %collective-permute-done.11.refs_3_ = bf16[72,1024]{1,0:T(8,128)(2,1)S(1)} collective-permute-done((bf16[72,1024]{1,0:T(8,128)(2,1)S(1)}, bf16[72,1024]{1,0:T(8,128)(2,1)S(1)}, u32[]{:S(2)}, u32[]{:S(2)}) %collective-permute-start.11) | collective-permute-done | bytes 147488 | tf_op jit(solution)/shard_map/ppermute | solution.py:400
  49.1 3.6 %collective-permute-done.10.refs_2_ = bf16[72,1024]{1,0:T(8,128)(2,1)S(1)} collective-permute-done((bf16[72,1024]{1,0:T(8,128)(2,1)S(1)}, bf16[72,1024]{1,0:T(8,128)(2,1)S(1)}, u32[]{:S(2)}, u32[]{:S(2)}) %collective-permute-start.10) | collective-permute-done | bytes 147488 | tf_op jit(solution)/shard_map/ppermute | solution.py:400
  52.7 1.2 %shard_map.92 = f32[2,69,4,256]{3,2,1,0:T(4,128)} custom-call(f32[72,512]{1,0:T(8,128)S(1)} %shard_map.90.refs_0_, bf16[72,512]{1,0:T(8,128)(2,1)S(1)} %collective-permute-done.12.refs_1_, bf16[72,1024]{1,0:T(8,128)(2,1)S(1)} %collective-permute-done.10.refs_2_, bf16[72,1024]{1,0:T(8,128)(2,1)S(1)} %collective-permute-done.11.refs_3_), custom_call_target="tpu_custom_call" | custom-call | flops 1000000000 | tf_op jit(solution)/shard_map/pallas_call | solution.py:69
  53.9 0.0 collective-permute-done.7.refs_1_
  53.9 1.2 %shard_map.89 = f32[2,69,4,256]{3,2,1,0:T(4,128)} custom-call(f32[72,512]{1,0:T(8,128)S(1)} %get-tuple-element.46.refs_0_, bf16[72,512]{1,0:T(8,128)(2,1)S(1)} %collective-permute-done.7.refs_1_, bf16[72,1024]{1,0:T(8,128)(2,1)S(1)} %collective-permute-done.10.refs_2_, bf16[72,1024]{1,0:T(8,128)(2,1)S(1)} %collective-permute-done.11.refs_3_), custom_call_target="tpu_custom_call" | custom-call | flops 1000000000 | tf_op jit(solution)/shard_map/pallas_call | solution.py:69
  (9 shorter events, 0.1 us)
Async XLA Ops:
  0.6 1.1 %copy-start.1 = (f32[2,69,4,256]{3,2,1,0:T(4,128)S(1)}, f32[2,69,4,256]{3,2,1,0:T(4,128)}, u32[]{:S(2)}) copy-start(f32[2,69,4,256]{3,2,1,0:T(4,128)} %refs_0_.2) | copy-start | bytes 1695748
  1.7 3.3 %copy-start.2 = (f32[2,69,4,256]{3,2,1,0:T(4,128)S(1)}, f32[2,69,4,256]{3,2,1,0:T(4,128)}, u32[]{:S(2)}) copy-start(f32[2,69,4,256]{3,2,1,0:T(4,128)} %refs_0_.3) | copy-start | bytes 1695748
  2.3 4.5 %collective-permute-start = (bf16[72,640]{1,0:T(8,128)(2,1)S(1)}, bf16[72,640]{1,0:T(8,128)(2,1)S(1)}, u32[]{:S(2)}, u32[]{:S(2)}) collective-permute-start(bf16[72,640]{1,0:T(8,128)(2,1)S(1)} %get-tuple-element.28), channel_id=1, source_target_pairs={{0,8},{8,0},{16,24},{24,16},{1,9},{9,1},{17,25},{25,17},{2,10},{10... | collective-permute-start | bytes 276488 | tf_op jit(solution)/shard_map/ppermute | solution.py:400
  2.6 4.2 %collective-permute-start.1 = (bf16[72,640]{1,0:T(8,128)(2,1)S(1)}, bf16[72,640]{1,0:T(8,128)(2,1)S(1)}, u32[]{:S(2)}, u32[]{:S(2)}) collective-permute-start(bf16[72,640]{1,0:T(8,128)(2,1)S(1)} %get-tuple-element.29), channel_id=1, source_target_pairs={{0,16},{8,24},{16,0},{24,8},{1,17},{9,25},{17,1},{25,9},{2,18},{10... | collective-permute-start | bytes 276488 | tf_op jit(solution)/shard_map/ppermute | solution.py:400
  3.8 2.2 %copy-start = (bf16[3,3,256,345]{2,3,1,0:T(8,128)(2,1)S(1)}, bf16[3,3,256,345]{2,3,1,0:T(8,128)(2,1)}, u32[]{:S(2)}) copy-start(bf16[3,3,256,345]{2,3,1,0:T(8,128)(2,1)} %param.8) | copy-start | bytes 4769284
  3.8 2.2 %copy-start.3 = (bf16[3,3,69,256]{3,2,1,0:T(8,128)(2,1)S(1)}, bf16[3,3,69,256]{3,2,1,0:T(8,128)(2,1)}, u32[]{:S(2)}) copy-start(bf16[3,3,69,256]{3,2,1,0:T(8,128)(2,1)} %refs_1_.1) | copy-start | bytes 953860
  3.8 5.0 %collective-permute-start.2 = (bf16[72,640]{1,0:T(8,128)(2,1)S(1)}, bf16[72,640]{1,0:T(8,128)(2,1)S(1)}, u32[]{:S(2)}, u32[]{:S(2)}) collective-permute-start(bf16[72,640]{1,0:T(8,128)(2,1)S(1)} %get-tuple-element.30), channel_id=1, source_target_pairs={{0,24},{8,16},{16,8},{24,0},{1,25},{9,17},{17,9},{25,1},{2,26},{10... | collective-permute-start | bytes 276488 | tf_op jit(solution)/shard_map/ppermute | solution.py:400
  5.7 12.4 %collective-permute-start.5 = (bf16[2,72,768]{2,1,0:T(8,128)(2,1)S(1)}, bf16[2,72,768]{2,1,0:T(8,128)(2,1)S(1)}, u32[]{:S(2)}, u32[]{:S(2)}) collective-permute-start(bf16[2,72,768]{2,1,0:T(8,128)(2,1)S(1)} %pad_maximum_fusion.2), channel_id=1, source_target_pairs={{0,8},{8,0},{16,24},{24,16},{1,9},{9,1},{17,25},{25,17},{2,10},{10... | collective-permute-start | bytes 663560 | tf_op jit(solution)/shard_map/ppermute | solution.py:400
  6.1 0.7 %copy-start.5 = (f32[69]{0:T(128)S(1)}, f32[69]{0:T(128)}, u32[]{:S(2)}) copy-start(f32[69]{0:T(128)} %param.11) | copy-start | bytes 832
  8.9 6.0 %copy-start.4 = (f32[256]{0:T(256)S(1)}, f32[256]{0:T(256)}, u32[]{:S(2)}) copy-start(f32[256]{0:T(256)} %param.9) | copy-start | bytes 3076
  8.9 9.6 %collective-permute-start.3 = (bf16[4,72,384]{2,1,0:T(8,128)(2,1)S(1)}, bf16[4,72,384]{2,1,0:T(8,128)(2,1)S(1)}, u32[]{:S(2)}, u32[]{:S(2)}) collective-permute-start(bf16[4,72,384]{2,1,0:T(8,128)(2,1)S(1)} %get-tuple-element.53), channel_id=1, source_target_pairs={{0,1},{1,0},{2,3},{3,2},{4,5},{5,4},{6,7},{7,6},{8,9},{9,8},{10,11... | collective-permute-start | bytes 663560 | tf_op jit(solution)/shard_map/ppermute | solution.py:413
  11.4 7.2 %collective-permute-start.4 = (bf16[4,72,384]{2,1,0:T(8,128)(2,1)S(1)}, bf16[4,72,384]{2,1,0:T(8,128)(2,1)S(1)}, u32[]{:S(2)}, u32[]{:S(2)}) collective-permute-start(bf16[4,72,384]{2,1,0:T(8,128)(2,1)S(1)} %get-tuple-element.52), channel_id=1, source_target_pairs={{1,2},{2,1},{3,4},{4,3},{5,6},{6,5},{9,10},{10,9},{11,12},{12,11},... | collective-permute-start | bytes 663560 | tf_op jit(solution)/shard_map/ppermute | solution.py:417
  18.2 7.1 %collective-permute-start.6 = (bf16[2,72,768]{2,1,0:T(8,128)(2,1)S(1)}, bf16[2,72,768]{2,1,0:T(8,128)(2,1)S(1)}, u32[]{:S(2)}, u32[]{:S(2)}) collective-permute-start(bf16[2,72,768]{2,1,0:T(8,128)(2,1)S(1)} %pad_maximum_fusion.3), channel_id=1, source_target_pairs={{0,16},{8,24},{16,0},{24,8},{1,17},{9,25},{17,1},{25,9},{2,18},{10... | collective-permute-start | bytes 663560 | tf_op jit(solution)/shard_map/ppermute | solution.py:400
  28.2 5.9 %collective-permute-start.8 = (bf16[4,72,384]{2,1,0:T(8,128)(2,1)S(1)}, bf16[4,72,384]{2,1,0:T(8,128)(2,1)S(1)}, u32[]{:S(2)}, u32[]{:S(2)}) collective-permute-start(bf16[4,72,384]{2,1,0:T(8,128)(2,1)S(1)} %get-tuple-element.42.refs_1_), channel_id=1, source_target_pairs={{0,1},{1,0},{2,3},{3,2},{4,5},{5,4},{6,7},{7,6},{8,9},{9,8},{10,11... | collective-permute-start | bytes 663560 | tf_op jit(solution)/shard_map/ppermute | solution.py:413
  28.6 7.5 %collective-permute-start.9 = (bf16[4,72,384]{2,1,0:T(8,128)(2,1)S(1)}, bf16[4,72,384]{2,1,0:T(8,128)(2,1)S(1)}, u32[]{:S(2)}, u32[]{:S(2)}) collective-permute-start(bf16[4,72,384]{2,1,0:T(8,128)(2,1)S(1)} %get-tuple-element.41.refs_0_), channel_id=1, source_target_pairs={{1,2},{2,1},{3,4},{4,3},{5,6},{6,5},{9,10},{10,9},{11,12},{12,11},... | collective-permute-start | bytes 663560 | tf_op jit(solution)/shard_map/ppermute | solution.py:417
  32.5 21.4 %collective-permute-start.7 = (bf16[72,512]{1,0:T(8,128)(2,1)S(1)}, bf16[72,512]{1,0:T(8,128)(2,1)S(1)}, u32[]{:S(2)}, u32[]{:S(2)}) collective-permute-start(bf16[72,512]{1,0:T(8,128)(2,1)S(1)} %get-tuple-element.47), channel_id=1, source_target_pairs={{0,8},{8,0},{16,24},{24,16},{1,9},{9,1},{17,25},{25,17},{2,10},{10... | collective-permute-start | bytes 221192 | tf_op jit(solution)/shard_map/ppermute | solution.py:400
  39.5 8.0 %collective-permute-start.12 = (bf16[72,512]{1,0:T(8,128)(2,1)S(1)}, bf16[72,512]{1,0:T(8,128)(2,1)S(1)}, u32[]{:S(2)}, u32[]{:S(2)}) collective-permute-start(bf16[72,512]{1,0:T(8,128)(2,1)S(1)} %shard_map.91), channel_id=1, source_target_pairs={{0,8},{8,0},{16,24},{24,16},{1,9},{9,1},{17,25},{25,17},{2,10},{10... | collective-permute-start | bytes 221192 | tf_op jit(solution)/shard_map/ppermute | solution.py:400
  42.8 6.3 %collective-permute-start.11 = (bf16[72,1024]{1,0:T(8,128)(2,1)S(1)}, bf16[72,1024]{1,0:T(8,128)(2,1)S(1)}, u32[]{:S(2)}, u32[]{:S(2)}) collective-permute-start(bf16[72,1024]{1,0:T(8,128)(2,1)S(1)} %shard_map.88), channel_id=1, source_target_pairs={{0,24},{8,16},{16,8},{24,0},{1,25},{9,17},{17,9},{25,1},{2,26},{10... | collective-permute-start | bytes 442376 | tf_op jit(solution)/shard_map/ppermute | solution.py:400
  44.5 8.2 %collective-permute-start.10 = (bf16[72,1024]{1,0:T(8,128)(2,1)S(1)}, bf16[72,1024]{1,0:T(8,128)(2,1)S(1)}, u32[]{:S(2)}, u32[]{:S(2)}) collective-permute-start(bf16[72,1024]{1,0:T(8,128)(2,1)S(1)} %shard_map.87), channel_id=1, source_target_pairs={{0,16},{8,24},{16,0},{24,8},{1,17},{9,25},{17,1},{25,9},{2,18},{10... | collective-permute-start | bytes 442376 | tf_op jit(solution)/shard_map/ppermute | solution.py:400

commit v8 on v7

--- a/solution.py
+++ b/solution.py
@@ -429,7 +429,7 @@
         shape = [sds((p.cp, width), BF16)] * n
         held = [scratch((n, p.cp, width), F32)]
         return call(
-            kernel(split_kernel, p, place, coded), shape, held, [field], 8 << 20, 1.5, states=p.local, ins_by=True
+            kernel(split_kernel, p, place, coded), shape, held, [pltpu.with_memory_space_constraint(field, pltpu.HBM)], 8 << 20, 1.5, states=p.local, ins_by=True
         )
 
     mine = split(states, p.at, False, p.posp)
@@ -501,7 +501,7 @@
         [near, far, slope, w_out, taps, grad], 24 << 20, 2, {5: 0},
     )[0]
     parts = [None] * n
-    for d in [*range(n - 1, 0, -1), 0]:
+    for d in back_order(n):
         part = [scratch((p.rows * p.local, p.wp + 16, LANES), F32)] * 2
         ride = [scores[d]] if d > 1 else []
         shape = sds((p.cp, (1 + len(ride)) * p.out), BF16 if d else F32)
@@ -521,6 +521,10 @@
     return join(scores[:2] + parts[2:], begins), join(parts, [0] * n)
 
 
+def back_order(n):
+    return [*range(n - 2, 1, -1), n - 1, 1, 0]
+
+
 def solution(mesh):
     in_specs = (P("tm", None, "lat", None), P("tm", None, "lat", None), P(), P(), P(), P())
     out_specs = (P("tm", None, "lat", None), P("tm", None, "lat", None))

time: 55.3 us -> 55 us (level)
  the two profiles are of different devices: /device:TPU:19 before, /device:TPU:11 now
where the time goes in v8:
time: 55 us; the launch traced here: 54.8 us
  Pallas kernels  28.7 us (52%)
  starting transfers between devices  17.9 us (33%)
  waiting for transfers between devices  7.07 us (13%)
  between operations  0.84 us (2%)
    pallas_call x16, Pallas kernels, call(): pl.pallas_call(lambda *refs: kernel(here(), *refs), grid=(states,) if sta...  28.7 us
    ppermute x9, starting transfers between devices, send_tm(): return lax.ppermute(value, 'tm', [(i, i ^ d) for i in range(p.n)])  9.15 us
    ppermute x2, starting transfers between devices, send_far(): lax.ppermute(value, 'lat', [(i, (i + 1 ^ 1) - 1) for i in range(1, p.m -...  6.49 us
    ppermute x9, waiting for transfers between devices, send_tm(): return lax.ppermute(value, 'tm', [(i, i ^ d) for i in range(p.n)])  6.31 us
    ppermute x2, starting transfers between devices, send_near(): return lax.ppermute(value, 'lat', [(i, i ^ 1) for i in range(p.m)])  2.22 us
  transfers between devices with their start and end apart: 13, of which 5 were waited for; matrix products, arithmetic and copies ran while one was open for 0% of the time, Pallas kernels for 42%

profile of v8, /device:TPU:11, one launch (start us, length us, event | category | flops | bytes accessed | tf_op | source)
XLA Modules:
  0.0 54.8 jit_solution(10768447504387056656)
XLA Ops:
  0.6 1.5 %shard_map.77 = (bf16[72,640]{1,0:T(8,128)(2,1)S(1)}, bf16[72,640]{1,0:T(8,128)(2,1)S(1)}, bf16[72,640]{1,0:T(8,128)(2,1)S(1)}, bf16[72,640]{1,0:T(8,128)(2,1)S(1)}) custom-call(f32[2,69,4,256]{3,2,1,0:T(4,128)} %refs_0_.2), custom_call_target="tpu_custom_call" | custom-call | flops 1500000000 | tf_op jit(solution)/shard_map/pallas_call | solution.py:69
  2.2 0.3 collective-permute-start
  2.5 1.2 %collective-permute-start.1 = (bf16[72,640]{1,0:T(8,128)(2,1)S(1)}, bf16[72,640]{1,0:T(8,128)(2,1)S(1)}, u32[]{:S(2)}, u32[]{:S(2)}) collective-permute-start(bf16[72,640]{1,0:T(8,128)(2,1)S(1)} %get-tuple-element.29), channel_id=1, source_target_pairs={{0,16},{8,24},{16,0},{24,8},{1,17},{9,25},{17,1},{25,9},{2,18},{10... | collective-permute-start | bytes 276488 | tf_op jit(solution)/shard_map/ppermute | solution.py:400
  3.7 0.0 copy-start
  3.7 0.0 copy-start.1
  3.7 1.2 %collective-permute-start.2 = (bf16[72,640]{1,0:T(8,128)(2,1)S(1)}, bf16[72,640]{1,0:T(8,128)(2,1)S(1)}, u32[]{:S(2)}, u32[]{:S(2)}) collective-permute-start(bf16[72,640]{1,0:T(8,128)(2,1)S(1)} %get-tuple-element.30), channel_id=1, source_target_pairs={{0,24},{8,16},{16,8},{24,0},{1,25},{9,17},{17,9},{25,1},{2,26},{10... | collective-permute-start | bytes 276488 | tf_op jit(solution)/shard_map/ppermute | solution.py:400
  4.9 1.7 %shard_map.82 = (bf16[72,768]{1,0:T(8,128)(2,1)S(1)}, bf16[72,768]{1,0:T(8,128)(2,1)S(1)}, bf16[72,768]{1,0:T(8,128)(2,1)S(1)}, bf16[72,768]{1,0:T(8,128)(2,1)S(1)}) custom-call(f32[2,69,4,256]{3,2,1,0:T(4,128)} %refs_0_.3), custom_call_target="tpu_custom_call" | custom-call | flops 1500000000 | tf_op jit(solution)/shard_map/pallas_call | solution.py:69
  6.6 0.4 collective-permute-start.5
  7.0 0.0 copy-done
  7.0 0.0 copy-done.1
  7.1 0.0 copy-start.3
  7.1 0.6 %shard_map.78 = (bf16[15,256,256]{2,1,0:T(8,128)(2,1)S(1)}, bf16[3,256,256]{2,1,0:T(8,128)(2,1)S(1)}) custom-call(bf16[3,3,345,256]{3,2,1,0:T(8,128)(2,1)S(1)} %bitcast.32, bf16[3,3,69,256]{3,2,1,0:T(8,128)(2,1)S(1)} %copy-done.1), custom_call_target="tpu_custom_call" | custom-call | flops 2000000000 | tf_op jit(solution)/shard_map/pallas_call | solution.py:69
  7.6 0.1 copy-done.3
  7.7 0.0 collective-permute-done.refs_1_
  7.7 0.0 collective-permute-done.1.refs_2_
  7.8 1.0 %collective-permute-done.2.refs_0_ = bf16[72,640]{1,0:T(8,128)(2,1)S(1)} collective-permute-done((bf16[72,640]{1,0:T(8,128)(2,1)S(1)}, bf16[72,640]{1,0:T(8,128)(2,1)S(1)}, u32[]{:S(2)}, u32[]{:S(2)}) %collective-permute-start.2) | collective-permute-done | bytes 92192 | tf_op jit(solution)/shard_map/ppermute | solution.py:400
  8.7 0.1 broadcast_select_fusion
  8.8 0.0 copy-start.2
  8.8 1.8 %collective-permute-start.3 = (bf16[4,72,384]{2,1,0:T(8,128)(2,1)S(1)}, bf16[4,72,384]{2,1,0:T(8,128)(2,1)S(1)}, u32[]{:S(2)}, u32[]{:S(2)}) collective-permute-start(bf16[4,72,384]{2,1,0:T(8,128)(2,1)S(1)} %get-tuple-element.53), channel_id=1, source_target_pairs={{0,1},{1,0},{2,3},{3,2},{4,5},{5,4},{6,7},{7,6},{8,9},{9,8},{10,11... | collective-permute-start | bytes 663560 | tf_op jit(solution)/shard_map/ppermute | solution.py:413
  10.6 3.1 %collective-permute-start.4 = (bf16[4,72,384]{2,1,0:T(8,128)(2,1)S(1)}, bf16[4,72,384]{2,1,0:T(8,128)(2,1)S(1)}, u32[]{:S(2)}, u32[]{:S(2)}) collective-permute-start(bf16[4,72,384]{2,1,0:T(8,128)(2,1)S(1)} %get-tuple-element.52), channel_id=1, source_target_pairs={{1,2},{2,1},{3,4},{4,3},{5,6},{6,5},{9,10},{10,9},{11,12},{12,11},... | collective-permute-start | bytes 663560 | tf_op jit(solution)/shard_map/ppermute | solution.py:417
  13.7 0.5 shard_map.79.refs_3_
  14.2 0.0 copy-done.2
  14.2 3.2 %shard_map.80 = (bf16[4,12,80,256]{3,2,1,0:T(8,128)(2,1)S(1)}, bf16[6,8,80,256]{3,2,1,0:T(8,128)(2,1)S(1)}, f32[6,8,80,256]{3,2,1,0:T(8,128)S(1)}) custom-call(bf16[72,640]{1,0:T(8,128)(2,1)S(1)} %collective-permute-done.2.refs_0_, bf16[15,256,256]{2,1,0:T(8,128)(2,1)S(1)} %get-tuple-element.31.refs_1_.refs_2_, ...), custom_call_target="tpu_custom_call", output_to_operand_aliasing={{0}: (3, {})} | custom-call | flops 5000000000 | tf_op jit(solution)/shard_map/pallas_call | solution.py:69
  17.4 0.0 collective-permute-done.5
  17.5 0.7 %collective-permute-start.6 = (bf16[2,72,768]{2,1,0:T(8,128)(2,1)S(1)}, bf16[2,72,768]{2,1,0:T(8,128)(2,1)S(1)}, u32[]{:S(2)}, u32[]{:S(2)}) collective-permute-start(bf16[2,72,768]{2,1,0:T(8,128)(2,1)S(1)} %pad_maximum_fusion.3), channel_id=1, source_target_pairs={{0,16},{8,24},{16,0},{24,8},{1,17},{9,25},{17,1},{25,9},{2,18},{10... | collective-permute-start | bytes 663560 | tf_op jit(solution)/shard_map/ppermute | solution.py:400
  18.2 0.0 collective-permute-done.3.refs_0_
  18.2 0.0 collective-permute-done.4.refs_1_
  18.2 6.2 %shard_map.81 = (bf16[6,8,80,256]{3,2,1,0:T(8,128)(2,1)S(1)}, f32[6,8,80,256]{3,2,1,0:T(8,128)S(1)}) custom-call(bf16[4,72,384]{2,1,0:T(8,128)(2,1)S(1)} %collective-permute-done.3.refs_0_, bf16[4,72,384]{2,1,0:T(8,128)(2,1)S(1)} %collective-permute-done.4.refs_1_, ...), custom_call_target="tpu_custom_call", output_to_operand_aliasing={{0}: (5, {}), {1}: (6, {})} | custom-call | flops 7000000000 | tf_op jit(solution)/shard_map/pallas_call | solution.py:69
  24.5 0.1 collective-permute-done.6
  24.6 1.4 %shard_map.84 = (f32[4,384,128]{2,1,0:T(8,128)S(1)}, bf16[4,72,384]{2,1,0:T(8,128)(2,1)S(1)}) custom-call(bf16[6,8,80,256]{3,2,1,0:T(8,128)(2,1)S(1)} %get-tuple-element.35.refs_0_, bf16[3,256,256]{2,1,0:T(8,128)(2,1)S(1)} %get-tuple-element.36.refs_1_.refs_5_.refs_3_, f32[1,128]{1,0:T(1,128)S(1)} %pad_bitcast_fusion.refs_2_, ...), custom_call_target="tpu_custom_call" | custom-call | flops 2000000000 | tf_op jit(solution)/shard_map/pallas_call | solution.py:69
  26.0 1.4 %shard_map.83 = (f32[4,384,128]{2,1,0:T(8,128)S(1)}, bf16[4,72,384]{2,1,0:T(8,128)(2,1)S(1)}) custom-call(bf16[6,8,80,256]{3,2,1,0:T(8,128)(2,1)S(1)} %get-tuple-element.35.refs_0_, bf16[3,256,256]{2,1,0:T(8,128)(2,1)S(1)} %get-tuple-element.36.refs_1_.refs_5_.refs_3_, f32[1,128]{1,0:T(1,128)S(1)} %pad_bitcast_fusion.refs_2_, ...), custom_call_target="tpu_custom_call" | custom-call | flops 2000000000 | tf_op jit(solution)/shard_map/pallas_call | solution.py:69
  27.4 0.5 collective-permute-start.8
  27.9 3.4 %collective-permute-start.9 = (bf16[4,72,384]{2,1,0:T(8,128)(2,1)S(1)}, bf16[4,72,384]{2,1,0:T(8,128)(2,1)S(1)}, u32[]{:S(2)}, u32[]{:S(2)}) collective-permute-start(bf16[4,72,384]{2,1,0:T(8,128)(2,1)S(1)} %get-tuple-element.41.refs_0_), channel_id=1, source_target_pairs={{1,2},{2,1},{3,4},{4,3},{5,6},{6,5},{9,10},{10,9},{11,12},{12,11},... | collective-permute-start | bytes 663560 | tf_op jit(solution)/shard_map/ppermute | solution.py:417
  31.3 1.4 %shard_map.85 = (bf16[4,8,80,256]{3,2,1,0:T(8,128)(2,1)S(1)}, bf16[6,12,80,256]{3,2,1,0:T(8,128)(2,1)S(1)}, f32[72,512]{1,0:T(8,128)S(1)}, bf16[72,512]{1,0:T(8,...) custom-call(bf16[4,72,384]{2,1,0:T(8,128)(2,1)S(1)} %get-tuple-element.41.refs_0_, ...), custom_call_target="tpu_custom_call" | custom-call | flops 2300000000 | tf_op jit(solution)/shard_map/pallas_call | solution.py:69
  32.7 2.0 %collective-permute-start.7 = (bf16[72,512]{1,0:T(8,128)(2,1)S(1)}, bf16[72,512]{1,0:T(8,128)(2,1)S(1)}, u32[]{:S(2)}, u32[]{:S(2)}) collective-permute-start(bf16[72,512]{1,0:T(8,128)(2,1)S(1)} %get-tuple-element.47), channel_id=1, source_target_pairs={{0,8},{8,0},{16,24},{24,16},{1,9},{9,1},{17,25},{25,17},{2,10},{10... | collective-permute-start | bytes 221192 | tf_op jit(solution)/shard_map/ppermute | solution.py:400
  34.7 0.0 collective-permute-done.8.refs_0_
  34.7 0.7 %collective-permute-done.9.refs_1_ = bf16[4,72,384]{2,1,0:T(8,128)(2,1)S(1)} collective-permute-done((bf16[4,72,384]{2,1,0:T(8,128)(2,1)S(1)}, bf16[4,72,384]{2,1,0:T(8,128)(2,1)S(1)}, u32[]{:S(2)}, u32[]{:S(2)}) %collective-permute-start.9) | collective-permute-done | bytes 221216 | tf_op jit(solution)/shard_map/ppermute | solution.py:417
  35.4 1.6 %shard_map.86.refs_0_ = bf16[6,12,80,256]{3,2,1,0:T(8,128)(2,1)S(1)} custom-call(bf16[4,72,384]{2,1,0:T(8,128)(2,1)S(1)} %collective-permute-done.8.refs_0_, bf16[4,72,384]{2,1,0:T(8,128)(2,1)S(1)} %collective-permute-done.9.refs_1_, f32[6,8,80,256]{3,2,1,0:T(8,128)S(1)} %get-tuple-element.45.refs_4_.refs_2_, ...), custom_call_target="tpu_custom_call", output_to_operand_aliasing={{}: (5, {})} | custom-call | flops 2000000000 | tf_op jit(solution)/shard_map/pallas_call | solution.py:69
  37.1 1.7 %shard_map.91 = bf16[72,512]{1,0:T(8,128)(2,1)S(1)} custom-call(bf16[6,12,80,256]{3,2,1,0:T(8,128)(2,1)S(1)} %shard_map.86.refs_0_, bf16[15,256,256]{2,1,0:T(8,128)(2,1)S(1)} %get-tuple-element.31.refs_1_.refs_2_), custom_call_target="tpu_custom_call" | custom-call | flops 2000000000 | tf_op jit(solution)/shard_map/pallas_call | solution.py:69
  38.7 2.0 %collective-permute-start.12 = (bf16[72,512]{1,0:T(8,128)(2,1)S(1)}, bf16[72,512]{1,0:T(8,128)(2,1)S(1)}, u32[]{:S(2)}, u32[]{:S(2)}) collective-permute-start(bf16[72,512]{1,0:T(8,128)(2,1)S(1)} %shard_map.91), channel_id=1, source_target_pairs={{0,8},{8,0},{16,24},{24,16},{1,9},{9,1},{17,25},{25,17},{2,10},{10... | collective-permute-start | bytes 221192 | tf_op jit(solution)/shard_map/ppermute | solution.py:400
  40.7 1.7 %shard_map.88 = bf16[72,1024]{1,0:T(8,128)(2,1)S(1)} custom-call(bf16[6,12,80,256]{3,2,1,0:T(8,128)(2,1)S(1)} %shard_map.86.refs_0_, bf16[15,256,256]{2,1,0:T(8,128)(2,1)S(1)} %get-tuple-element.31.refs_1_.refs_2_, bf16[72,512]{1,0:T(8,128)(2,1)S(1)} %get-tuple-element.51.refs_2_), custom_call_target="tpu_custom_call" | custom-call | flops 2000000000 | tf_op jit(solution)/shard_map/pallas_call | solution.py:69
  42.4 0.2 collective-permute-start.11
  42.5 1.7 %shard_map.87 = bf16[72,1024]{1,0:T(8,128)(2,1)S(1)} custom-call(bf16[6,12,80,256]{3,2,1,0:T(8,128)(2,1)S(1)} %shard_map.86.refs_0_, bf16[15,256,256]{2,1,0:T(8,128)(2,1)S(1)} %get-tuple-element.31.refs_1_.refs_2_, bf16[72,512]{1,0:T(8,128)(2,1)S(1)} %get-tuple-element.50.refs_2_), custom_call_target="tpu_custom_call" | custom-call | flops 2000000000 | tf_op jit(solution)/shard_map/pallas_call | solution.py:69
  44.2 1.2 %collective-permute-start.10 = (bf16[72,1024]{1,0:T(8,128)(2,1)S(1)}, bf16[72,1024]{1,0:T(8,128)(2,1)S(1)}, u32[]{:S(2)}, u32[]{:S(2)}) collective-permute-start(bf16[72,1024]{1,0:T(8,128)(2,1)S(1)} %shard_map.87), channel_id=1, source_target_pairs={{0,16},{8,24},{16,0},{24,8},{1,17},{9,25},{17,1},{25,9},{2,18},{10... | collective-permute-start | bytes 442376 | tf_op jit(solution)/shard_map/ppermute | solution.py:400
  45.3 1.7 %shard_map.90.refs_0_ = f32[72,512]{1,0:T(8,128)S(1)} custom-call(bf16[6,12,80,256]{3,2,1,0:T(8,128)(2,1)S(1)} %shard_map.86.refs_0_, bf16[15,256,256]{2,1,0:T(8,128)(2,1)S(1)} %get-tuple-element.31.refs_1_.refs_2_), custom_call_target="tpu_custom_call" | custom-call | flops 2000000000 | tf_op jit(solution)/shard_map/pallas_call | solution.py:69
  47.1 0.0 collective-permute-done.12.refs_1_
  47.1 1.6 %collective-permute-done.11.refs_3_ = bf16[72,1024]{1,0:T(8,128)(2,1)S(1)} collective-permute-done((bf16[72,1024]{1,0:T(8,128)(2,1)S(1)}, bf16[72,1024]{1,0:T(8,128)(2,1)S(1)}, u32[]{:S(2)}, u32[]{:S(2)}) %collective-permute-start.11) | collective-permute-done | bytes 147488 | tf_op jit(solution)/shard_map/ppermute | solution.py:400
  48.6 3.6 %collective-permute-done.10.refs_2_ = bf16[72,1024]{1,0:T(8,128)(2,1)S(1)} collective-permute-done((bf16[72,1024]{1,0:T(8,128)(2,1)S(1)}, bf16[72,1024]{1,0:T(8,128)(2,1)S(1)}, u32[]{:S(2)}, u32[]{:S(2)}) %collective-permute-start.10) | collective-permute-done | bytes 147488 | tf_op jit(solution)/shard_map/ppermute | solution.py:400
  52.3 1.2 %shard_map.92 = f32[2,69,4,256]{3,2,1,0:T(4,128)} custom-call(f32[72,512]{1,0:T(8,128)S(1)} %shard_map.90.refs_0_, bf16[72,512]{1,0:T(8,128)(2,1)S(1)} %collective-permute-done.12.refs_1_, bf16[72,1024]{1,0:T(8,128)(2,1)S(1)} %collective-permute-done.10.refs_2_, bf16[72,1024]{1,0:T(8,128)(2,1)S(1)} %collective-permute-done.11.refs_3_), custom_call_target="tpu_custom_call" | custom-call | flops 1000000000 | tf_op jit(solution)/shard_map/pallas_call | solution.py:69
  53.5 0.0 collective-permute-done.7.refs_1_
  53.5 1.2 %shard_map.89 = f32[2,69,4,256]{3,2,1,0:T(4,128)} custom-call(f32[72,512]{1,0:T(8,128)S(1)} %get-tuple-element.46.refs_0_, bf16[72,512]{1,0:T(8,128)(2,1)S(1)} %collective-permute-done.7.refs_1_, bf16[72,1024]{1,0:T(8,128)(2,1)S(1)} %collective-permute-done.10.refs_2_, bf16[72,1024]{1,0:T(8,128)(2,1)S(1)} %collective-permute-done.11.refs_3_), custom_call_target="tpu_custom_call" | custom-call | flops 1000000000 | tf_op jit(solution)/shard_map/pallas_call | solution.py:69
  (9 shorter events, 0.1 us)
Async XLA Ops:
  2.2 5.5 %collective-permute-start = (bf16[72,640]{1,0:T(8,128)(2,1)S(1)}, bf16[72,640]{1,0:T(8,128)(2,1)S(1)}, u32[]{:S(2)}, u32[]{:S(2)}) collective-permute-start(bf16[72,640]{1,0:T(8,128)(2,1)S(1)} %get-tuple-element.28), channel_id=1, source_target_pairs={{0,8},{8,0},{16,24},{24,16},{1,9},{9,1},{17,25},{25,17},{2,10},{10... | collective-permute-start | bytes 276488 | tf_op jit(solution)/shard_map/ppermute | solution.py:400
  2.5 5.2 %collective-permute-start.1 = (bf16[72,640]{1,0:T(8,128)(2,1)S(1)}, bf16[72,640]{1,0:T(8,128)(2,1)S(1)}, u32[]{:S(2)}, u32[]{:S(2)}) collective-permute-start(bf16[72,640]{1,0:T(8,128)(2,1)S(1)} %get-tuple-element.29), channel_id=1, source_target_pairs={{0,16},{8,24},{16,0},{24,8},{1,17},{9,25},{17,1},{25,9},{2,18},{10... | collective-permute-start | bytes 276488 | tf_op jit(solution)/shard_map/ppermute | solution.py:400
  3.7 3.3 %copy-start = (bf16[3,3,256,345]{2,3,1,0:T(8,128)(2,1)S(1)}, bf16[3,3,256,345]{2,3,1,0:T(8,128)(2,1)}, u32[]{:S(2)}) copy-start(bf16[3,3,256,345]{2,3,1,0:T(8,128)(2,1)} %param.8) | copy-start | bytes 4769284
  3.7 3.3 %copy-start.1 = (bf16[3,3,69,256]{3,2,1,0:T(8,128)(2,1)S(1)}, bf16[3,3,69,256]{3,2,1,0:T(8,128)(2,1)}, u32[]{:S(2)}) copy-start(bf16[3,3,69,256]{3,2,1,0:T(8,128)(2,1)} %refs_1_.1) | copy-start | bytes 953860
  3.7 5.0 %collective-permute-start.2 = (bf16[72,640]{1,0:T(8,128)(2,1)S(1)}, bf16[72,640]{1,0:T(8,128)(2,1)S(1)}, u32[]{:S(2)}, u32[]{:S(2)}) collective-permute-start(bf16[72,640]{1,0:T(8,128)(2,1)S(1)} %get-tuple-element.30), channel_id=1, source_target_pairs={{0,24},{8,16},{16,8},{24,0},{1,25},{9,17},{17,9},{25,1},{2,26},{10... | collective-permute-start | bytes 276488 | tf_op jit(solution)/shard_map/ppermute | solution.py:400
  6.6 10.8 %collective-permute-start.5 = (bf16[2,72,768]{2,1,0:T(8,128)(2,1)S(1)}, bf16[2,72,768]{2,1,0:T(8,128)(2,1)S(1)}, u32[]{:S(2)}, u32[]{:S(2)}) collective-permute-start(bf16[2,72,768]{2,1,0:T(8,128)(2,1)S(1)} %pad_maximum_fusion.2), channel_id=1, source_target_pairs={{0,8},{8,0},{16,24},{24,16},{1,9},{9,1},{17,25},{25,17},{2,10},{10... | collective-permute-start | bytes 663560 | tf_op jit(solution)/shard_map/ppermute | solution.py:400
  7.1 0.7 %copy-start.3 = (f32[69]{0:T(128)S(1)}, f32[69]{0:T(128)}, u32[]{:S(2)}) copy-start(f32[69]{0:T(128)} %param.11) | copy-start | bytes 832
  8.8 5.4 %copy-start.2 = (f32[256]{0:T(256)S(1)}, f32[256]{0:T(256)}, u32[]{:S(2)}) copy-start(f32[256]{0:T(256)} %param.9) | copy-start | bytes 3076
  8.8 9.4 %collective-permute-start.3 = (bf16[4,72,384]{2,1,0:T(8,128)(2,1)S(1)}, bf16[4,72,384]{2,1,0:T(8,128)(2,1)S(1)}, u32[]{:S(2)}, u32[]{:S(2)}) collective-permute-start(bf16[4,72,384]{2,1,0:T(8,128)(2,1)S(1)} %get-tuple-element.53), channel_id=1, source_target_pairs={{0,1},{1,0},{2,3},{3,2},{4,5},{5,4},{6,7},{7,6},{8,9},{9,8},{10,11... | collective-permute-start | bytes 663560 | tf_op jit(solution)/shard_map/ppermute | solution.py:413
  10.6 7.6 %collective-permute-start.4 = (bf16[4,72,384]{2,1,0:T(8,128)(2,1)S(1)}, bf16[4,72,384]{2,1,0:T(8,128)(2,1)S(1)}, u32[]{:S(2)}, u32[]{:S(2)}) collective-permute-start(bf16[4,72,384]{2,1,0:T(8,128)(2,1)S(1)} %get-tuple-element.52), channel_id=1, source_target_pairs={{1,2},{2,1},{3,4},{4,3},{5,6},{6,5},{9,10},{10,9},{11,12},{12,11},... | collective-permute-start | bytes 663560 | tf_op jit(solution)/shard_map/ppermute | solution.py:417
  17.5 7.1 %collective-permute-start.6 = (bf16[2,72,768]{2,1,0:T(8,128)(2,1)S(1)}, bf16[2,72,768]{2,1,0:T(8,128)(2,1)S(1)}, u32[]{:S(2)}, u32[]{:S(2)}) collective-permute-start(bf16[2,72,768]{2,1,0:T(8,128)(2,1)S(1)} %pad_maximum_fusion.3), channel_id=1, source_target_pairs={{0,16},{8,24},{16,0},{24,8},{1,17},{9,25},{17,1},{25,9},{2,18},{10... | collective-permute-start | bytes 663560 | tf_op jit(solution)/shard_map/ppermute | solution.py:400
  27.4 7.2 %collective-permute-start.8 = (bf16[4,72,384]{2,1,0:T(8,128)(2,1)S(1)}, bf16[4,72,384]{2,1,0:T(8,128)(2,1)S(1)}, u32[]{:S(2)}, u32[]{:S(2)}) collective-permute-start(bf16[4,72,384]{2,1,0:T(8,128)(2,1)S(1)} %get-tuple-element.42.refs_1_), channel_id=1, source_target_pairs={{0,1},{1,0},{2,3},{3,2},{4,5},{5,4},{6,7},{7,6},{8,9},{9,8},{10,11... | collective-permute-start | bytes 663560 | tf_op jit(solution)/shard_map/ppermute | solution.py:413
  27.9 7.5 %collective-permute-start.9 = (bf16[4,72,384]{2,1,0:T(8,128)(2,1)S(1)}, bf16[4,72,384]{2,1,0:T(8,128)(2,1)S(1)}, u32[]{:S(2)}, u32[]{:S(2)}) collective-permute-start(bf16[4,72,384]{2,1,0:T(8,128)(2,1)S(1)} %get-tuple-element.41.refs_0_), channel_id=1, source_target_pairs={{1,2},{2,1},{3,4},{4,3},{5,6},{6,5},{9,10},{10,9},{11,12},{12,11},... | collective-permute-start | bytes 663560 | tf_op jit(solution)/shard_map/ppermute | solution.py:417
  32.7 20.8 %collective-permute-start.7 = (bf16[72,512]{1,0:T(8,128)(2,1)S(1)}, bf16[72,512]{1,0:T(8,128)(2,1)S(1)}, u32[]{:S(2)}, u32[]{:S(2)}) collective-permute-start(bf16[72,512]{1,0:T(8,128)(2,1)S(1)} %get-tuple-element.47), channel_id=1, source_target_pairs={{0,8},{8,0},{16,24},{24,16},{1,9},{9,1},{17,25},{25,17},{2,10},{10... | collective-permute-start | bytes 221192 | tf_op jit(solution)/shard_map/ppermute | solution.py:400
  38.7 8.3 %collective-permute-start.12 = (bf16[72,512]{1,0:T(8,128)(2,1)S(1)}, bf16[72,512]{1,0:T(8,128)(2,1)S(1)}, u32[]{:S(2)}, u32[]{:S(2)}) collective-permute-start(bf16[72,512]{1,0:T(8,128)(2,1)S(1)} %shard_map.91), channel_id=1, source_target_pairs={{0,8},{8,0},{16,24},{24,16},{1,9},{9,1},{17,25},{25,17},{2,10},{10... | collective-permute-start | bytes 221192 | tf_op jit(solution)/shard_map/ppermute | solution.py:400
  42.4 6.3 %collective-permute-start.11 = (bf16[72,1024]{1,0:T(8,128)(2,1)S(1)}, bf16[72,1024]{1,0:T(8,128)(2,1)S(1)}, u32[]{:S(2)}, u32[]{:S(2)}) collective-permute-start(bf16[72,1024]{1,0:T(8,128)(2,1)S(1)} %shard_map.88), channel_id=1, source_target_pairs={{0,24},{8,16},{16,8},{24,0},{1,25},{9,17},{17,9},{25,1},{2,26},{10... | collective-permute-start | bytes 442376 | tf_op jit(solution)/shard_map/ppermute | solution.py:400
  44.2 8.1 %collective-permute-start.10 = (bf16[72,1024]{1,0:T(8,128)(2,1)S(1)}, bf16[72,1024]{1,0:T(8,128)(2,1)S(1)}, u32[]{:S(2)}, u32[]{:S(2)}) collective-permute-start(bf16[72,1024]{1,0:T(8,128)(2,1)S(1)} %shard_map.87), channel_id=1, source_target_pairs={{0,16},{8,24},{16,0},{24,8},{1,17},{9,25},{17,1},{25,9},{2,18},{10... | collective-permute-start | bytes 442376 | tf_op jit(solution)/shard_map/ppermute | solution.py:400
